TPU v7x, 32 devices: a whole 2x2x4 slice. The times are simulated.
32 devices in a mesh: seq: 8 (over z, x), head: 4 (over y, core).
Axes of the slice: x: 2, y: 2, z: 4, core: 2. Of those that a mesh axis runs over, the one named last changes fastest.
Arguments:
- query_rows: bfloat16 [1, 2048, 2048], P(None, 'seq', 'head'), may hold values from -28 to 28
- key_rows: bfloat16 [1, 2048, 2048], P(None, 'seq', 'head'), may hold values from -4 to 4
- value_rows: bfloat16 [1, 2048, 2048], P(None, 'seq', 'head'), may hold values from -6 to 6
- grad_out: bfloat16 [1, 2048, 2048], P(None, 'seq', 'head'), may hold values from -6 to 6
- rand_blocks: int32 [1, 16, 32, 3], P(None, 'head'), may hold values from 0 to 31, as said below
- global_pos: int32 [128], replicated, may hold values from 0 to 2047, as said below
Outputs:
- attended: bfloat16 [1, 2048, 2048], P(None, 'seq', 'head')
- grad_query: bfloat16 [1, 2048, 2048], P(None, 'seq', 'head')
- grad_key: bfloat16 [1, 2048, 2048], P(None, 'seq', 'head')
- grad_value: bfloat16 [1, 2048, 2048], P(None, 'seq', 'head')
Inputs may be any that keep to these rules, and one draw needn't show every extreme that they name: `rand_blocks`: for each run of 4 query blocks and each run of 4 heads that start at multiples of these counts, taking the one sequence and all 3 picks together, at most 6 picks name a block of any one run of 4 key blocks that starts at a multiple of 4; in each such run of query blocks and heads some run of key blocks is named exactly 6 times. `global_pos`: distinct positions; the first and the last token of the sequence are among them.
All inputs are finite; a program needn't handle non-finite values.
Results may differ from a plain program's by a relative error of at most 0.006.
The roundings to bfloat16 on the way count: a program that leaves them out, or rounds other values in their place, can miss the bound.
Values may be sent and summed in bfloat16 or wider, within the bound.
No kernel may reach another device: no remote copies, remote signals or barrier semaphores. Data moves between devices by JAX's collectives and lax.ppermute only.
A program may use at most 64 MiB of HBM per device.

v0:
```python
import jax
import jax.numpy as jnp
from jax import lax
from jax.sharding import PartitionSpec as P

BLOCK = 64


def extended_2(value, sides, width):
    for axis, dim in sides:
        size, length = (lax.axis_size(axis), value.shape[dim])
        up = [(i, (i + 1) % size) for i in range(size - 1)]
        down = [(j, i) for i, j in up]
        last = lax.slice_in_dim(value, length - width, length, axis=dim)
        first = lax.slice_in_dim(value, 0, width, axis=dim)
        before = lax.ppermute(last, axis, up)
        after = lax.ppermute(first, axis, down)
        value = jnp.concatenate([before, value, after], axis=dim)
    return value


def body(query_rows, key_rows, value_rows, grad_out, rand_blocks, global_pos):
    batch_count, tok_local, columns = query_rows.shape
    seq_count = lax.axis_size("seq")
    seq_index = lax.axis_index("seq")
    heads_local = rand_blocks.shape[1]
    total_blocks = rand_blocks.shape[2]
    pick_count = rand_blocks.shape[3]
    head_dim = columns // heads_local
    blocks_local = tok_local // BLOCK
    score_scale = head_dim ** (-0.5)
    slot_count = batch_count * heads_local * blocks_local * pick_count
    capacity = (slot_count + seq_count - 1) // seq_count
    buffer_rows = seq_count * capacity
    f32 = jnp.float32
    bf16 = jnp.bfloat16

    def to_blocks(array):
        return array.reshape(batch_count, blocks_local, BLOCK, heads_local, head_dim).transpose(
            0, 3, 1, 2, 4
        )

    def from_blocks(array):
        return array.transpose(0, 2, 3, 1, 4).reshape(batch_count, tok_local, columns)

    def pair_blocks(array):
        return array.reshape(2, batch_count, blocks_local, BLOCK, heads_local, head_dim).transpose(
            0, 1, 4, 2, 3, 5
        )

    def global_sum(array):
        return lax.psum(array, "seq")

    key_value = jnp.stack([key_rows, value_rows])
    edge_rows = jnp.concatenate([key_value[:, :, :BLOCK], key_value[:, :, -BLOCK:]], axis=2)
    extended = extended_2(edge_rows, (("seq", 2),), BLOCK)
    padded = jnp.concatenate([extended[:, :, :BLOCK], key_value, extended[:, :, -BLOCK:]], axis=2)

    def shifted(start):
        return pair_blocks(padded[:, :, start : start + tok_local])

    window_lists = jnp.concatenate([shifted(0), shifted(BLOCK), shifted(2 * BLOCK)], axis=4)
    my_table = lax.dynamic_slice_in_dim(
        rand_blocks, seq_index * blocks_local, blocks_local, 2
    ).reshape(slot_count)
    holder = my_table // blocks_local
    holder_hot = (holder[:, None] == jnp.arange(seq_count)[None, :]).astype(jnp.int32)
    holder_rank = jnp.sum((jnp.cumsum(holder_hot, axis=0) - 1) * holder_hot, axis=1)
    position = holder * capacity + holder_rank
    requests = rand_blocks.reshape(batch_count, heads_local, seq_count, blocks_local, pick_count)
    requests = requests.transpose(2, 0, 1, 3, 4).reshape(seq_count, slot_count)
    wanted = (requests // blocks_local == seq_index).astype(jnp.int32)
    wanted_rank = jnp.cumsum(wanted, axis=1) - 1
    chosen = wanted[:, None, :] * (
        wanted_rank[:, None, :] == jnp.arange(capacity)[None, :, None]
    ).astype(jnp.int32)
    slot_live = (jnp.sum(chosen, axis=2) > 0).reshape(buffer_rows)
    slot_index = jnp.sum(chosen * jnp.arange(slot_count)[None, None, :], axis=2)
    which_batch = slot_index // (heads_local * blocks_local * pick_count)
    which_head = slot_index // (blocks_local * pick_count) % heads_local
    which_block = jnp.take_along_axis(requests, slot_index, axis=1) % blocks_local
    stacked = key_value.reshape(
        2, batch_count, blocks_local, BLOCK, heads_local, head_dim
    ).transpose(1, 2, 4, 0, 3, 5)
    outgoing = stacked[which_batch, which_block, which_head].reshape(
        buffer_rows, 2, BLOCK, head_dim
    )
    incoming = lax.all_to_all(outgoing, "seq", split_axis=0, concat_axis=0, tiled=True)
    fetched = incoming[position].reshape(
        batch_count, heads_local, blocks_local, pick_count, 2, BLOCK, head_dim
    )
    fetched = fetched.transpose(4, 0, 1, 2, 3, 5, 6).reshape(
        2, batch_count, heads_local, blocks_local, pick_count * BLOCK, head_dim
    )
    local_pos = global_pos - seq_index * tok_local
    pick_hot = (local_pos[:, None] == jnp.arange(tok_local)[None, :]).astype(bf16)
    owned_rows = jnp.einsum("gt,pbtc->pbgc", pick_hot, key_value, preferred_element_type=f32)
    shared = global_sum(owned_rows).astype(bf16)
    globals_count = shared.shape[2]
    global_kv = shared.reshape(2, batch_count, globals_count, heads_local, head_dim).transpose(
        0, 1, 3, 2, 4
    )
    global_kv = jnp.broadcast_to(
        global_kv[:, :, :, None],
        (2, batch_count, heads_local, blocks_local, globals_count, head_dim),
    )
    lists_all = jnp.concatenate([window_lists, fetched, global_kv], axis=4)
    key_lists = lists_all[0]
    value_lists = lists_all[1]
    key_count = key_lists.shape[3]
    block_ids = seq_index * blocks_local + jnp.arange(blocks_local)
    column_ids = jnp.arange(key_count)[None, :]
    middle_ok = jnp.where(
        (column_ids >= 2 * BLOCK) & (column_ids < 3 * BLOCK),
        (block_ids < total_blocks - 1)[:, None],
        True,
    )
    valid_mask = jnp.where(column_ids < BLOCK, (block_ids > 0)[:, None], middle_ok)
    query_blocks = to_blocks(query_rows)
    grad_blocks = to_blocks(grad_out)
    scores = (
        jnp.einsum("bhjqd,bhjkd->bhjqk", query_blocks, key_lists, preferred_element_type=f32)
        * score_scale
    )
    scores = jnp.where(valid_mask[None, None, :, None, :], scores, -1e30)
    row_max = jnp.max(scores, axis=-1, keepdims=True)
    log_total = row_max + jnp.log(jnp.sum(jnp.exp(scores - row_max), axis=-1, keepdims=True))
    weights = jnp.exp(scores - log_total)
    weights_b = weights.astype(bf16)
    mixed_rows = jnp.einsum(
        "bhjqk,bhjkd->bhjqd", weights_b, value_lists, preferred_element_type=f32
    )
    attended = from_blocks(mixed_rows.astype(bf16))
    row_delta = jnp.sum(grad_blocks.astype(f32) * mixed_rows, axis=-1, keepdims=True)
    grad_probs = jnp.einsum(
        "bhjqd,bhjkd->bhjqk", grad_blocks, value_lists, preferred_element_type=f32
    )
    dscore_b = (weights * (grad_probs - row_delta)).astype(bf16)
    grad_query = (
        jnp.einsum("bhjqk,bhjkd->bhjqd", dscore_b, key_lists, preferred_element_type=f32)
        * score_scale
    )

    def key_grads(lower, upper):
        key_part = (
            jnp.einsum(
                "bhjqk,bhjqd->bhjkd",
                dscore_b[..., lower:upper],
                query_blocks,
                preferred_element_type=f32,
            )
            * score_scale
        )
        value_part = jnp.einsum(
            "bhjqk,bhjqd->bhjkd",
            weights_b[..., lower:upper],
            grad_blocks,
            preferred_element_type=f32,
        )
        return jnp.stack([key_part, value_part])

    window_cols = 3 * BLOCK
    random_cols = pick_count * BLOCK
    window_grads = key_grads(0, window_cols).reshape(
        2, batch_count, heads_local, blocks_local, 3, BLOCK, head_dim
    )
    padded_grads = jnp.pad(
        window_grads[:, :, :, :, 0], ((0, 0), (0, 0), (0, 0), (0, 2), (0, 0), (0, 0))
    )
    padded_grads = padded_grads + jnp.pad(
        window_grads[:, :, :, :, 1], ((0, 0), (0, 0), (0, 0), (1, 1), (0, 0), (0, 0))
    )
    padded_grads = padded_grads + jnp.pad(
        window_grads[:, :, :, :, 2], ((0, 0), (0, 0), (0, 0), (2, 0), (0, 0), (0, 0))
    )
    own_grads = padded_grads[:, :, :, 1:-1]
    rim_grads = jnp.stack([padded_grads[:, :, :, 0], padded_grads[:, :, :, -1]], axis=3)
    returned = extended_2(rim_grads.astype(jnp.bfloat16), (("seq", 3),), 1).astype(rim_grads.dtype)
    own_grads = own_grads.at[:, :, :, 0].add(returned[:, :, :, 0])
    own_grads = own_grads.at[:, :, :, -1].add(returned[:, :, :, 3])
    global_grads = jnp.sum(key_grads(window_cols + random_cols, key_count), axis=3)
    global_grads = global_grads.transpose(0, 1, 3, 2, 4).reshape(
        2, batch_count, globals_count, columns
    )
    global_summed = global_sum(global_grads)
    inside = (local_pos >= 0) & (local_pos < tok_local)
    safe_pos = jnp.where(inside, local_pos, tok_local)
    global_local = (
        jnp.zeros((2, batch_count, tok_local, columns), f32)
        .at[:, :, safe_pos]
        .add(global_summed, mode="drop")
    )
    global_part = pair_blocks(global_local)
    target = ((which_batch * blocks_local + which_block) * heads_local + which_head).reshape(
        buffer_rows
    )
    random_grads = key_grads(window_cols, window_cols + random_cols)
    per_slot = random_grads.reshape(
        2, batch_count, heads_local, blocks_local, pick_count, BLOCK, head_dim
    )
    per_slot = per_slot.transpose(1, 2, 3, 4, 0, 5, 6).reshape(slot_count, 2, BLOCK, head_dim)
    sending = jnp.zeros((buffer_rows, 2, BLOCK, head_dim), f32).at[position].set(per_slot)
    arrived = lax.all_to_all(
        sending.astype(jnp.bfloat16), "seq", split_axis=0, concat_axis=0, tiled=True
    ).astype(sending.dtype)
    kept = jnp.where(slot_live[:, None, None, None], arrived, 0.0)
    summed = (
        jnp.zeros((batch_count * blocks_local * heads_local, 2, BLOCK, head_dim), f32)
        .at[target]
        .add(kept)
    )
    random_part = summed.reshape(
        batch_count, blocks_local, heads_local, 2, BLOCK, head_dim
    ).transpose(3, 0, 2, 1, 4, 5)
    total_grads = own_grads + random_part + global_part
    grad_key = from_blocks(total_grads[0].astype(bf16))
    grad_value = from_blocks(total_grads[1].astype(bf16))
    return (attended, from_blocks(grad_query.astype(bf16)), grad_key, grad_value)


def solution(mesh):
    return jax.shard_map(
        body,
        mesh=mesh,
        in_specs=(
            P(None, "seq", "head"),
            P(None, "seq", "head"),
            P(None, "seq", "head"),
            P(None, "seq", "head"),
            P(None, "head", None, None),
            P(),
        ),
        out_specs=(
            P(None, "seq", "head"),
            P(None, "seq", "head"),
            P(None, "seq", "head"),
            P(None, "seq", "head"),
        ),
        check_vma=False,
    )
```

profile of v0, /device:TPU:0, one launch (start us, length us, event | category | flops | bytes accessed | tf_op | source)
XLA Modules:
  0.0 257.3 jit_solution(15945176738781555091)
XLA Ops:
  7.2 1.1 copy.138
  8.3 1.1 copy.139
  9.4 0.9 fusion.24
  10.3 1.3 collective-permute-start.1
  11.6 6.2 %collective-permute-start = (bf16[2,1,64,512]{2,3,0,1:T(8,128)(2,1)}, bf16[2,1,64,512]{2,3,0,1:T(8,128)(2,1)}, u32[]{:S(2)}, u32[]{:S(2)}) collective-permute-start(bf16[2,1,64,512]{2,3,0,1:T(8,128)(2,1)} %get-tuple-element.42), channel_id=1, source_target_pairs={{0,4},{4,8},{8,12},{12,16},{16,20},{20,24},{24,28},{1,5},{5,9},{9,... | collective-permute-start | bytes 393224 | tf_op jit(solution)/shard_map/ppermute | solution.py:16
  19.1 1.0 gather_fusion.2
  20.3 2.1 gather_fusion
  22.5 5.6 %all-to-all-start = ((bf16[48,2,64,128]{3,2,1,0:T(8,128)(2,1)}), bf16[48,2,64,128]{3,2,1,0:T(8,128)(2,1)S(1)}, u32[]{:S(2)}, u32[]{:S(2)}) async-start(bf16[48,2,64,128]{3,2,1,0:T(8,128)(2,1)} %gather_fusion), calls=%async_computation | async-start | bytes 3145728 | tf_op jit(solution)/shard_map/all_to_all | solution.py:88
  28.7 0.4 convolution_bitcast_fusion.1
  29.3 66.9 %all-reduce.7 = bf16[2,1,128,512]{2,3,0,1:T(8,128)(2,1)S(1)} all-reduce(f32[2,1,128,512]{2,3,0,1:T(8,128)S(1)} %convolution_bitcast_fusion.1), channel_id=1, replica_groups=mesh['seq'=8,'head'=4] {'seq'}, use_global_device_ids=true, to_apply=%region_4.5 | all-reduce | flops 131072 | bytes 786432 | tf_op jit(solution)/shard_map/psum | solution.py:52
  96.4 1.0 reshape.1055
  97.4 0.8 copy.174
  98.2 0.8 reshape.1051
  99.0 2.5 pad_maximum_fusion.2
  101.6 2.0 reshape.1122
  103.6 1.2 copy.141
  104.8 2.0 reshape.1123
  106.9 1.2 copy.145
  108.1 2.1 bitcast_dynamic-update-slice_fusion.2
  110.1 1.0 bitcast_dynamic-update-slice_fusion.1
  111.1 0.9 bitcast_dynamic-update-slice_fusion
  112.0 2.0 gather_fusion.1
  114.0 1.5 copy.154
  115.6 1.4 constant_dynamic-update-slice_fusion
  117.0 1.2 broadcast_dynamic-update-slice_fusion
  118.2 2.5 bitcast_reduce_fusion
  120.8 0.7 fusion.2
  121.5 0.4 fusion.21
  121.9 3.4 %fusion.20 = (f32[4,4,64]{2,1,0:T(4,128)S(1)}, bf16[4,4,64,128]{3,2,1,0:T(8,128)(2,1)}) fusion(bf16[1,4,64,4,128]{4,3,2,1,0:T(4,128)(2,1)S(1)} %reshape.1055, bf16[2,1,4,4,512,128]{5,4,3,2,1,0:T(8,128)(2,1)} %broadcast_dynamic-update-slice_fusion, f32[4,4,512,64]{2,3,1,0:T(8,128)S(1)} %get-tuple-element.48, f32[4,4,64]{2,1,0:T(4,128)S(1)} %bitcast.280), kind=kOutput, calls=%fused_computation.64 | convolution fusion | flops 135789568 | bytes 4726784 | tf_op jit(solution)/shard_map/bhjqk,bhjkd->bhjqd/dot_general | solution.py:130
  125.3 2.5 fusion
  127.8 0.7 fusion.18
  128.6 0.7 convolution_multiply_fusion
  129.3 0.4 maximum_bitcast_fusion
  129.7 1.9 copy.164
  131.6 0.4 broadcast_in_dim.120
  132.0 5.7 %scatter_fusion = f32[48,2,64,128]{3,2,1,0:T(8,128)S(1)} fusion(f32[48,2,64,128]{3,2,1,0:T(8,128)S(1)} %broadcast_in_dim.120, s32[48]{0:T(128)S(1)} %fusion.72, f32[48,2,64,128]{3,2,1,0:T(8,128)} %bitcast.256), kind=kCustom, calls=%fused_computation.3 | custom fusion | bytes 9437376 | tf_op jit(solution)/shard_map/scatter | solution.py:202
  137.7 1.5 convert_element_type.122
  139.3 4.4 %all-to-all-start.1 = ((bf16[48,2,64,128]{3,2,1,0:T(8,128)(2,1)}), bf16[48,2,64,128]{3,2,1,0:T(8,128)(2,1)}, u32[]{:S(2)}, u32[]{:S(2)}) async-start(bf16[48,2,64,128]{3,2,1,0:T(8,128)(2,1)} %convert_element_type.122), calls=%async_computation.1 | async-start | bytes 3145728 | tf_op jit(solution)/shard_map/all_to_all | solution.py:203
  144.7 0.4 fusion.9
  145.2 1.1 copy.165
  146.2 0.4 convolution_multiply_fusion.1
  146.7 0.4 fusion.19
  147.2 0.4 fusion.14
  147.8 0.7 add_convert_fusion.1
  148.6 1.3 collective-permute-start.3
  149.8 5.2 %collective-permute-start.2 = (bf16[2,1,4,1,64,128]{5,4,0,2,3,1:T(8,128)(2,1)}, bf16[2,1,4,1,64,128]{5,4,0,2,3,1:T(8,128)(2,1)}, u32[]{:S(2)}, u32[]{:S(2)}) collective-permute-start(bf16[2,1,4,1,64,128]{5,4,0,2,3,1:T(8,128)(2,1)} %get-tuple-element.32), channel_id=1, source_target_pairs={{0,4},{4,8},{8,12},{12,16},{16,20},{20,24},{24,28},{1,5},{5,9},{9,... | collective-permute-start | bytes 393224 | tf_op jit(solution)/shard_map/ppermute | solution.py:16
  155.0 2.8 %fusion.12 = bf16[1,4,64,4,128]{4,2,1,3,0:T(8,128)(2,1)} fusion(bf16[4,4,64,512]{3,2,1,0:T(8,128)(2,1)S(1)} %copy-done.7, bf16[2,1,4,4,512,128]{5,4,3,2,1,0:T(8,128)(2,1)} %broadcast_dynamic-update-slice_fusion), kind=kOutput, calls=%fused_computation.38 | convolution fusion | flops 134479872 | bytes 3407872 | tf_op jit(solution)/shard_map/bhjqk,bhjkd->bhjqd/dot_general | solution.py:140
  157.9 1.4 pad_add_fusion
  159.5 0.8 reshape.1054
  160.3 1.2 copy.159
  161.4 0.8 reshape.1057
  162.3 2.3 slice.213
  164.6 1.0 maximum_bitcast_fusion.1
  165.6 1.7 fusion.26
  167.3 1.7 fusion.25
  168.9 59.2 %all-reduce.6.cloned.1.call-done = f32[2,1,128,512]{2,3,0,1:T(8,128)} async-done(((f32[2,1,128,512]{2,3,0,1:T(8,128)}), f32[2,1,128,512]{2,3,0,1:T(8,128)}) %all-reduce.6.cloned.1.call-update) | async-done | bytes 524304 | tf_op jit(solution)/shard_map/psum | solution.py:52
  228.1 1.3 copy.166
  229.7 5.8 %scatter_fusion.2 = f32[2,256,512]{2,0,1:T(2,128)S(1)} fusion(f32[2,256,512]{2,0,1:T(2,128)S(1)} %broadcast.874, s32[128]{0:T(128)S(1)} %get-tuple-element.30, f32[128,2,512]{2,1,0:T(2,128)S(1)} %copy.166), kind=kCustom, calls=%fused_computation.5 | custom fusion | flops 131072 | bytes 1573376 | tf_op jit(solution)/shard_map/scatter-add | solution.py:191
  235.5 1.0 reshape.1067
  236.5 3.4 %convert_select_fusion = f32[48,2,64,128]{3,2,1,0:T(8,128)} fusion(bf16[48,2,64,128]{3,2,1,0:T(8,128)(2,1)} %all-to-all-done.1, pred[48]{0:T(512)(128)(4,1)S(1)} %gt.19), kind=kLoop, calls=%fused_computation.11 | loop fusion | flops 1572864 | bytes 4718640 | tf_op jit(solution)/shard_map/jit(_where)/select_n | solution.py:206
  240.0 6.7 %scatter_fusion.1 = f32[16,2,64,128]{3,2,1,0:T(8,128)S(1)} fusion(f32[16,2,64,128]{3,2,1,0:T(8,128)S(1)} %broadcast_in_dim.117, s32[48]{0:T(128)S(1)} %fusion.73, f32[48,2,64,128]{3,2,1,0:T(8,128)} %convert_select_fusion), kind=kCustom, calls=%fused_computation.4 | custom fusion | flops 786432 | bytes 9437376 | tf_op jit(solution)/shard_map/scatter-add | solution.py:210
  246.8 1.6 fusion.15
  248.6 0.8 reshape.1068
  249.6 0.8 reshape.1069
  (89 shorter events, 4.7 us)
Async XLA Ops:
  7.2 10.7 %copy-start.10 = (bf16[1,256,512]{2,1,0:T(8,128)(2,1)S(1)}, bf16[1,256,512]{2,1,0:T(8,128)(2,1)}, u32[]{:S(2)}) copy-start(bf16[1,256,512]{2,1,0:T(8,128)(2,1)} %param.11) | copy-start | bytes 786436
  7.2 10.7 %copy-start.11 = (bf16[1,256,512]{2,1,0:T(8,128)(2,1)S(1)}, bf16[1,256,512]{2,1,0:T(8,128)(2,1)}, u32[]{:S(2)}) copy-start(bf16[1,256,512]{2,1,0:T(8,128)(2,1)} %param.12) | copy-start | bytes 786436
  7.2 10.9 %copy-start.13 = (s32[1,4,32,3]{2,1,3,0:T(4,128)S(1)}, s32[1,4,32,3]{2,1,3,0:T(4,128)}, u32[]{:S(2)}) copy-start(s32[1,4,32,3]{2,1,3,0:T(4,128)} %param.14) | copy-start | bytes 4612
  10.3 88.7 %collective-permute-start.1 = (bf16[2,1,64,512]{2,3,0,1:T(8,128)(2,1)}, bf16[2,1,64,512]{2,3,0,1:T(8,128)(2,1)}, u32[]{:S(2)}, u32[]{:S(2)}) collective-permute-start(bf16[2,1,64,512]{2,3,0,1:T(8,128)(2,1)} %get-tuple-element.41), channel_id=1, source_target_pairs={{4,0},{8,4},{12,8},{16,12},{20,16},{24,20},{28,24},{5,1},{9,5},{13... | collective-permute-start | bytes 393224 | tf_op jit(solution)/shard_map/ppermute | solution.py:17
  11.6 87.4 %collective-permute-start = (bf16[2,1,64,512]{2,3,0,1:T(8,128)(2,1)}, bf16[2,1,64,512]{2,3,0,1:T(8,128)(2,1)}, u32[]{:S(2)}, u32[]{:S(2)}) collective-permute-start(bf16[2,1,64,512]{2,3,0,1:T(8,128)(2,1)} %get-tuple-element.42), channel_id=1, source_target_pairs={{0,4},{4,8},{8,12},{12,16},{16,20},{20,24},{24,28},{1,5},{5,9},{9,... | collective-permute-start | bytes 393224 | tf_op jit(solution)/shard_map/ppermute | solution.py:16
  22.5 6.2 %copy-start.14 = (s32[128]{0:T(128)S(1)}, s32[128]{0:T(128)}, u32[]{:S(2)}) copy-start(s32[128]{0:T(128)} %param.15) | copy-start | bytes 1540
  22.5 89.6 %all-to-all-start = ((bf16[48,2,64,128]{3,2,1,0:T(8,128)(2,1)}), bf16[48,2,64,128]{3,2,1,0:T(8,128)(2,1)S(1)}, u32[]{:S(2)}, u32[]{:S(2)}) async-start(bf16[48,2,64,128]{3,2,1,0:T(8,128)(2,1)} %gather_fusion), calls=%async_computation | async-start | bytes 3145728 | tf_op jit(solution)/shard_map/all_to_all | solution.py:88
  96.3 1.9 copy-start.12
  108.1 3.0 %copy-start.4 = (bf16[2,1,4,64,4,128]{5,3,2,4,1,0:T(8,128)(2,1)S(1)}, bf16[2,1,4,64,4,128]{5,3,2,4,1,0:T(8,128)(2,1)}, u32[]{:S(2)}) copy-start(bf16[2,1,4,64,4,128]{5,3,2,4,1,0:T(8,128)(2,1)} %copy.145) | copy-start | bytes 1572868
  115.6 1.5 copy-start.9
  115.6 2.7 %copy-start.2 = (bf16[1,4,64,4,128]{4,3,2,1,0:T(4,128)(2,1)S(1)}, bf16[1,4,64,4,128]{4,3,2,1,0:T(4,128)(2,1)}, u32[]{:S(2)}) copy-start(bf16[1,4,64,4,128]{4,3,2,1,0:T(4,128)(2,1)} %reshape.1051) | copy-start | bytes 786436
  121.9 5.9 %copy-start = (bf16[1,4,4,64,512]{4,3,2,1,0:T(8,128)(2,1)}, bf16[1,4,4,64,512]{4,3,2,1,0:T(8,128)(2,1)S(1)}, u32[]{:S(2)}) copy-start(bf16[1,4,4,64,512]{4,3,2,1,0:T(8,128)(2,1)S(1)} %fusion.21) | copy-start | bytes 3145732
  127.8 1.5 copy-start.5
  139.3 5.0 %copy-start.1 = (bf16[1,4,4,64,512]{4,3,2,1,0:T(8,128)(2,1)S(1)}, bf16[1,4,4,64,512]{4,3,2,1,0:T(8,128)(2,1)}, u32[]{:S(2)}) copy-start(bf16[1,4,4,64,512]{4,3,2,1,0:T(8,128)(2,1)} %copy-done) | copy-start | bytes 3145732
  139.3 5.4 %copy-start.3 = (bf16[1,4,64,4,128]{4,3,2,1,0:T(4,128)(2,1)S(1)}, bf16[1,4,64,4,128]{4,3,2,1,0:T(4,128)(2,1)}, u32[]{:S(2)}) copy-start(bf16[1,4,64,4,128]{4,3,2,1,0:T(4,128)(2,1)} %reshape.1051) | copy-start | bytes 786436
  139.3 5.4 %copy-start.6 = (bf16[4,4,64,512]{3,2,1,0:T(8,128)(2,1)S(1)}, bf16[4,4,64,512]{3,2,1,0:T(8,128)(2,1)}, u32[]{:S(2)}) copy-start(bf16[4,4,64,512]{3,2,1,0:T(8,128)(2,1)} %copy-done.5) | copy-start | bytes 3145732
  139.3 97.2 %all-to-all-start.1 = ((bf16[48,2,64,128]{3,2,1,0:T(8,128)(2,1)}), bf16[48,2,64,128]{3,2,1,0:T(8,128)(2,1)}, u32[]{:S(2)}, u32[]{:S(2)}) async-start(bf16[48,2,64,128]{3,2,1,0:T(8,128)(2,1)} %convert_element_type.122), calls=%async_computation.1 | async-start | bytes 3145728 | tf_op jit(solution)/shard_map/all_to_all | solution.py:203
  143.7 84.4 %all-reduce.6.cloned.1.call-start = ((), (), s32[]{:S(2)}) async-start(), calls=%async_computation.2 | async-start | bytes 1048576 | tf_op jit(solution)/shard_map/psum | solution.py:52
  147.8 7.2 %copy-start.7 = (bf16[4,4,64,512]{3,2,1,0:T(8,128)(2,1)S(1)}, bf16[4,4,64,512]{3,2,1,0:T(8,128)(2,1)}, u32[]{:S(2)}) copy-start(bf16[4,4,64,512]{3,2,1,0:T(8,128)(2,1)} %copy-done.5) | copy-start | bytes 3145732
  148.6 17.0 %collective-permute-start.3 = (bf16[2,1,4,1,64,128]{5,4,0,2,3,1:T(8,128)(2,1)}, bf16[2,1,4,1,64,128]{5,4,0,2,3,1:T(8,128)(2,1)S(1)}, u32[]{:S(2)}, u32[]{:S(2)}) collective-permute-start(bf16[2,1,4,1,64,128]{5,4,0,2,3,1:T(8,128)(2,1)} %get-tuple-element.33), channel_id=1, source_target_pairs={{4,0},{8,4},{12,8},{16,12},{20,16},{24,20},{28,24},{5,1},{9,5},{13... | collective-permute-start | bytes 393224 | tf_op jit(solution)/shard_map/ppermute | solution.py:17
  149.8 15.7 %collective-permute-start.2 = (bf16[2,1,4,1,64,128]{5,4,0,2,3,1:T(8,128)(2,1)}, bf16[2,1,4,1,64,128]{5,4,0,2,3,1:T(8,128)(2,1)}, u32[]{:S(2)}, u32[]{:S(2)}) collective-permute-start(bf16[2,1,4,1,64,128]{5,4,0,2,3,1:T(8,128)(2,1)} %get-tuple-element.32), channel_id=1, source_target_pairs={{0,4},{4,8},{8,12},{12,16},{16,20},{20,24},{24,28},{1,5},{5,9},{9,... | collective-permute-start | bytes 393224 | tf_op jit(solution)/shard_map/ppermute | solution.py:16
  157.9 1.4 copy-start.8
Sparse Core Ops, SparseCore 0:
  147.9 80.1 all-reduce.5
where the time goes:
time: 258 us; the launch traced here: 257 us
  blocking collectives  66.9 us (26%)
  waiting for transfers between devices  59.2 us (23%)
  local copies, waits for them, and re-layouts  45.5 us (18%)
  other arithmetic  32.1 us (12%)
  starting transfers between devices  24.3 us (9%)
  matrix products  14.7 us (6%)
  between operations  14.6 us (6%)
    psum x1, blocking collectives, global_sum(): return lax.psum(array, 'seq')  66.9 us
    psum x1, waiting for transfers between devices, global_sum(): return lax.psum(array, 'seq')  59.2 us
    ppermute x2, starting transfers between devices, extended_2(): before = lax.ppermute(last, axis, up)  11.4 us
    unnamed x40, local copies, waits for them, and re-layouts  7.94 us
    reshape x5, local copies, waits for them, and re-layouts, pair_blocks(): array.reshape(2, batch_count, blocks_local, BLOCK, heads_local, head_dim)  7.5 us
    scatter-add x1, other arithmetic, body(): summed = jnp.zeros((batch_count * blocks_local * heads_local, 2, BLOCK, h...  6.73 us
    scatter-add x1, other arithmetic, body(): global_local = jnp.zeros((2, batch_count, tok_local, columns), f32).at[:,...  5.83 us
    scatter x1, local copies, waits for them, and re-layouts, body(): jnp.zeros((buffer_rows, 2, BLOCK, head_dim), f32).at[position].set(per_slot)  5.72 us
  transfers between devices with their start and end apart: 7, of which 1 were waited for; matrix products, arithmetic and copies ran while one was open for 19% of the time, Pallas kernels for 0%

commit v1 on v0

--- a/solution.py
+++ b/solution.py
@@ -1,9 +1,372 @@
+import functools
+
 import jax
 import jax.numpy as jnp
 from jax import lax
+from jax.experimental import pallas as pl
+from jax.experimental.pallas import tpu as pltpu
 from jax.sharding import PartitionSpec as P
 
+
 BLOCK = 64
+AXES = ("seq", "head")
+GROUPS = 2
+CHUNK = 2
+GRANT = 24 * 1024 * 1024
+VMEM = pl.BlockSpec(memory_space=pltpu.VMEM)
+SMEM = pl.BlockSpec(memory_space=pltpu.SMEM)
+PARAMS = pltpu.CompilerParams(vmem_limit_bytes=GRANT)
+PACK_PARAMS = pltpu.CompilerParams(vmem_limit_bytes=GRANT)
+HBM = pl.BlockSpec(memory_space=pltpu.HBM)
+F32 = jnp.float32
+BF16 = jnp.bfloat16
+
+
+def dot(a, b, dims):
+    return lax.dot_general(a, b, (dims, ((), ())), preferred_element_type=F32)
+
+
+def round_pairs(seq_count, head_count, i):
+    rounds = seq_count // 2
+    pairs = []
+    for s in range(seq_count):
+        for head in range(head_count):
+            y, c = head // 2, head % 2
+            k = rounds * c + (s % rounds ^ i)
+            pairs.append((s * head_count + head, k * head_count + 2 * y + s // rounds))
+    return pairs
+
+
+def keep_in_hbm(array):
+    return pltpu.with_memory_space_constraint(array, pltpu.HBM)
+
+
+def pack_kernel(rounds, width, where_ref, *rest):
+    ins, outs, sem = rest[:4], rest[4:-1], rest[-1]
+    turn = lax.rem(where_ref[0], rounds)
+    copies = []
+    for m in range(2):
+        for i in range(rounds):
+            col = pl.multiple_of((turn ^ i) * width, width)
+            for n in range(2):
+                copy = pltpu.make_async_copy(
+                    ins[2 * m + n].at[0, :, pl.ds(col, width)],
+                    outs[m * rounds + i].at[n],
+                    sem.at[m * rounds + i, n],
+                )
+                copy.start()
+                copies.append(copy)
+    for copy in copies:
+        copy.wait()
+
+
+def pack(where, arrays, rounds):
+    _, tokens, columns = arrays[0].shape
+    width = columns // rounds
+    out = jax.ShapeDtypeStruct((2, tokens, width), BF16)
+    outs = pl.pallas_call(
+        functools.partial(pack_kernel, rounds, width),
+        out_shape=[out] * (2 * rounds),
+        in_specs=[SMEM] + [HBM] * 4,
+        out_specs=[VMEM] * (2 * rounds),
+        scratch_shapes=[pltpu.SemaphoreType.DMA((2 * rounds, 2))],
+        compiler_params=PACK_PARAMS,
+        cost_estimate=pl.CostEstimate(
+            flops=0, transcendentals=0, bytes_accessed=16 * tokens * columns
+        ),
+        name="pack",
+    )(where, *[keep_in_hbm(a) for a in arrays])
+    return outs[:rounds], outs[rounds:]
+
+
+def unpack_kernel(rounds, width, where_ref, *rest):
+    ins, outs, sem = rest[:rounds], rest[rounds:-1], rest[-1]
+    turn = lax.rem(where_ref[0], rounds)
+    copies = []
+    for i in range(rounds):
+        col = pl.multiple_of((turn ^ i) * width, width)
+        for n in range(2):
+            copy = pltpu.make_async_copy(
+                ins[i].at[n], outs[n].at[0, :, pl.ds(col, width)], sem.at[i, n]
+            )
+            copy.start()
+            copies.append(copy)
+    for copy in copies:
+        copy.wait()
+
+
+def unpack(where, parts):
+    rounds = len(parts)
+    _, tokens, width = parts[0].shape
+    out = jax.ShapeDtypeStruct((1, tokens, rounds * width), BF16)
+    return pl.pallas_call(
+        functools.partial(unpack_kernel, rounds, width),
+        out_shape=[out] * 2,
+        in_specs=[SMEM] + [VMEM] * rounds,
+        out_specs=[HBM] * 2,
+        scratch_shapes=[pltpu.SemaphoreType.DMA((rounds, 2))],
+        compiler_params=PARAMS,
+        cost_estimate=pl.CostEstimate(
+            flops=0, transcendentals=0, bytes_accessed=8 * rounds * tokens * width
+        ),
+        name="unpack",
+    )(where, *parts)
+
+
+def attend_kernel(
+    rounds, run_blocks, picks, turns, opens, closes, where_ref, mine_ref, other_table_ref, *rest
+):
+    rest = list(rest)
+    take = lambda n: [rest.pop(0) for _ in range(n)]
+    count = len(turns)
+    if opens:
+        (global_ref,), parts = take(1), take(2 * rounds)
+    else:
+        all_ref, picked_ref, _ = take(3)
+    sides = take(count)
+    mixes = take(count)
+    if opens:
+        all_ref, picked_ref = take(2)
+    (acc,) = take(1)
+    if closes:
+        (send_ref,) = take(1)
+    (keep,) = take(1)
+
+    k, h = where_ref[0], where_ref[1]
+    tokens = run_blocks * BLOCK
+    half = rounds * tokens
+    total_blocks = 2 * rounds * run_blocks
+    listed = (3 + picks) * BLOCK
+    flip = (h * rounds + lax.rem(k, rounds)) * run_blocks
+    head = lax.rem(k, rounds) * (total_blocks * picks)
+    mine = k // rounds == h
+    scale = all_ref.shape[2] ** -0.5
+    column = lax.broadcasted_iota(jnp.int32, (1, 4 * BLOCK), 1)
+
+    if opens:
+        spots = global_ref[...] ^ (flip * BLOCK)
+        sums = [None, None]
+        for n in range(2 * rounds):
+            ids = lax.broadcasted_iota(jnp.int32, (spots.shape[0], tokens), 1) + n * tokens
+            hot = jnp.where(ids == spots, 1.0, 0.0).astype(BF16)
+            for m in range(2):
+                part = parts[n][m]
+                all_ref[m, n * tokens : (n + 1) * tokens] = part
+                product = dot(hot, part, ((1,), (0,)))
+                sums[m] = product if n == 0 else sums[m] + product
+        for m in range(2):
+            picked_ref[m] = sums[m].astype(BF16)
+        acc[...] = jnp.zeros_like(acc)
+
+    def begin(n, block):
+        rows_of = slice(block * BLOCK, (block + 1) * BLOCK)
+        query, grad = sides[n][0, rows_of], sides[n][1, rows_of]
+        index = (turns[n] * run_blocks + block) ^ flip
+        named = [
+            jnp.maximum(index - 1, 0),
+            index,
+            jnp.minimum(index + 1, total_blocks - 1),
+        ]
+        for m in range(picks):
+            at = head + index * picks + m
+            named.append(jnp.where(mine, mine_ref[at], other_table_ref[at]))
+        rows = [pl.multiple_of((b ^ flip) * BLOCK, BLOCK) for b in named]
+        keys, values = [
+            jnp.concatenate(
+                [all_ref[m, pl.ds(r, BLOCK)] for r in rows] + [picked_ref[m]], axis=0
+            )
+            for m in range(2)
+        ]
+        scores = dot(query, keys, ((1,), (1,))) * scale
+        probs = dot(grad, values, ((1,), (1,)))
+        out = ((column < BLOCK) & (index == 0)) | (
+            (column >= 2 * BLOCK) & (column < 3 * BLOCK) & (index == total_blocks - 1)
+        )
+        near = jnp.where(out, -1e30, scores[:, : 4 * BLOCK])
+        scores = jnp.concatenate([near, scores[:, 4 * BLOCK :]], axis=1)
+        return n, rows_of, rows, query, grad, keys, values, scores, probs
+
+    def finish(state):
+        weighed, scored = [], []
+        for n, rows_of, rows, query, grad, keys, values, scores, probs in state:
+            peak = jnp.max(scores, axis=1, keepdims=True)
+            powers = jnp.exp(scores - peak)
+            weights = powers * (1.0 / jnp.sum(powers, axis=1, keepdims=True))
+            weighed.append((weights, weights.astype(BF16)))
+        for (*_, probs), (weights, weights_b) in zip(state, weighed):
+            delta = jnp.sum(weights_b.astype(F32) * probs, axis=1, keepdims=True)
+            scored.append((weights * (probs - delta)).astype(BF16))
+        for (n, rows_of, rows, query, grad, keys, values, _, _), (_, weights_b), dscore_b in zip(
+            state, weighed, scored
+        ):
+            mixed = dot(weights_b, values, ((1,), (0,)))
+            grad_query = dot(dscore_b, keys, ((1,), (0,))) * scale
+            mixes[n][0, rows_of] = mixed.astype(BF16)
+            mixes[n][1, rows_of] = grad_query.astype(BF16)
+            keep[n, 0, rows_of] = dscore_b[:, listed:]
+            keep[n, 1, rows_of] = weights_b[:, listed:]
+            key_part = dot(dscore_b[:, :listed], query, ((0,), (0,)))
+            value_part = dot(weights_b[:, :listed], grad, ((0,), (0,)))
+            for m, r in enumerate(rows):
+                span = slice(m * BLOCK, (m + 1) * BLOCK)
+                acc[0, pl.ds(r, BLOCK)] += key_part[span]
+                acc[1, pl.ds(r, BLOCK)] += value_part[span]
+
+    held = None
+    for n in range(count):
+        for block in range(0, run_blocks, CHUNK):
+            state = [begin(n, b) for b in range(block, block + CHUNK)]
+            if held is not None:
+                finish(held)
+            held = state
+    finish(held)
+    for m in range(2):
+        shared = acc[m, 2 * half :]
+        for n in range(count):
+            shared = shared + dot(keep[n, m], sides[n][m], ((0,), (0,)))
+        acc[m, 2 * half :] = shared
+        if closes:
+            send_ref[m, :half] = acc[m, half : 2 * half]
+            send_ref[m, half:] = shared
+
+
+def attend(where, tables, global_pos, parts, state, sides, turns, rounds, picks):
+    opens, closes = state is None, turns[-1] == rounds - 1
+    _, tokens, width = sides[0].shape
+    run_blocks = tokens // BLOCK
+    shared = global_pos.shape[0]
+    entries = (3 + picks) * BLOCK + shared
+    count = len(turns)
+    half = rounds * tokens
+    one = jax.ShapeDtypeStruct((2, tokens, width), BF16)
+    acc = jax.ShapeDtypeStruct((2, 2 * half + shared, width), F32)
+    out_shape = [one] * count
+    if opens:
+        given = [global_pos.reshape(shared, 1), *parts]
+        out_shape += [
+            jax.ShapeDtypeStruct((2, 2 * half, width), BF16),
+            jax.ShapeDtypeStruct((2, shared, width), BF16),
+        ]
+        aliases = {}
+    else:
+        given = list(state)
+        aliases = {3 + len(given) - 1: count}
+    out_shape += [acc]
+    if closes:
+        out_shape += [jax.ShapeDtypeStruct((2, half + shared, width), F32)]
+    outs = pl.pallas_call(
+        functools.partial(
+            attend_kernel, rounds, run_blocks, picks, turns, opens, closes
+        ),
+        out_shape=out_shape,
+        in_specs=[SMEM] * 3 + [VMEM] * (len(given) + count),
+        out_specs=[VMEM] * len(out_shape),
+        input_output_aliases=aliases,
+        scratch_shapes=[pltpu.VMEM((count, 2, tokens, shared), BF16)],
+        compiler_params=PARAMS,
+        cost_estimate=pl.CostEstimate(
+            flops=12 * count * tokens * entries * width,
+            transcendentals=count * tokens * entries,
+            bytes_accessed=12 * half * width,
+        ),
+        name="attend",
+    )(where, *tables, *given, *sides)
+    return outs[:count], outs[count:]
+
+
+def total_kernel(rounds, where_ref, global_ref, acc_ref, came_ref, *outs):
+    tokens, width = outs[0].shape[1:]
+    half = rounds * tokens
+    count = global_ref.shape[1]
+    scale = width**-0.5
+    flip = (where_ref[1] * rounds + lax.rem(where_ref[0], rounds)) * tokens
+    spots = global_ref[...] ^ flip
+    halves = []
+    for n in range(2):
+        shared = acc_ref[n, 2 * half :] + came_ref[n, half:]
+        high = shared.astype(BF16)
+        halves += [high, (shared - high.astype(F32)).astype(BF16)]
+    halves = jnp.concatenate(halves, axis=1)
+    for i in range(rounds):
+        ids = lax.broadcasted_iota(jnp.int32, (tokens, count), 0) + i * tokens
+        hot = jnp.where(ids == spots, 1.0, 0.0).astype(BF16)
+        spread = dot(hot, halves, ((1,), (0,)))
+        mine = slice(i * tokens, (i + 1) * tokens)
+        for n in range(2):
+            whole = acc_ref[n, mine] + came_ref[n, mine]
+            whole = whole + spread[:, 2 * n * width : (2 * n + 1) * width]
+            whole = whole + spread[:, (2 * n + 1) * width : (2 * n + 2) * width]
+            if n == 0:
+                whole = whole * scale
+            outs[i][n] = whole.astype(BF16)
+
+
+def total(where, global_pos, acc, came, rounds):
+    rows, width = came.shape[1:]
+    count = global_pos.shape[0]
+    tokens = (rows - count) // rounds
+    return pl.pallas_call(
+        functools.partial(total_kernel, rounds),
+        out_shape=[jax.ShapeDtypeStruct((2, tokens, width), BF16)] * rounds,
+        in_specs=[SMEM] + [VMEM] * 3,
+        out_specs=[VMEM] * rounds,
+        compiler_params=PARAMS,
+        cost_estimate=pl.CostEstimate(
+            flops=4 * rows * width, transcendentals=0, bytes_accessed=20 * rows * width
+        ),
+        name="total",
+    )(where, global_pos.reshape(1, count), acc, came)
+
+
+def by_heads(query_rows, key_rows, value_rows, grad_out, rand_blocks, global_pos):
+    seq_count, head_count = lax.axis_size("seq"), lax.axis_size("head")
+    _, rounds, _, picks = rand_blocks.shape
+    k, head_index = lax.axis_index("seq"), lax.axis_index("head")
+    where = jnp.stack([k, head_index & 1]).astype(jnp.int32)
+    sibling = [(i, i ^ 1) for i in range(head_count)]
+    trades = [round_pairs(seq_count, head_count, i) for i in range(rounds)]
+
+    def send(parts, first=0):
+        out = []
+        for n, part in enumerate(parts):
+            out.append(lax.ppermute(part, AXES, trades[first + n]))
+        return out
+
+    def swap(parts):
+        out = []
+        for part in parts:
+            out.append(lax.ppermute(part, "head", sibling))
+        return out
+
+    kv, sides = pack(where, [key_rows, value_rows, query_rows, grad_out], rounds)
+    kv = send(kv)
+    sides = send(sides)
+    table = rand_blocks.reshape(rand_blocks.size)
+    tables = [table, *swap([table])]
+    parts = kv + swap(kv)
+    mixes, state = [], None
+    for n in range(GROUPS):
+        turns = tuple(range(n * rounds // GROUPS, (n + 1) * rounds // GROUPS))
+        mix, new = attend(
+            where,
+            tables,
+            global_pos,
+            parts,
+            state,
+            [sides[t] for t in turns],
+            turns,
+            rounds,
+            picks,
+        )
+        mixes += send(mix, turns[0])
+        state = new if state is None else (*state[:2], *new)
+    _, _, acc, leaving = state
+    (came,) = swap([leaving])
+    grads = total(where, global_pos, acc, came, rounds)
+    grads = send(grads)
+    attended, grad_query = unpack(where, mixes)
+    grad_key, grad_value = unpack(where, grads)
+    return attended, grad_query, grad_key, grad_value
 
 
 def extended_2(value, sides, width):
@@ -19,7 +382,7 @@
     return value
 
 
-def body(query_rows, key_rows, value_rows, grad_out, rand_blocks, global_pos):
+def by_blocks(query_rows, key_rows, value_rows, grad_out, rand_blocks, global_pos):
     batch_count, tok_local, columns = query_rows.shape
     seq_count = lax.axis_size("seq")
     seq_index = lax.axis_index("seq")
@@ -218,6 +581,17 @@
     return (attended, from_blocks(grad_query.astype(bf16)), grad_key, grad_value)
 
 
+def body(query_rows, key_rows, value_rows, grad_out, rand_blocks, global_pos):
+    seq_count, head_count = lax.axis_size("seq"), lax.axis_size("head")
+    batch_count, heads_local = rand_blocks.shape[:2]
+    tokens = query_rows.shape[1]
+    whole_heads = seq_count == 2 * heads_local and heads_local & (heads_local - 1) == 0
+    whole_heads = whole_heads and heads_local > 1 and tokens & (tokens - 1) == 0
+    whole_heads = whole_heads and head_count % 2 == 0 and batch_count == 1
+    form = by_heads if whole_heads else by_blocks
+    return form(query_rows, key_rows, value_rows, grad_out, rand_blocks, global_pos)
+
+
 def solution(mesh):
     return jax.shard_map(
         body,

time: 258 us -> 69.1 us (0.27)
  the two profiles are of different devices: /device:TPU:0 before, /device:TPU:9 now
where the time goes in v1:
time: 69.1 us; the launch traced here: 68.8 us
  starting transfers between devices  37.2 us (54%)
  waiting for transfers between devices  16.1 us (23%)
  Pallas kernels  12.8 us (19%)
  local copies, waits for them, and re-layouts  1.76 us (3%)
  between operations  0.81 us (1%)
    ppermute x16, starting transfers between devices, send(): out.append(lax.ppermute(part, AXES, trades[first + n]))  36.5 us
    ppermute x16, waiting for transfers between devices, send(): out.append(lax.ppermute(part, AXES, trades[first + n]))  16.1 us
    pallas_call x2, Pallas kernels, attend(): pl.pallas_call(functools.partial(attend_kernel, rounds, run_blocks, picks...  7.09 us
    pallas_call x2, Pallas kernels, unpack(): pl.pallas_call(functools.partial(unpack_kernel, rounds, width), out_shape...  2.79 us
    pallas_call x1, Pallas kernels, pack(): pl.pallas_call(functools.partial(pack_kernel, rounds, width), out_shape=[...  1.95 us
  transfers between devices with their start and end apart: 22, of which 7 were waited for; matrix products, arithmetic and copies ran while one was open for 3% of the time, Pallas kernels for 9%

profile of v1, /device:TPU:9, one launch (start us, length us, event | category | flops | bytes accessed | tf_op | source)
XLA Modules:
  0.0 68.8 jit_solution(14517724773983658374)
XLA Ops:
  0.6 0.1 pad_add_fusion.where_ref
  0.7 2.0 %pack.1 = (bf16[2,256,128]{2,1,0:T(8,128)(2,1)S(1)}, bf16[2,256,128]{2,1,0:T(8,128)(2,1)S(1)}, bf16[2,256,128]{2,1,0:T(8,128)(2,1)S(1)}, bf16[2,256,128]{2,1,0:T...) custom-call(s32[2]{0:T(128)S(1)} %pad_add_fusion.where_ref, ...), custom_call_target="tpu_custom_call" | custom-call | bytes 2097152 | tf_op jit(solution)/shard_map/pack/pallas_call | solution.py:67
  2.7 4.8 %collective-permute-start.1 = (bf16[2,256,128]{2,1,0:T(8,128)(2,1)S(1)}, bf16[2,256,128]{2,1,0:T(8,128)(2,1)S(1)}, u32[]{:S(2)}, u32[]{:S(2)}) collective-permute-start(bf16[2,256,128]{2,1,0:T(8,128)(2,1)S(1)} %get-tuple-element.29), channel_id=1, source_target_pairs={{0,0},{1,16},{2,2},{3,18},{4,4},{5,20},{6,6},{7,22},{8,8},{9,24},{... | collective-permute-start | bytes 393224 | tf_op jit(solution)/shard_map/ppermute | solution.py:332
  7.5 1.0 %collective-permute-start.2 = (bf16[2,256,128]{2,1,0:T(8,128)(2,1)S(1)}, bf16[2,256,128]{2,1,0:T(8,128)(2,1)S(1)}, u32[]{:S(2)}, u32[]{:S(2)}) collective-permute-start(bf16[2,256,128]{2,1,0:T(8,128)(2,1)S(1)} %get-tuple-element.30), channel_id=1, source_target_pairs={{0,4},{1,20},{2,6},{3,22},{4,0},{5,16},{6,2},{7,18},{8,12},{9,28},... | collective-permute-start | bytes 393224 | tf_op jit(solution)/shard_map/ppermute | solution.py:332
  8.5 0.8 %copy.12 = s32[1,4,32,3]{3,2,1,0:T(8,128)S(1)} copy(s32[1,4,32,3]{2,1,3,0:T(4,128)} %param.10) | data formatting | bytes 3072 | tf_op args[4]
  9.3 0.2 reshape.17.mine_ref
  9.5 0.1 collective-permute-start
  9.5 1.7 %collective-permute-start.3 = (bf16[2,256,128]{2,1,0:T(8,128)(2,1)S(1)}, bf16[2,256,128]{2,1,0:T(8,128)(2,1)S(1)}, u32[]{:S(2)}, u32[]{:S(2)}) collective-permute-start(bf16[2,256,128]{2,1,0:T(8,128)(2,1)S(1)} %get-tuple-element.31), channel_id=1, source_target_pairs={{0,8},{1,24},{2,10},{3,26},{4,12},{5,28},{6,14},{7,30},{8,0},{9,16... | collective-permute-start | bytes 393224 | tf_op jit(solution)/shard_map/ppermute | solution.py:332
  11.2 0.1 collective-permute-start.4
  11.4 0.0 collective-permute-done.other_table_ref
  11.4 6.3 %collective-permute-start.9 = (bf16[2,256,128]{2,1,0:T(8,128)(2,1)S(1)}, bf16[2,256,128]{2,1,0:T(8,128)(2,1)S(1)}, u32[]{:S(2)}, u32[]{:S(2)}) collective-permute-start(bf16[2,256,128]{2,1,0:T(8,128)(2,1)S(1)} %get-tuple-element.33), channel_id=1, source_target_pairs={{0,0},{1,16},{2,2},{3,18},{4,4},{5,20},{6,6},{7,22},{8,8},{9,24},{... | collective-permute-start | bytes 393224 | tf_op jit(solution)/shard_map/ppermute | solution.py:332
  17.7 0.0 collective-permute-done.1.rest_1_
  17.7 1.0 %collective-permute-start.10 = (bf16[2,256,128]{2,1,0:T(8,128)(2,1)S(1)}, bf16[2,256,128]{2,1,0:T(8,128)(2,1)S(1)}, u32[]{:S(2)}, u32[]{:S(2)}) collective-permute-start(bf16[2,256,128]{2,1,0:T(8,128)(2,1)S(1)} %get-tuple-element.34), channel_id=1, source_target_pairs={{0,4},{1,20},{2,6},{3,22},{4,0},{5,16},{6,2},{7,18},{8,12},{9,28},... | collective-permute-start | bytes 393224 | tf_op jit(solution)/shard_map/ppermute | solution.py:332
  18.7 0.0 collective-permute-done.2.rest_2_
  18.7 0.0 collective-permute-start.5
  18.7 0.0 collective-permute-done.3.rest_3_
  18.7 0.5 collective-permute-start.6
  19.2 2.7 %collective-permute-done.4.rest_4_ = bf16[2,256,128]{2,1,0:T(8,128)(2,1)S(1)} collective-permute-done((bf16[2,256,128]{2,1,0:T(8,128)(2,1)S(1)}, bf16[2,256,128]{2,1,0:T(8,128)(2,1)S(1)}, u32[]{:S(2)}, u32[]{:S(2)}) %collective-permute-start.4) | collective-permute-done | bytes 131104 | tf_op jit(solution)/shard_map/ppermute | solution.py:332
  21.9 0.0 collective-permute-start.7
  21.9 1.4 %collective-permute-done.9.rest_9_ = bf16[2,256,128]{2,1,0:T(8,128)(2,1)S(1)} collective-permute-done((bf16[2,256,128]{2,1,0:T(8,128)(2,1)S(1)}, bf16[2,256,128]{2,1,0:T(8,128)(2,1)S(1)}, u32[]{:S(2)}, u32[]{:S(2)}) %collective-permute-start.9) | collective-permute-done | bytes 131104 | tf_op jit(solution)/shard_map/ppermute | solution.py:332
  23.3 0.0 collective-permute-start.8
  23.3 1.4 %collective-permute-done.10.rest_10_ = bf16[2,256,128]{2,1,0:T(8,128)(2,1)S(1)} collective-permute-done((bf16[2,256,128]{2,1,0:T(8,128)(2,1)S(1)}, bf16[2,256,128]{2,1,0:T(8,128)(2,1)S(1)}, u32[]{:S(2)}, u32[]{:S(2)}) %collective-permute-start.10) | collective-permute-done | bytes 131104 | tf_op jit(solution)/shard_map/ppermute | solution.py:332
  24.7 1.1 %collective-permute-start.13 = (bf16[2,256,128]{2,1,0:T(8,128)(2,1)S(1)}, bf16[2,256,128]{2,1,0:T(8,128)(2,1)S(1)}, u32[]{:S(2)}, u32[]{:S(2)}) collective-permute-start(bf16[2,256,128]{2,1,0:T(8,128)(2,1)S(1)} %get-tuple-element.40), channel_id=1, source_target_pairs={{0,8},{1,24},{2,10},{3,26},{4,12},{5,28},{6,14},{7,30},{8,0},{9,16... | collective-permute-start | bytes 393224 | tf_op jit(solution)/shard_map/ppermute | solution.py:332
  25.8 0.0 collective-permute-done.5.rest_5_
  25.8 1.6 %collective-permute-start.14 = (bf16[2,256,128]{2,1,0:T(8,128)(2,1)S(1)}, bf16[2,256,128]{2,1,0:T(8,128)(2,1)S(1)}, u32[]{:S(2)}, u32[]{:S(2)}) collective-permute-start(bf16[2,256,128]{2,1,0:T(8,128)(2,1)S(1)} %get-tuple-element.41), channel_id=1, source_target_pairs={{0,12},{1,28},{2,14},{3,30},{4,8},{5,24},{6,10},{7,26},{8,4},{9,20... | collective-permute-start | bytes 393224 | tf_op jit(solution)/shard_map/ppermute | solution.py:332
  27.4 0.8 %copy.13.rest_0_ = s32[128,1]{1,0:T(8,128)S(1)} copy(s32[128,1]{0,1:T(1,128)} %bitcast.6) | data formatting | bytes 1024 | tf_op jit(solution)/shard_map/reshape | solution.py:245
  28.2 0.0 copy-start
  28.2 0.0 collective-permute-done.6.rest_6_
  28.2 0.0 collective-permute-done.7.rest_7_
  28.2 0.0 collective-permute-done.8.rest_8_
  28.2 3.9 %attend.2 = (bf16[2,256,128]{2,1,0:T(8,128)(2,1)S(1)}, bf16[2,256,128]{2,1,0:T(8,128)(2,1)S(1)}, bf16[2,2048,128]{2,1,0:T(8,128)(2,1)S(1)}, bf16[2,128,128]{2,1,0:T(8,128)(2,1)S(1)}, f32[2,2176,128]{2,1,0:T(8,128)S(1)}) custom-call(s32[2]{0:T(128)S(1)} %pad_add_fusion.where_ref, s32[384]{0:T(512)S(1)} %reshape.17.mine_ref, ...), custom_call_target="tpu_custom_call" | custom-call | flops 402653184 | bytes 1572864 | tf_op jit(solution)/shard_map/attend/pallas_call | solution.py:257
  32.1 0.0 collective-permute-done.13.rest_3_
  32.1 0.0 collective-permute-done.14.rest_4_
  32.1 3.2 %attend.3 = (bf16[2,256,128]{2,1,0:T(8,128)(2,1)S(1)}, bf16[2,256,128]{2,1,0:T(8,128)(2,1)S(1)}, f32[2,2176,128]{2,1,0:T(8,128)S(1)}, f32[2,1152,128]{2,1,0:T(8,128)S(1)}) custom-call(s32[2]{0:T(128)S(1)} %pad_add_fusion.where_ref, s32[384]{0:T(512)S(1)} %reshape.17.mine_ref, ...), custom_call_target="tpu_custom_call", output_to_operand_aliasing={{2}: (5, {})} | custom-call | flops 402653184 | bytes 1572864 | tf_op jit(solution)/shard_map/attend/pallas_call | solution.py:257
  35.3 0.1 collective-permute-start.17
  35.4 7.0 %collective-permute-start.11 = (bf16[2,256,128]{2,1,0:T(8,128)(2,1)S(1)}, bf16[2,256,128]{2,1,0:T(8,128)(2,1)S(1)}, u32[]{:S(2)}, u32[]{:S(2)}) collective-permute-start(bf16[2,256,128]{2,1,0:T(8,128)(2,1)S(1)} %get-tuple-element.35), channel_id=1, source_target_pairs={{0,0},{1,16},{2,2},{3,18},{4,4},{5,20},{6,6},{7,22},{8,8},{9,24},{... | collective-permute-start | bytes 393224 | tf_op jit(solution)/shard_map/ppermute | solution.py:332
  42.4 1.0 %collective-permute-start.12 = (bf16[2,256,128]{2,1,0:T(8,128)(2,1)S(1)}, bf16[2,256,128]{2,1,0:T(8,128)(2,1)S(1)}, u32[]{:S(2)}, u32[]{:S(2)}) collective-permute-start(bf16[2,256,128]{2,1,0:T(8,128)(2,1)S(1)} %get-tuple-element.36), channel_id=1, source_target_pairs={{0,4},{1,20},{2,6},{3,22},{4,0},{5,16},{6,2},{7,18},{8,12},{9,28},... | collective-permute-start | bytes 393224 | tf_op jit(solution)/shard_map/ppermute | solution.py:332
  43.5 0.7 collective-permute-start.15
  44.1 1.1 %collective-permute-start.16 = (bf16[2,256,128]{2,1,0:T(8,128)(2,1)S(1)}, bf16[2,256,128]{2,1,0:T(8,128)(2,1)S(1)}, u32[]{:S(2)}, u32[]{:S(2)}) collective-permute-start(bf16[2,256,128]{2,1,0:T(8,128)(2,1)S(1)} %get-tuple-element.43), channel_id=1, source_target_pairs={{0,12},{1,28},{2,14},{3,30},{4,8},{5,24},{6,10},{7,26},{8,4},{9,20... | collective-permute-start | bytes 393224 | tf_op jit(solution)/shard_map/ppermute | solution.py:332
  45.3 0.0 collective-permute-done.17.came_ref
  45.3 0.0 copy-done
  45.3 1.0 %total.1 = (bf16[2,256,128]{2,1,0:T(8,128)(2,1)S(1)}, bf16[2,256,128]{2,1,0:T(8,128)(2,1)S(1)}, bf16[2,256,128]{2,1,0:T(8,128)(2,1)S(1)}, bf16[2,256,128]{2,1,0:T(8,128)(2,1)S(1)}) custom-call(s32[2]{0:T(128)S(1)} %pad_add_fusion.where_ref, s32[1,128]{1,0:T(1,128)S(1)} %bitcast.7, f32[2,2176,128]{2,1,0:T(8,128)S(1)} %get-tuple-element.46.acc_ref, ...), custom_call_target="tpu_custom_call" | custom-call | flops 589824 | bytes 2949120 | tf_op jit(solution)/shard_map/total/pallas_call | solution.py:308
  46.3 6.2 %collective-permute-start.18 = (bf16[2,256,128]{2,1,0:T(8,128)(2,1)S(1)}, bf16[2,256,128]{2,1,0:T(8,128)(2,1)S(1)}, u32[]{:S(2)}, u32[]{:S(2)}) collective-permute-start(bf16[2,256,128]{2,1,0:T(8,128)(2,1)S(1)} %get-tuple-element.48), channel_id=1, source_target_pairs={{0,0},{1,16},{2,2},{3,18},{4,4},{5,20},{6,6},{7,22},{8,8},{9,24},{... | collective-permute-start | bytes 393224 | tf_op jit(solution)/shard_map/ppermute | solution.py:332
  52.5 0.0 collective-permute-done.11.rest_0_
  52.5 1.0 %collective-permute-start.19 = (bf16[2,256,128]{2,1,0:T(8,128)(2,1)S(1)}, bf16[2,256,128]{2,1,0:T(8,128)(2,1)S(1)}, u32[]{:S(2)}, u32[]{:S(2)}) collective-permute-start(bf16[2,256,128]{2,1,0:T(8,128)(2,1)S(1)} %get-tuple-element.49), channel_id=1, source_target_pairs={{0,4},{1,20},{2,6},{3,22},{4,0},{5,16},{6,2},{7,18},{8,12},{9,28},... | collective-permute-start | bytes 393224 | tf_op jit(solution)/shard_map/ppermute | solution.py:332
  53.5 0.0 collective-permute-done.12.rest_1_
  53.5 0.7 collective-permute-start.20
  54.2 0.0 collective-permute-done.15.rest_2_
  54.2 1.1 %collective-permute-start.21 = (bf16[2,256,128]{2,1,0:T(8,128)(2,1)S(1)}, bf16[2,256,128]{2,1,0:T(8,128)(2,1)S(1)}, u32[]{:S(2)}, u32[]{:S(2)}) collective-permute-start(bf16[2,256,128]{2,1,0:T(8,128)(2,1)S(1)} %get-tuple-element.51), channel_id=1, source_target_pairs={{0,12},{1,28},{2,14},{3,30},{4,8},{5,24},{6,10},{7,26},{8,4},{9,20... | collective-permute-start | bytes 393224 | tf_op jit(solution)/shard_map/ppermute | solution.py:332
  55.4 3.6 %collective-permute-done.16.rest_3_ = bf16[2,256,128]{2,1,0:T(8,128)(2,1)S(1)} collective-permute-done((bf16[2,256,128]{2,1,0:T(8,128)(2,1)S(1)}, bf16[2,256,128]{2,1,0:T(8,128)(2,1)S(1)}, u32[]{:S(2)}, u32[]{:S(2)}) %collective-permute-start.16) | collective-permute-done | bytes 131104 | tf_op jit(solution)/shard_map/ppermute | solution.py:332
  58.9 1.4 %unpack.2 = (bf16[1,256,512]{2,1,0:T(8,128)(2,1)}, bf16[1,256,512]{2,1,0:T(8,128)(2,1)}) custom-call(s32[2]{0:T(128)S(1)} %pad_add_fusion.where_ref, bf16[2,256,128]{2,1,0:T(8,128)(2,1)S(1)} %collective-permute-done.11.rest_0_, bf16[2,256,128]{2,1,0:T(8,128)(2,1)S(1)} %collective-permute-done.12.rest_1_, ...), custom_call_target="tpu_custom_call" | custom-call | bytes 1048576 | tf_op jit(solution)/shard_map/unpack/pallas_call | solution.py:102
  60.3 0.0 collective-permute-done.18.rest_0_
  60.3 2.1 %collective-permute-done.19.rest_1_ = bf16[2,256,128]{2,1,0:T(8,128)(2,1)S(1)} collective-permute-done((bf16[2,256,128]{2,1,0:T(8,128)(2,1)S(1)}, bf16[2,256,128]{2,1,0:T(8,128)(2,1)S(1)}, u32[]{:S(2)}, u32[]{:S(2)}) %collective-permute-start.19) | collective-permute-done | bytes 131104 | tf_op jit(solution)/shard_map/ppermute | solution.py:332
  62.5 3.0 %collective-permute-done.20.rest_2_ = bf16[2,256,128]{2,1,0:T(8,128)(2,1)S(1)} collective-permute-done((bf16[2,256,128]{2,1,0:T(8,128)(2,1)S(1)}, bf16[2,256,128]{2,1,0:T(8,128)(2,1)S(1)}, u32[]{:S(2)}, u32[]{:S(2)}) %collective-permute-start.20) | collective-permute-done | bytes 131104 | tf_op jit(solution)/shard_map/ppermute | solution.py:332
  65.5 1.9 %collective-permute-done.21.rest_3_ = bf16[2,256,128]{2,1,0:T(8,128)(2,1)S(1)} collective-permute-done((bf16[2,256,128]{2,1,0:T(8,128)(2,1)S(1)}, bf16[2,256,128]{2,1,0:T(8,128)(2,1)S(1)}, u32[]{:S(2)}, u32[]{:S(2)}) %collective-permute-start.21) | collective-permute-done | bytes 131104 | tf_op jit(solution)/shard_map/ppermute | solution.py:332
  67.4 1.4 %unpack.3 = (bf16[1,256,512]{2,1,0:T(8,128)(2,1)}, bf16[1,256,512]{2,1,0:T(8,128)(2,1)}) custom-call(s32[2]{0:T(128)S(1)} %pad_add_fusion.where_ref, bf16[2,256,128]{2,1,0:T(8,128)(2,1)S(1)} %collective-permute-done.18.rest_0_, bf16[2,256,128]{2,1,0:T(8,128)(2,1)S(1)} %collective-permute-done.19.rest_1_, ...), custom_call_target="tpu_custom_call" | custom-call | bytes 1048576 | tf_op jit(solution)/shard_map/unpack/pallas_call | solution.py:102
Async XLA Ops:
  2.7 15.0 %collective-permute-start.1 = (bf16[2,256,128]{2,1,0:T(8,128)(2,1)S(1)}, bf16[2,256,128]{2,1,0:T(8,128)(2,1)S(1)}, u32[]{:S(2)}, u32[]{:S(2)}) collective-permute-start(bf16[2,256,128]{2,1,0:T(8,128)(2,1)S(1)} %get-tuple-element.29), channel_id=1, source_target_pairs={{0,0},{1,16},{2,2},{3,18},{4,4},{5,20},{6,6},{7,22},{8,8},{9,24},{... | collective-permute-start | bytes 393224 | tf_op jit(solution)/shard_map/ppermute | solution.py:332
  7.5 11.2 %collective-permute-start.2 = (bf16[2,256,128]{2,1,0:T(8,128)(2,1)S(1)}, bf16[2,256,128]{2,1,0:T(8,128)(2,1)S(1)}, u32[]{:S(2)}, u32[]{:S(2)}) collective-permute-start(bf16[2,256,128]{2,1,0:T(8,128)(2,1)S(1)} %get-tuple-element.30), channel_id=1, source_target_pairs={{0,4},{1,20},{2,6},{3,22},{4,0},{5,16},{6,2},{7,18},{8,12},{9,28},... | collective-permute-start | bytes 393224 | tf_op jit(solution)/shard_map/ppermute | solution.py:332
  9.5 1.9 %collective-permute-start = (s32[384]{0:T(512)S(1)}, s32[384]{0:T(512)S(1)}, u32[]{:S(2)}, u32[]{:S(2)}) collective-permute-start(s32[384]{0:T(512)S(1)} %reshape.17.mine_ref), channel_id=1, source_target_pairs={{0,1},{1,0},{2,3},{3,2},{4,5},{5,4},{6,7},{7,6},{8,9},{9,8},{10,11... | collective-permute-start | bytes 4616 | tf_op jit(solution)/shard_map/ppermute | solution.py:338
  9.5 9.1 %collective-permute-start.3 = (bf16[2,256,128]{2,1,0:T(8,128)(2,1)S(1)}, bf16[2,256,128]{2,1,0:T(8,128)(2,1)S(1)}, u32[]{:S(2)}, u32[]{:S(2)}) collective-permute-start(bf16[2,256,128]{2,1,0:T(8,128)(2,1)S(1)} %get-tuple-element.31), channel_id=1, source_target_pairs={{0,8},{1,24},{2,10},{3,26},{4,12},{5,28},{6,14},{7,30},{8,0},{9,16... | collective-permute-start | bytes 393224 | tf_op jit(solution)/shard_map/ppermute | solution.py:332
  11.2 10.7 %collective-permute-start.4 = (bf16[2,256,128]{2,1,0:T(8,128)(2,1)S(1)}, bf16[2,256,128]{2,1,0:T(8,128)(2,1)S(1)}, u32[]{:S(2)}, u32[]{:S(2)}) collective-permute-start(bf16[2,256,128]{2,1,0:T(8,128)(2,1)S(1)} %get-tuple-element.32), channel_id=1, source_target_pairs={{0,12},{1,28},{2,14},{3,30},{4,8},{5,24},{6,10},{7,26},{8,4},{9,20... | collective-permute-start | bytes 393224 | tf_op jit(solution)/shard_map/ppermute | solution.py:332
  11.4 11.9 %collective-permute-start.9 = (bf16[2,256,128]{2,1,0:T(8,128)(2,1)S(1)}, bf16[2,256,128]{2,1,0:T(8,128)(2,1)S(1)}, u32[]{:S(2)}, u32[]{:S(2)}) collective-permute-start(bf16[2,256,128]{2,1,0:T(8,128)(2,1)S(1)} %get-tuple-element.33), channel_id=1, source_target_pairs={{0,0},{1,16},{2,2},{3,18},{4,4},{5,20},{6,6},{7,22},{8,8},{9,24},{... | collective-permute-start | bytes 393224 | tf_op jit(solution)/shard_map/ppermute | solution.py:332
  17.7 7.0 %collective-permute-start.10 = (bf16[2,256,128]{2,1,0:T(8,128)(2,1)S(1)}, bf16[2,256,128]{2,1,0:T(8,128)(2,1)S(1)}, u32[]{:S(2)}, u32[]{:S(2)}) collective-permute-start(bf16[2,256,128]{2,1,0:T(8,128)(2,1)S(1)} %get-tuple-element.34), channel_id=1, source_target_pairs={{0,4},{1,20},{2,6},{3,22},{4,0},{5,16},{6,2},{7,18},{8,12},{9,28},... | collective-permute-start | bytes 393224 | tf_op jit(solution)/shard_map/ppermute | solution.py:332
  18.7 7.2 %collective-permute-start.5 = (bf16[2,256,128]{2,1,0:T(8,128)(2,1)S(1)}, bf16[2,256,128]{2,1,0:T(8,128)(2,1)S(1)}, u32[]{:S(2)}, u32[]{:S(2)}) collective-permute-start(bf16[2,256,128]{2,1,0:T(8,128)(2,1)S(1)} %collective-permute-done.1.rest_1_), channel_id=1, source_target_pairs={{0,1},{1,0},{2,3},{3,2},{4,5},{5,4},{6,7},{7,6},{8,9},{9,8},{10,11... | collective-permute-start | bytes 393224 | tf_op jit(solution)/shard_map/ppermute | solution.py:338
  18.7 9.5 %collective-permute-start.6 = (bf16[2,256,128]{2,1,0:T(8,128)(2,1)S(1)}, bf16[2,256,128]{2,1,0:T(8,128)(2,1)S(1)}, u32[]{:S(2)}, u32[]{:S(2)}) collective-permute-start(bf16[2,256,128]{2,1,0:T(8,128)(2,1)S(1)} %collective-permute-done.2.rest_2_), channel_id=1, source_target_pairs={{0,1},{1,0},{2,3},{3,2},{4,5},{5,4},{6,7},{7,6},{8,9},{9,8},{10,11... | collective-permute-start | bytes 393224 | tf_op jit(solution)/shard_map/ppermute | solution.py:338
  21.9 6.3 %collective-permute-start.7 = (bf16[2,256,128]{2,1,0:T(8,128)(2,1)S(1)}, bf16[2,256,128]{2,1,0:T(8,128)(2,1)S(1)}, u32[]{:S(2)}, u32[]{:S(2)}) collective-permute-start(bf16[2,256,128]{2,1,0:T(8,128)(2,1)S(1)} %collective-permute-done.3.rest_3_), channel_id=1, source_target_pairs={{0,1},{1,0},{2,3},{3,2},{4,5},{5,4},{6,7},{7,6},{8,9},{9,8},{10,11... | collective-permute-start | bytes 393224 | tf_op jit(solution)/shard_map/ppermute | solution.py:338
  23.3 4.9 %collective-permute-start.8 = (bf16[2,256,128]{2,1,0:T(8,128)(2,1)S(1)}, bf16[2,256,128]{2,1,0:T(8,128)(2,1)S(1)}, u32[]{:S(2)}, u32[]{:S(2)}) collective-permute-start(bf16[2,256,128]{2,1,0:T(8,128)(2,1)S(1)} %collective-permute-done.4.rest_4_), channel_id=1, source_target_pairs={{0,1},{1,0},{2,3},{3,2},{4,5},{5,4},{6,7},{7,6},{8,9},{9,8},{10,11... | collective-permute-start | bytes 393224 | tf_op jit(solution)/shard_map/ppermute | solution.py:338
  24.7 7.4 %collective-permute-start.13 = (bf16[2,256,128]{2,1,0:T(8,128)(2,1)S(1)}, bf16[2,256,128]{2,1,0:T(8,128)(2,1)S(1)}, u32[]{:S(2)}, u32[]{:S(2)}) collective-permute-start(bf16[2,256,128]{2,1,0:T(8,128)(2,1)S(1)} %get-tuple-element.40), channel_id=1, source_target_pairs={{0,8},{1,24},{2,10},{3,26},{4,12},{5,28},{6,14},{7,30},{8,0},{9,16... | collective-permute-start | bytes 393224 | tf_op jit(solution)/shard_map/ppermute | solution.py:332
  25.8 6.2 %collective-permute-start.14 = (bf16[2,256,128]{2,1,0:T(8,128)(2,1)S(1)}, bf16[2,256,128]{2,1,0:T(8,128)(2,1)S(1)}, u32[]{:S(2)}, u32[]{:S(2)}) collective-permute-start(bf16[2,256,128]{2,1,0:T(8,128)(2,1)S(1)} %get-tuple-element.41), channel_id=1, source_target_pairs={{0,12},{1,28},{2,14},{3,30},{4,8},{5,24},{6,10},{7,26},{8,4},{9,20... | collective-permute-start | bytes 393224 | tf_op jit(solution)/shard_map/ppermute | solution.py:332
  28.2 17.1 %copy-start = (s32[128]{0:T(128)S(1)}, s32[128]{0:T(128)}, u32[]{:S(2)}) copy-start(s32[128]{0:T(128)} %param.11) | copy-start | bytes 1540
  35.3 10.0 %collective-permute-start.17 = (f32[2,1152,128]{2,1,0:T(8,128)S(1)}, f32[2,1152,128]{2,1,0:T(8,128)S(1)}, u32[]{:S(2)}, u32[]{:S(2)}) collective-permute-start(f32[2,1152,128]{2,1,0:T(8,128)S(1)} %get-tuple-element.47), channel_id=1, source_target_pairs={{0,1},{1,0},{2,3},{3,2},{4,5},{5,4},{6,7},{7,6},{8,9},{9,8},{10,11... | collective-permute-start | bytes 3538952 | tf_op jit(solution)/shard_map/ppermute | solution.py:338
  35.4 17.1 %collective-permute-start.11 = (bf16[2,256,128]{2,1,0:T(8,128)(2,1)S(1)}, bf16[2,256,128]{2,1,0:T(8,128)(2,1)S(1)}, u32[]{:S(2)}, u32[]{:S(2)}) collective-permute-start(bf16[2,256,128]{2,1,0:T(8,128)(2,1)S(1)} %get-tuple-element.35), channel_id=1, source_target_pairs={{0,0},{1,16},{2,2},{3,18},{4,4},{5,20},{6,6},{7,22},{8,8},{9,24},{... | collective-permute-start | bytes 393224 | tf_op jit(solution)/shard_map/ppermute | solution.py:332
  42.4 11.1 %collective-permute-start.12 = (bf16[2,256,128]{2,1,0:T(8,128)(2,1)S(1)}, bf16[2,256,128]{2,1,0:T(8,128)(2,1)S(1)}, u32[]{:S(2)}, u32[]{:S(2)}) collective-permute-start(bf16[2,256,128]{2,1,0:T(8,128)(2,1)S(1)} %get-tuple-element.36), channel_id=1, source_target_pairs={{0,4},{1,20},{2,6},{3,22},{4,0},{5,16},{6,2},{7,18},{8,12},{9,28},... | collective-permute-start | bytes 393224 | tf_op jit(solution)/shard_map/ppermute | solution.py:332
  43.5 10.7 %collective-permute-start.15 = (bf16[2,256,128]{2,1,0:T(8,128)(2,1)S(1)}, bf16[2,256,128]{2,1,0:T(8,128)(2,1)S(1)}, u32[]{:S(2)}, u32[]{:S(2)}) collective-permute-start(bf16[2,256,128]{2,1,0:T(8,128)(2,1)S(1)} %get-tuple-element.42), channel_id=1, source_target_pairs={{0,8},{1,24},{2,10},{3,26},{4,12},{5,28},{6,14},{7,30},{8,0},{9,16... | collective-permute-start | bytes 393224 | tf_op jit(solution)/shard_map/ppermute | solution.py:332
  44.1 14.8 %collective-permute-start.16 = (bf16[2,256,128]{2,1,0:T(8,128)(2,1)S(1)}, bf16[2,256,128]{2,1,0:T(8,128)(2,1)S(1)}, u32[]{:S(2)}, u32[]{:S(2)}) collective-permute-start(bf16[2,256,128]{2,1,0:T(8,128)(2,1)S(1)} %get-tuple-element.43), channel_id=1, source_target_pairs={{0,12},{1,28},{2,14},{3,30},{4,8},{5,24},{6,10},{7,26},{8,4},{9,20... | collective-permute-start | bytes 393224 | tf_op jit(solution)/shard_map/ppermute | solution.py:332
  46.3 14.1 %collective-permute-start.18 = (bf16[2,256,128]{2,1,0:T(8,128)(2,1)S(1)}, bf16[2,256,128]{2,1,0:T(8,128)(2,1)S(1)}, u32[]{:S(2)}, u32[]{:S(2)}) collective-permute-start(bf16[2,256,128]{2,1,0:T(8,128)(2,1)S(1)} %get-tuple-element.48), channel_id=1, source_target_pairs={{0,0},{1,16},{2,2},{3,18},{4,4},{5,20},{6,6},{7,22},{8,8},{9,24},{... | collective-permute-start | bytes 393224 | tf_op jit(solution)/shard_map/ppermute | solution.py:332
  52.5 10.0 %collective-permute-start.19 = (bf16[2,256,128]{2,1,0:T(8,128)(2,1)S(1)}, bf16[2,256,128]{2,1,0:T(8,128)(2,1)S(1)}, u32[]{:S(2)}, u32[]{:S(2)}) collective-permute-start(bf16[2,256,128]{2,1,0:T(8,128)(2,1)S(1)} %get-tuple-element.49), channel_id=1, source_target_pairs={{0,4},{1,20},{2,6},{3,22},{4,0},{5,16},{6,2},{7,18},{8,12},{9,28},... | collective-permute-start | bytes 393224 | tf_op jit(solution)/shard_map/ppermute | solution.py:332
  53.5 12.0 %collective-permute-start.20 = (bf16[2,256,128]{2,1,0:T(8,128)(2,1)S(1)}, bf16[2,256,128]{2,1,0:T(8,128)(2,1)S(1)}, u32[]{:S(2)}, u32[]{:S(2)}) collective-permute-start(bf16[2,256,128]{2,1,0:T(8,128)(2,1)S(1)} %get-tuple-element.50), channel_id=1, source_target_pairs={{0,8},{1,24},{2,10},{3,26},{4,12},{5,28},{6,14},{7,30},{8,0},{9,16... | collective-permute-start | bytes 393224 | tf_op jit(solution)/shard_map/ppermute | solution.py:332
  54.2 13.1 %collective-permute-start.21 = (bf16[2,256,128]{2,1,0:T(8,128)(2,1)S(1)}, bf16[2,256,128]{2,1,0:T(8,128)(2,1)S(1)}, u32[]{:S(2)}, u32[]{:S(2)}) collective-permute-start(bf16[2,256,128]{2,1,0:T(8,128)(2,1)S(1)} %get-tuple-element.51), channel_id=1, source_target_pairs={{0,12},{1,28},{2,14},{3,30},{4,8},{5,24},{6,10},{7,26},{8,4},{9,20... | collective-permute-start | bytes 393224 | tf_op jit(solution)/shard_map/ppermute | solution.py:332

commit v2 on v1

--- a/solution.py
+++ b/solution.py
@@ -144,10 +144,11 @@
     column = lax.broadcasted_iota(jnp.int32, (1, 4 * BLOCK), 1)
 
     if opens:
-        spots = global_ref[...] ^ (flip * BLOCK)
+        shared = global_ref.shape[1]
+        spots = jnp.broadcast_to(global_ref[...] ^ (flip * BLOCK), (shared, shared)).T[:, :1]
         sums = [None, None]
         for n in range(2 * rounds):
-            ids = lax.broadcasted_iota(jnp.int32, (spots.shape[0], tokens), 1) + n * tokens
+            ids = lax.broadcasted_iota(jnp.int32, (shared, tokens), 1) + n * tokens
             hot = jnp.where(ids == spots, 1.0, 0.0).astype(BF16)
             for m in range(2):
                 part = parts[n][m]
@@ -242,7 +243,7 @@
     acc = jax.ShapeDtypeStruct((2, 2 * half + shared, width), F32)
     out_shape = [one] * count
     if opens:
-        given = [global_pos.reshape(shared, 1), *parts]
+        given = [global_pos.reshape(1, shared), *parts]
         out_shape += [
             jax.ShapeDtypeStruct((2, 2 * half, width), BF16),
             jax.ShapeDtypeStruct((2, shared, width), BF16),

time: 69.1 us -> 68.9 us (level)
    reshape x1 -> x0, local copies, waits for them, and re-layouts: 0.76 us -> none  [attend(): given = [global_pos.reshape(shared, 1), *parts]]
  transfers between devices with their start and end apart: 22 -> 22, of which waited for: 7 -> 7; matrix products, arithmetic and copies ran while one was open for 3% -> 1% of each run, Pallas kernels for 9% -> 9%
where the time goes in v2:
time: 68.9 us; the launch traced here: 68.6 us
  starting transfers between devices  37.2 us (54%)
  waiting for transfers between devices  16.1 us (23%)
  Pallas kernels  12.8 us (19%)
  local copies, waits for them, and re-layouts  1.65 us (2%)
  between operations  0.79 us (1%)
    ppermute x16, starting transfers between devices, send(): out.append(lax.ppermute(part, AXES, trades[first + n]))  36.5 us
    ppermute x16, waiting for transfers between devices, send(): out.append(lax.ppermute(part, AXES, trades[first + n]))  16.1 us
    pallas_call x2, Pallas kernels, attend(): pl.pallas_call(functools.partial(attend_kernel, rounds, run_blocks, picks...  7.1 us
    pallas_call x2, Pallas kernels, unpack(): pl.pallas_call(functools.partial(unpack_kernel, rounds, width), out_shape...  2.79 us
    pallas_call x1, Pallas kernels, pack(): pl.pallas_call(functools.partial(pack_kernel, rounds, width), out_shape=[...  1.95 us
    unnamed x3, local copies, waits for them, and re-layouts  1.44 us
  transfers between devices with their start and end apart: 22, of which 7 were waited for; matrix products, arithmetic and copies ran while one was open for 1% of the time, Pallas kernels for 9%

profile of v2, /device:TPU:9, one launch (start us, length us, event | category | flops | bytes accessed | tf_op | source)
XLA Modules:
  0.0 68.6 jit_solution(7631943740822900222)
XLA Ops:
  0.6 0.1 pad_add_fusion.where_ref
  0.7 2.0 %pack.1 = (bf16[2,256,128]{2,1,0:T(8,128)(2,1)S(1)}, bf16[2,256,128]{2,1,0:T(8,128)(2,1)S(1)}, bf16[2,256,128]{2,1,0:T(8,128)(2,1)S(1)}, bf16[2,256,128]{2,1,0:T...) custom-call(s32[2]{0:T(128)S(1)} %pad_add_fusion.where_ref, ...), custom_call_target="tpu_custom_call" | custom-call | bytes 2097152 | tf_op jit(solution)/shard_map/pack/pallas_call | solution.py:67
  2.7 4.8 %collective-permute-start.1 = (bf16[2,256,128]{2,1,0:T(8,128)(2,1)S(1)}, bf16[2,256,128]{2,1,0:T(8,128)(2,1)S(1)}, u32[]{:S(2)}, u32[]{:S(2)}) collective-permute-start(bf16[2,256,128]{2,1,0:T(8,128)(2,1)S(1)} %get-tuple-element.29), channel_id=1, source_target_pairs={{0,0},{1,16},{2,2},{3,18},{4,4},{5,20},{6,6},{7,22},{8,8},{9,24},{... | collective-permute-start | bytes 393224 | tf_op jit(solution)/shard_map/ppermute | solution.py:333
  7.5 1.0 %collective-permute-start.2 = (bf16[2,256,128]{2,1,0:T(8,128)(2,1)S(1)}, bf16[2,256,128]{2,1,0:T(8,128)(2,1)S(1)}, u32[]{:S(2)}, u32[]{:S(2)}) collective-permute-start(bf16[2,256,128]{2,1,0:T(8,128)(2,1)S(1)} %get-tuple-element.30), channel_id=1, source_target_pairs={{0,4},{1,20},{2,6},{3,22},{4,0},{5,16},{6,2},{7,18},{8,12},{9,28},... | collective-permute-start | bytes 393224 | tf_op jit(solution)/shard_map/ppermute | solution.py:333
  8.5 0.8 %copy.11 = s32[1,4,32,3]{3,2,1,0:T(8,128)S(1)} copy(s32[1,4,32,3]{2,1,3,0:T(4,128)} %param.10) | data formatting | bytes 3072 | tf_op args[4]
  9.3 0.2 reshape.15.mine_ref
  9.5 0.1 collective-permute-start
  9.5 1.7 %collective-permute-start.3 = (bf16[2,256,128]{2,1,0:T(8,128)(2,1)S(1)}, bf16[2,256,128]{2,1,0:T(8,128)(2,1)S(1)}, u32[]{:S(2)}, u32[]{:S(2)}) collective-permute-start(bf16[2,256,128]{2,1,0:T(8,128)(2,1)S(1)} %get-tuple-element.31), channel_id=1, source_target_pairs={{0,8},{1,24},{2,10},{3,26},{4,12},{5,28},{6,14},{7,30},{8,0},{9,16... | collective-permute-start | bytes 393224 | tf_op jit(solution)/shard_map/ppermute | solution.py:333
  11.2 0.1 collective-permute-start.4
  11.4 0.0 collective-permute-done.other_table_ref
  11.4 6.3 %collective-permute-start.9 = (bf16[2,256,128]{2,1,0:T(8,128)(2,1)S(1)}, bf16[2,256,128]{2,1,0:T(8,128)(2,1)S(1)}, u32[]{:S(2)}, u32[]{:S(2)}) collective-permute-start(bf16[2,256,128]{2,1,0:T(8,128)(2,1)S(1)} %get-tuple-element.33), channel_id=1, source_target_pairs={{0,0},{1,16},{2,2},{3,18},{4,4},{5,20},{6,6},{7,22},{8,8},{9,24},{... | collective-permute-start | bytes 393224 | tf_op jit(solution)/shard_map/ppermute | solution.py:333
  17.7 0.0 collective-permute-done.1.rest_1_
  17.7 1.0 %collective-permute-start.10 = (bf16[2,256,128]{2,1,0:T(8,128)(2,1)S(1)}, bf16[2,256,128]{2,1,0:T(8,128)(2,1)S(1)}, u32[]{:S(2)}, u32[]{:S(2)}) collective-permute-start(bf16[2,256,128]{2,1,0:T(8,128)(2,1)S(1)} %get-tuple-element.34), channel_id=1, source_target_pairs={{0,4},{1,20},{2,6},{3,22},{4,0},{5,16},{6,2},{7,18},{8,12},{9,28},... | collective-permute-start | bytes 393224 | tf_op jit(solution)/shard_map/ppermute | solution.py:333
  18.7 0.0 collective-permute-done.2.rest_2_
  18.7 0.0 collective-permute-start.5
  18.7 0.0 collective-permute-done.3.rest_3_
  18.7 0.5 collective-permute-start.6
  19.2 2.7 %collective-permute-done.4.rest_4_ = bf16[2,256,128]{2,1,0:T(8,128)(2,1)S(1)} collective-permute-done((bf16[2,256,128]{2,1,0:T(8,128)(2,1)S(1)}, bf16[2,256,128]{2,1,0:T(8,128)(2,1)S(1)}, u32[]{:S(2)}, u32[]{:S(2)}) %collective-permute-start.4) | collective-permute-done | bytes 131104 | tf_op jit(solution)/shard_map/ppermute | solution.py:333
  21.9 0.0 collective-permute-start.7
  21.9 1.4 %collective-permute-done.9.rest_9_ = bf16[2,256,128]{2,1,0:T(8,128)(2,1)S(1)} collective-permute-done((bf16[2,256,128]{2,1,0:T(8,128)(2,1)S(1)}, bf16[2,256,128]{2,1,0:T(8,128)(2,1)S(1)}, u32[]{:S(2)}, u32[]{:S(2)}) %collective-permute-start.9) | collective-permute-done | bytes 131104 | tf_op jit(solution)/shard_map/ppermute | solution.py:333
  23.3 0.0 collective-permute-start.8
  23.3 1.4 %collective-permute-done.10.rest_10_ = bf16[2,256,128]{2,1,0:T(8,128)(2,1)S(1)} collective-permute-done((bf16[2,256,128]{2,1,0:T(8,128)(2,1)S(1)}, bf16[2,256,128]{2,1,0:T(8,128)(2,1)S(1)}, u32[]{:S(2)}, u32[]{:S(2)}) %collective-permute-start.10) | collective-permute-done | bytes 131104 | tf_op jit(solution)/shard_map/ppermute | solution.py:333
  24.7 1.1 %collective-permute-start.13 = (bf16[2,256,128]{2,1,0:T(8,128)(2,1)S(1)}, bf16[2,256,128]{2,1,0:T(8,128)(2,1)S(1)}, u32[]{:S(2)}, u32[]{:S(2)}) collective-permute-start(bf16[2,256,128]{2,1,0:T(8,128)(2,1)S(1)} %get-tuple-element.40), channel_id=1, source_target_pairs={{0,8},{1,24},{2,10},{3,26},{4,12},{5,28},{6,14},{7,30},{8,0},{9,16... | collective-permute-start | bytes 393224 | tf_op jit(solution)/shard_map/ppermute | solution.py:333
  25.8 0.0 collective-permute-done.5.rest_5_
  25.8 1.6 %collective-permute-start.14 = (bf16[2,256,128]{2,1,0:T(8,128)(2,1)S(1)}, bf16[2,256,128]{2,1,0:T(8,128)(2,1)S(1)}, u32[]{:S(2)}, u32[]{:S(2)}) collective-permute-start(bf16[2,256,128]{2,1,0:T(8,128)(2,1)S(1)} %get-tuple-element.41), channel_id=1, source_target_pairs={{0,12},{1,28},{2,14},{3,30},{4,8},{5,24},{6,10},{7,26},{8,4},{9,20... | collective-permute-start | bytes 393224 | tf_op jit(solution)/shard_map/ppermute | solution.py:333
  27.4 0.0 collective-permute-done.6.rest_6_
  27.4 0.0 collective-permute-done.7.rest_7_
  27.4 0.0 collective-permute-done.8.rest_8_
  27.4 0.0 copy-start
  27.4 0.6 copy-done
  28.1 3.9 %attend.2 = (bf16[2,256,128]{2,1,0:T(8,128)(2,1)S(1)}, bf16[2,256,128]{2,1,0:T(8,128)(2,1)S(1)}, bf16[2,2048,128]{2,1,0:T(8,128)(2,1)S(1)}, bf16[2,128,128]{2,1,0:T(8,128)(2,1)S(1)}, f32[2,2176,128]{2,1,0:T(8,128)S(1)}) custom-call(s32[2]{0:T(128)S(1)} %pad_add_fusion.where_ref, s32[384]{0:T(512)S(1)} %reshape.15.mine_ref, ...), custom_call_target="tpu_custom_call" | custom-call | flops 402653184 | bytes 1572864 | tf_op jit(solution)/shard_map/attend/pallas_call | solution.py:258
  32.0 0.0 collective-permute-done.13.rest_3_
  32.0 0.0 collective-permute-done.14.rest_4_
  32.0 3.2 %attend.3 = (bf16[2,256,128]{2,1,0:T(8,128)(2,1)S(1)}, bf16[2,256,128]{2,1,0:T(8,128)(2,1)S(1)}, f32[2,2176,128]{2,1,0:T(8,128)S(1)}, f32[2,1152,128]{2,1,0:T(8,128)S(1)}) custom-call(s32[2]{0:T(128)S(1)} %pad_add_fusion.where_ref, s32[384]{0:T(512)S(1)} %reshape.15.mine_ref, ...), custom_call_target="tpu_custom_call", output_to_operand_aliasing={{2}: (5, {})} | custom-call | flops 402653184 | bytes 1572864 | tf_op jit(solution)/shard_map/attend/pallas_call | solution.py:258
  35.2 0.1 collective-permute-start.17
  35.3 7.0 %collective-permute-start.11 = (bf16[2,256,128]{2,1,0:T(8,128)(2,1)S(1)}, bf16[2,256,128]{2,1,0:T(8,128)(2,1)S(1)}, u32[]{:S(2)}, u32[]{:S(2)}) collective-permute-start(bf16[2,256,128]{2,1,0:T(8,128)(2,1)S(1)} %get-tuple-element.35), channel_id=1, source_target_pairs={{0,0},{1,16},{2,2},{3,18},{4,4},{5,20},{6,6},{7,22},{8,8},{9,24},{... | collective-permute-start | bytes 393224 | tf_op jit(solution)/shard_map/ppermute | solution.py:333
  42.3 1.0 %collective-permute-start.12 = (bf16[2,256,128]{2,1,0:T(8,128)(2,1)S(1)}, bf16[2,256,128]{2,1,0:T(8,128)(2,1)S(1)}, u32[]{:S(2)}, u32[]{:S(2)}) collective-permute-start(bf16[2,256,128]{2,1,0:T(8,128)(2,1)S(1)} %get-tuple-element.36), channel_id=1, source_target_pairs={{0,4},{1,20},{2,6},{3,22},{4,0},{5,16},{6,2},{7,18},{8,12},{9,28},... | collective-permute-start | bytes 393224 | tf_op jit(solution)/shard_map/ppermute | solution.py:333
  43.4 0.8 %collective-permute-start.15 = (bf16[2,256,128]{2,1,0:T(8,128)(2,1)S(1)}, bf16[2,256,128]{2,1,0:T(8,128)(2,1)S(1)}, u32[]{:S(2)}, u32[]{:S(2)}) collective-permute-start(bf16[2,256,128]{2,1,0:T(8,128)(2,1)S(1)} %get-tuple-element.42), channel_id=1, source_target_pairs={{0,8},{1,24},{2,10},{3,26},{4,12},{5,28},{6,14},{7,30},{8,0},{9,16... | collective-permute-start | bytes 393224 | tf_op jit(solution)/shard_map/ppermute | solution.py:333
  44.1 1.1 %collective-permute-start.16 = (bf16[2,256,128]{2,1,0:T(8,128)(2,1)S(1)}, bf16[2,256,128]{2,1,0:T(8,128)(2,1)S(1)}, u32[]{:S(2)}, u32[]{:S(2)}) collective-permute-start(bf16[2,256,128]{2,1,0:T(8,128)(2,1)S(1)} %get-tuple-element.43), channel_id=1, source_target_pairs={{0,12},{1,28},{2,14},{3,30},{4,8},{5,24},{6,10},{7,26},{8,4},{9,20... | collective-permute-start | bytes 393224 | tf_op jit(solution)/shard_map/ppermute | solution.py:333
  45.2 0.0 collective-permute-done.17.came_ref
  45.2 1.0 %total.1 = (bf16[2,256,128]{2,1,0:T(8,128)(2,1)S(1)}, bf16[2,256,128]{2,1,0:T(8,128)(2,1)S(1)}, bf16[2,256,128]{2,1,0:T(8,128)(2,1)S(1)}, bf16[2,256,128]{2,1,0:T(8,128)(2,1)S(1)}) custom-call(s32[2]{0:T(128)S(1)} %pad_add_fusion.where_ref, s32[1,128]{1,0:T(1,128)S(1)} %bitcast.6, f32[2,2176,128]{2,1,0:T(8,128)S(1)} %get-tuple-element.46.acc_ref, ...), custom_call_target="tpu_custom_call" | custom-call | flops 589824 | bytes 2949120 | tf_op jit(solution)/shard_map/total/pallas_call | solution.py:309
  46.2 6.2 %collective-permute-start.18 = (bf16[2,256,128]{2,1,0:T(8,128)(2,1)S(1)}, bf16[2,256,128]{2,1,0:T(8,128)(2,1)S(1)}, u32[]{:S(2)}, u32[]{:S(2)}) collective-permute-start(bf16[2,256,128]{2,1,0:T(8,128)(2,1)S(1)} %get-tuple-element.48), channel_id=1, source_target_pairs={{0,0},{1,16},{2,2},{3,18},{4,4},{5,20},{6,6},{7,22},{8,8},{9,24},{... | collective-permute-start | bytes 393224 | tf_op jit(solution)/shard_map/ppermute | solution.py:333
  52.4 0.0 collective-permute-done.11.rest_0_
  52.4 1.0 %collective-permute-start.19 = (bf16[2,256,128]{2,1,0:T(8,128)(2,1)S(1)}, bf16[2,256,128]{2,1,0:T(8,128)(2,1)S(1)}, u32[]{:S(2)}, u32[]{:S(2)}) collective-permute-start(bf16[2,256,128]{2,1,0:T(8,128)(2,1)S(1)} %get-tuple-element.49), channel_id=1, source_target_pairs={{0,4},{1,20},{2,6},{3,22},{4,0},{5,16},{6,2},{7,18},{8,12},{9,28},... | collective-permute-start | bytes 393224 | tf_op jit(solution)/shard_map/ppermute | solution.py:333
  53.4 0.0 collective-permute-done.12.rest_1_
  53.4 0.8 %collective-permute-start.20 = (bf16[2,256,128]{2,1,0:T(8,128)(2,1)S(1)}, bf16[2,256,128]{2,1,0:T(8,128)(2,1)S(1)}, u32[]{:S(2)}, u32[]{:S(2)}) collective-permute-start(bf16[2,256,128]{2,1,0:T(8,128)(2,1)S(1)} %get-tuple-element.50), channel_id=1, source_target_pairs={{0,8},{1,24},{2,10},{3,26},{4,12},{5,28},{6,14},{7,30},{8,0},{9,16... | collective-permute-start | bytes 393224 | tf_op jit(solution)/shard_map/ppermute | solution.py:333
  54.2 0.0 collective-permute-done.15.rest_2_
  54.2 1.1 %collective-permute-start.21 = (bf16[2,256,128]{2,1,0:T(8,128)(2,1)S(1)}, bf16[2,256,128]{2,1,0:T(8,128)(2,1)S(1)}, u32[]{:S(2)}, u32[]{:S(2)}) collective-permute-start(bf16[2,256,128]{2,1,0:T(8,128)(2,1)S(1)} %get-tuple-element.51), channel_id=1, source_target_pairs={{0,12},{1,28},{2,14},{3,30},{4,8},{5,24},{6,10},{7,26},{8,4},{9,20... | collective-permute-start | bytes 393224 | tf_op jit(solution)/shard_map/ppermute | solution.py:333
  55.2 3.6 %collective-permute-done.16.rest_3_ = bf16[2,256,128]{2,1,0:T(8,128)(2,1)S(1)} collective-permute-done((bf16[2,256,128]{2,1,0:T(8,128)(2,1)S(1)}, bf16[2,256,128]{2,1,0:T(8,128)(2,1)S(1)}, u32[]{:S(2)}, u32[]{:S(2)}) %collective-permute-start.16) | collective-permute-done | bytes 131104 | tf_op jit(solution)/shard_map/ppermute | solution.py:333
  58.8 1.4 %unpack.2 = (bf16[1,256,512]{2,1,0:T(8,128)(2,1)}, bf16[1,256,512]{2,1,0:T(8,128)(2,1)}) custom-call(s32[2]{0:T(128)S(1)} %pad_add_fusion.where_ref, bf16[2,256,128]{2,1,0:T(8,128)(2,1)S(1)} %collective-permute-done.11.rest_0_, bf16[2,256,128]{2,1,0:T(8,128)(2,1)S(1)} %collective-permute-done.12.rest_1_, ...), custom_call_target="tpu_custom_call" | custom-call | bytes 1048576 | tf_op jit(solution)/shard_map/unpack/pallas_call | solution.py:102
  60.2 0.0 collective-permute-done.18.rest_0_
  60.2 2.2 %collective-permute-done.19.rest_1_ = bf16[2,256,128]{2,1,0:T(8,128)(2,1)S(1)} collective-permute-done((bf16[2,256,128]{2,1,0:T(8,128)(2,1)S(1)}, bf16[2,256,128]{2,1,0:T(8,128)(2,1)S(1)}, u32[]{:S(2)}, u32[]{:S(2)}) %collective-permute-start.19) | collective-permute-done | bytes 131104 | tf_op jit(solution)/shard_map/ppermute | solution.py:333
  62.4 3.0 %collective-permute-done.20.rest_2_ = bf16[2,256,128]{2,1,0:T(8,128)(2,1)S(1)} collective-permute-done((bf16[2,256,128]{2,1,0:T(8,128)(2,1)S(1)}, bf16[2,256,128]{2,1,0:T(8,128)(2,1)S(1)}, u32[]{:S(2)}, u32[]{:S(2)}) %collective-permute-start.20) | collective-permute-done | bytes 131104 | tf_op jit(solution)/shard_map/ppermute | solution.py:333
  65.4 1.8 %collective-permute-done.21.rest_3_ = bf16[2,256,128]{2,1,0:T(8,128)(2,1)S(1)} collective-permute-done((bf16[2,256,128]{2,1,0:T(8,128)(2,1)S(1)}, bf16[2,256,128]{2,1,0:T(8,128)(2,1)S(1)}, u32[]{:S(2)}, u32[]{:S(2)}) %collective-permute-start.21) | collective-permute-done | bytes 131104 | tf_op jit(solution)/shard_map/ppermute | solution.py:333
  67.2 1.4 %unpack.3 = (bf16[1,256,512]{2,1,0:T(8,128)(2,1)}, bf16[1,256,512]{2,1,0:T(8,128)(2,1)}) custom-call(s32[2]{0:T(128)S(1)} %pad_add_fusion.where_ref, bf16[2,256,128]{2,1,0:T(8,128)(2,1)S(1)} %collective-permute-done.18.rest_0_, bf16[2,256,128]{2,1,0:T(8,128)(2,1)S(1)} %collective-permute-done.19.rest_1_, ...), custom_call_target="tpu_custom_call" | custom-call | bytes 1048576 | tf_op jit(solution)/shard_map/unpack/pallas_call | solution.py:102
Async XLA Ops:
  2.7 15.0 %collective-permute-start.1 = (bf16[2,256,128]{2,1,0:T(8,128)(2,1)S(1)}, bf16[2,256,128]{2,1,0:T(8,128)(2,1)S(1)}, u32[]{:S(2)}, u32[]{:S(2)}) collective-permute-start(bf16[2,256,128]{2,1,0:T(8,128)(2,1)S(1)} %get-tuple-element.29), channel_id=1, source_target_pairs={{0,0},{1,16},{2,2},{3,18},{4,4},{5,20},{6,6},{7,22},{8,8},{9,24},{... | collective-permute-start | bytes 393224 | tf_op jit(solution)/shard_map/ppermute | solution.py:333
  7.5 11.2 %collective-permute-start.2 = (bf16[2,256,128]{2,1,0:T(8,128)(2,1)S(1)}, bf16[2,256,128]{2,1,0:T(8,128)(2,1)S(1)}, u32[]{:S(2)}, u32[]{:S(2)}) collective-permute-start(bf16[2,256,128]{2,1,0:T(8,128)(2,1)S(1)} %get-tuple-element.30), channel_id=1, source_target_pairs={{0,4},{1,20},{2,6},{3,22},{4,0},{5,16},{6,2},{7,18},{8,12},{9,28},... | collective-permute-start | bytes 393224 | tf_op jit(solution)/shard_map/ppermute | solution.py:333
  9.5 1.9 %collective-permute-start = (s32[384]{0:T(512)S(1)}, s32[384]{0:T(512)S(1)}, u32[]{:S(2)}, u32[]{:S(2)}) collective-permute-start(s32[384]{0:T(512)S(1)} %reshape.15.mine_ref), channel_id=1, source_target_pairs={{0,1},{1,0},{2,3},{3,2},{4,5},{5,4},{6,7},{7,6},{8,9},{9,8},{10,11... | collective-permute-start | bytes 4616 | tf_op jit(solution)/shard_map/ppermute | solution.py:339
  9.5 9.1 %collective-permute-start.3 = (bf16[2,256,128]{2,1,0:T(8,128)(2,1)S(1)}, bf16[2,256,128]{2,1,0:T(8,128)(2,1)S(1)}, u32[]{:S(2)}, u32[]{:S(2)}) collective-permute-start(bf16[2,256,128]{2,1,0:T(8,128)(2,1)S(1)} %get-tuple-element.31), channel_id=1, source_target_pairs={{0,8},{1,24},{2,10},{3,26},{4,12},{5,28},{6,14},{7,30},{8,0},{9,16... | collective-permute-start | bytes 393224 | tf_op jit(solution)/shard_map/ppermute | solution.py:333
  11.2 10.7 %collective-permute-start.4 = (bf16[2,256,128]{2,1,0:T(8,128)(2,1)S(1)}, bf16[2,256,128]{2,1,0:T(8,128)(2,1)S(1)}, u32[]{:S(2)}, u32[]{:S(2)}) collective-permute-start(bf16[2,256,128]{2,1,0:T(8,128)(2,1)S(1)} %get-tuple-element.32), channel_id=1, source_target_pairs={{0,12},{1,28},{2,14},{3,30},{4,8},{5,24},{6,10},{7,26},{8,4},{9,20... | collective-permute-start | bytes 393224 | tf_op jit(solution)/shard_map/ppermute | solution.py:333
  11.4 11.9 %collective-permute-start.9 = (bf16[2,256,128]{2,1,0:T(8,128)(2,1)S(1)}, bf16[2,256,128]{2,1,0:T(8,128)(2,1)S(1)}, u32[]{:S(2)}, u32[]{:S(2)}) collective-permute-start(bf16[2,256,128]{2,1,0:T(8,128)(2,1)S(1)} %get-tuple-element.33), channel_id=1, source_target_pairs={{0,0},{1,16},{2,2},{3,18},{4,4},{5,20},{6,6},{7,22},{8,8},{9,24},{... | collective-permute-start | bytes 393224 | tf_op jit(solution)/shard_map/ppermute | solution.py:333
  17.7 7.0 %collective-permute-start.10 = (bf16[2,256,128]{2,1,0:T(8,128)(2,1)S(1)}, bf16[2,256,128]{2,1,0:T(8,128)(2,1)S(1)}, u32[]{:S(2)}, u32[]{:S(2)}) collective-permute-start(bf16[2,256,128]{2,1,0:T(8,128)(2,1)S(1)} %get-tuple-element.34), channel_id=1, source_target_pairs={{0,4},{1,20},{2,6},{3,22},{4,0},{5,16},{6,2},{7,18},{8,12},{9,28},... | collective-permute-start | bytes 393224 | tf_op jit(solution)/shard_map/ppermute | solution.py:333
  18.7 7.2 %collective-permute-start.5 = (bf16[2,256,128]{2,1,0:T(8,128)(2,1)S(1)}, bf16[2,256,128]{2,1,0:T(8,128)(2,1)S(1)}, u32[]{:S(2)}, u32[]{:S(2)}) collective-permute-start(bf16[2,256,128]{2,1,0:T(8,128)(2,1)S(1)} %collective-permute-done.1.rest_1_), channel_id=1, source_target_pairs={{0,1},{1,0},{2,3},{3,2},{4,5},{5,4},{6,7},{7,6},{8,9},{9,8},{10,11... | collective-permute-start | bytes 393224 | tf_op jit(solution)/shard_map/ppermute | solution.py:339
  18.7 8.7 %collective-permute-start.6 = (bf16[2,256,128]{2,1,0:T(8,128)(2,1)S(1)}, bf16[2,256,128]{2,1,0:T(8,128)(2,1)S(1)}, u32[]{:S(2)}, u32[]{:S(2)}) collective-permute-start(bf16[2,256,128]{2,1,0:T(8,128)(2,1)S(1)} %collective-permute-done.2.rest_2_), channel_id=1, source_target_pairs={{0,1},{1,0},{2,3},{3,2},{4,5},{5,4},{6,7},{7,6},{8,9},{9,8},{10,11... | collective-permute-start | bytes 393224 | tf_op jit(solution)/shard_map/ppermute | solution.py:339
  21.9 5.5 %collective-permute-start.7 = (bf16[2,256,128]{2,1,0:T(8,128)(2,1)S(1)}, bf16[2,256,128]{2,1,0:T(8,128)(2,1)S(1)}, u32[]{:S(2)}, u32[]{:S(2)}) collective-permute-start(bf16[2,256,128]{2,1,0:T(8,128)(2,1)S(1)} %collective-permute-done.3.rest_3_), channel_id=1, source_target_pairs={{0,1},{1,0},{2,3},{3,2},{4,5},{5,4},{6,7},{7,6},{8,9},{9,8},{10,11... | collective-permute-start | bytes 393224 | tf_op jit(solution)/shard_map/ppermute | solution.py:339
  23.3 4.1 %collective-permute-start.8 = (bf16[2,256,128]{2,1,0:T(8,128)(2,1)S(1)}, bf16[2,256,128]{2,1,0:T(8,128)(2,1)S(1)}, u32[]{:S(2)}, u32[]{:S(2)}) collective-permute-start(bf16[2,256,128]{2,1,0:T(8,128)(2,1)S(1)} %collective-permute-done.4.rest_4_), channel_id=1, source_target_pairs={{0,1},{1,0},{2,3},{3,2},{4,5},{5,4},{6,7},{7,6},{8,9},{9,8},{10,11... | collective-permute-start | bytes 393224 | tf_op jit(solution)/shard_map/ppermute | solution.py:339
  24.7 7.3 %collective-permute-start.13 = (bf16[2,256,128]{2,1,0:T(8,128)(2,1)S(1)}, bf16[2,256,128]{2,1,0:T(8,128)(2,1)S(1)}, u32[]{:S(2)}, u32[]{:S(2)}) collective-permute-start(bf16[2,256,128]{2,1,0:T(8,128)(2,1)S(1)} %get-tuple-element.40), channel_id=1, source_target_pairs={{0,8},{1,24},{2,10},{3,26},{4,12},{5,28},{6,14},{7,30},{8,0},{9,16... | collective-permute-start | bytes 393224 | tf_op jit(solution)/shard_map/ppermute | solution.py:333
  25.8 6.2 %collective-permute-start.14 = (bf16[2,256,128]{2,1,0:T(8,128)(2,1)S(1)}, bf16[2,256,128]{2,1,0:T(8,128)(2,1)S(1)}, u32[]{:S(2)}, u32[]{:S(2)}) collective-permute-start(bf16[2,256,128]{2,1,0:T(8,128)(2,1)S(1)} %get-tuple-element.41), channel_id=1, source_target_pairs={{0,12},{1,28},{2,14},{3,30},{4,8},{5,24},{6,10},{7,26},{8,4},{9,20... | collective-permute-start | bytes 393224 | tf_op jit(solution)/shard_map/ppermute | solution.py:333
  27.4 0.7 copy-start
  35.2 10.0 %collective-permute-start.17 = (f32[2,1152,128]{2,1,0:T(8,128)S(1)}, f32[2,1152,128]{2,1,0:T(8,128)S(1)}, u32[]{:S(2)}, u32[]{:S(2)}) collective-permute-start(f32[2,1152,128]{2,1,0:T(8,128)S(1)} %get-tuple-element.47), channel_id=1, source_target_pairs={{0,1},{1,0},{2,3},{3,2},{4,5},{5,4},{6,7},{7,6},{8,9},{9,8},{10,11... | collective-permute-start | bytes 3538952 | tf_op jit(solution)/shard_map/ppermute | solution.py:339
  35.3 17.1 %collective-permute-start.11 = (bf16[2,256,128]{2,1,0:T(8,128)(2,1)S(1)}, bf16[2,256,128]{2,1,0:T(8,128)(2,1)S(1)}, u32[]{:S(2)}, u32[]{:S(2)}) collective-permute-start(bf16[2,256,128]{2,1,0:T(8,128)(2,1)S(1)} %get-tuple-element.35), channel_id=1, source_target_pairs={{0,0},{1,16},{2,2},{3,18},{4,4},{5,20},{6,6},{7,22},{8,8},{9,24},{... | collective-permute-start | bytes 393224 | tf_op jit(solution)/shard_map/ppermute | solution.py:333
  42.3 11.1 %collective-permute-start.12 = (bf16[2,256,128]{2,1,0:T(8,128)(2,1)S(1)}, bf16[2,256,128]{2,1,0:T(8,128)(2,1)S(1)}, u32[]{:S(2)}, u32[]{:S(2)}) collective-permute-start(bf16[2,256,128]{2,1,0:T(8,128)(2,1)S(1)} %get-tuple-element.36), channel_id=1, source_target_pairs={{0,4},{1,20},{2,6},{3,22},{4,0},{5,16},{6,2},{7,18},{8,12},{9,28},... | collective-permute-start | bytes 393224 | tf_op jit(solution)/shard_map/ppermute | solution.py:333
  43.4 10.8 %collective-permute-start.15 = (bf16[2,256,128]{2,1,0:T(8,128)(2,1)S(1)}, bf16[2,256,128]{2,1,0:T(8,128)(2,1)S(1)}, u32[]{:S(2)}, u32[]{:S(2)}) collective-permute-start(bf16[2,256,128]{2,1,0:T(8,128)(2,1)S(1)} %get-tuple-element.42), channel_id=1, source_target_pairs={{0,8},{1,24},{2,10},{3,26},{4,12},{5,28},{6,14},{7,30},{8,0},{9,16... | collective-permute-start | bytes 393224 | tf_op jit(solution)/shard_map/ppermute | solution.py:333
  44.1 14.7 %collective-permute-start.16 = (bf16[2,256,128]{2,1,0:T(8,128)(2,1)S(1)}, bf16[2,256,128]{2,1,0:T(8,128)(2,1)S(1)}, u32[]{:S(2)}, u32[]{:S(2)}) collective-permute-start(bf16[2,256,128]{2,1,0:T(8,128)(2,1)S(1)} %get-tuple-element.43), channel_id=1, source_target_pairs={{0,12},{1,28},{2,14},{3,30},{4,8},{5,24},{6,10},{7,26},{8,4},{9,20... | collective-permute-start | bytes 393224 | tf_op jit(solution)/shard_map/ppermute | solution.py:333
  46.2 14.1 %collective-permute-start.18 = (bf16[2,256,128]{2,1,0:T(8,128)(2,1)S(1)}, bf16[2,256,128]{2,1,0:T(8,128)(2,1)S(1)}, u32[]{:S(2)}, u32[]{:S(2)}) collective-permute-start(bf16[2,256,128]{2,1,0:T(8,128)(2,1)S(1)} %get-tuple-element.48), channel_id=1, source_target_pairs={{0,0},{1,16},{2,2},{3,18},{4,4},{5,20},{6,6},{7,22},{8,8},{9,24},{... | collective-permute-start | bytes 393224 | tf_op jit(solution)/shard_map/ppermute | solution.py:333
  52.4 10.0 %collective-permute-start.19 = (bf16[2,256,128]{2,1,0:T(8,128)(2,1)S(1)}, bf16[2,256,128]{2,1,0:T(8,128)(2,1)S(1)}, u32[]{:S(2)}, u32[]{:S(2)}) collective-permute-start(bf16[2,256,128]{2,1,0:T(8,128)(2,1)S(1)} %get-tuple-element.49), channel_id=1, source_target_pairs={{0,4},{1,20},{2,6},{3,22},{4,0},{5,16},{6,2},{7,18},{8,12},{9,28},... | collective-permute-start | bytes 393224 | tf_op jit(solution)/shard_map/ppermute | solution.py:333
  53.4 12.0 %collective-permute-start.20 = (bf16[2,256,128]{2,1,0:T(8,128)(2,1)S(1)}, bf16[2,256,128]{2,1,0:T(8,128)(2,1)S(1)}, u32[]{:S(2)}, u32[]{:S(2)}) collective-permute-start(bf16[2,256,128]{2,1,0:T(8,128)(2,1)S(1)} %get-tuple-element.50), channel_id=1, source_target_pairs={{0,8},{1,24},{2,10},{3,26},{4,12},{5,28},{6,14},{7,30},{8,0},{9,16... | collective-permute-start | bytes 393224 | tf_op jit(solution)/shard_map/ppermute | solution.py:333
  54.2 13.1 %collective-permute-start.21 = (bf16[2,256,128]{2,1,0:T(8,128)(2,1)S(1)}, bf16[2,256,128]{2,1,0:T(8,128)(2,1)S(1)}, u32[]{:S(2)}, u32[]{:S(2)}) collective-permute-start(bf16[2,256,128]{2,1,0:T(8,128)(2,1)S(1)} %get-tuple-element.51), channel_id=1, source_target_pairs={{0,12},{1,28},{2,14},{3,30},{4,8},{5,24},{6,10},{7,26},{8,4},{9,20... | collective-permute-start | bytes 393224 | tf_op jit(solution)/shard_map/ppermute | solution.py:333

commit v3 on v2

--- a/solution.py
+++ b/solution.py
@@ -10,8 +10,7 @@
 
 BLOCK = 64
 AXES = ("seq", "head")
-GROUPS = 2
-CHUNK = 2
+CHUNK = 4
 GRANT = 24 * 1024 * 1024
 VMEM = pl.BlockSpec(memory_space=pltpu.VMEM)
 SMEM = pl.BlockSpec(memory_space=pltpu.SMEM)
@@ -24,6 +23,15 @@
 
 def dot(a, b, dims):
     return lax.dot_general(a, b, (dims, ((), ())), preferred_element_type=F32)
+
+
+def round_order(rounds):
+    return tuple(reversed(range(rounds)))
+
+
+def attend_calls(rounds):
+    order = round_order(rounds)
+    return [order[:1], order[1:2], order[2:]] if rounds > 2 else [order]
 
 
 def round_pairs(seq_count, head_count, i):
@@ -42,7 +50,8 @@
 
 
 def pack_kernel(rounds, width, where_ref, *rest):
-    ins, outs, sem = rest[:4], rest[4:-1], rest[-1]
+    ins, place_ref = rest[:4], rest[4]
+    outs, place_out, sem, place_sem = rest[5:-3], rest[-3], rest[-2], rest[-1]
     turn = lax.rem(where_ref[0], rounds)
     copies = []
     for m in range(2):
@@ -56,27 +65,34 @@
                 )
                 copy.start()
                 copies.append(copy)
+    copy = pltpu.make_async_copy(place_ref, place_out, place_sem.at[0])
+    copy.start()
+    copies.append(copy)
     for copy in copies:
         copy.wait()
 
 
-def pack(where, arrays, rounds):
+def pack(where, arrays, global_pos, rounds):
     _, tokens, columns = arrays[0].shape
     width = columns // rounds
     out = jax.ShapeDtypeStruct((2, tokens, width), BF16)
     outs = pl.pallas_call(
         functools.partial(pack_kernel, rounds, width),
-        out_shape=[out] * (2 * rounds),
-        in_specs=[SMEM] + [HBM] * 4,
-        out_specs=[VMEM] * (2 * rounds),
-        scratch_shapes=[pltpu.SemaphoreType.DMA((2 * rounds, 2))],
+        out_shape=[out] * (2 * rounds)
+        + [jax.ShapeDtypeStruct((1, global_pos.shape[0]), jnp.int32)],
+        in_specs=[SMEM] + [HBM] * 5,
+        out_specs=[VMEM] * (2 * rounds + 1),
+        scratch_shapes=[
+            pltpu.SemaphoreType.DMA((2 * rounds, 2)),
+            pltpu.SemaphoreType.DMA((1,)),
+        ],
         compiler_params=PACK_PARAMS,
         cost_estimate=pl.CostEstimate(
             flops=0, transcendentals=0, bytes_accessed=16 * tokens * columns
         ),
         name="pack",
-    )(where, *[keep_in_hbm(a) for a in arrays])
-    return outs[:rounds], outs[rounds:]
+    )(where, *[keep_in_hbm(a) for a in arrays], keep_in_hbm(global_pos.reshape(1, -1)))
+    return outs[:rounds], outs[rounds:-1], outs[-1]
 
 
 def unpack_kernel(rounds, width, where_ref, *rest):
@@ -138,7 +154,7 @@
     total_blocks = 2 * rounds * run_blocks
     listed = (3 + picks) * BLOCK
     flip = (h * rounds + lax.rem(k, rounds)) * run_blocks
-    head = lax.rem(k, rounds) * (total_blocks * picks)
+    head = lax.rem(k, rounds)
     mine = k // rounds == h
     scale = all_ref.shape[2] ** -0.5
     column = lax.broadcasted_iota(jnp.int32, (1, 4 * BLOCK), 1)
@@ -169,8 +185,9 @@
             jnp.minimum(index + 1, total_blocks - 1),
         ]
         for m in range(picks):
-            at = head + index * picks + m
-            named.append(jnp.where(mine, mine_ref[at], other_table_ref[at]))
+            named.append(
+                jnp.where(mine, mine_ref[0, head, index, m], other_table_ref[0, head, index, m])
+            )
         rows = [pl.multiple_of((b ^ flip) * BLOCK, BLOCK) for b in named]
         keys, values = [
             jnp.concatenate(
@@ -231,11 +248,11 @@
             send_ref[m, half:] = shared
 
 
-def attend(where, tables, global_pos, parts, state, sides, turns, rounds, picks):
-    opens, closes = state is None, turns[-1] == rounds - 1
+def attend(where, tables, places, parts, state, sides, turns, rounds, picks, closes):
+    opens = state is None
     _, tokens, width = sides[0].shape
     run_blocks = tokens // BLOCK
-    shared = global_pos.shape[0]
+    shared = places.shape[1]
     entries = (3 + picks) * BLOCK + shared
     count = len(turns)
     half = rounds * tokens
@@ -243,7 +260,7 @@
     acc = jax.ShapeDtypeStruct((2, 2 * half + shared, width), F32)
     out_shape = [one] * count
     if opens:
-        given = [global_pos.reshape(1, shared), *parts]
+        given = [places, *parts]
         out_shape += [
             jax.ShapeDtypeStruct((2, 2 * half, width), BF16),
             jax.ShapeDtypeStruct((2, shared, width), BF16),
@@ -302,9 +319,9 @@
             outs[i][n] = whole.astype(BF16)
 
 
-def total(where, global_pos, acc, came, rounds):
+def total(where, places, acc, came, rounds):
     rows, width = came.shape[1:]
-    count = global_pos.shape[0]
+    count = places.shape[1]
     tokens = (rows - count) // rounds
     return pl.pallas_call(
         functools.partial(total_kernel, rounds),
@@ -316,7 +333,7 @@
             flops=4 * rows * width, transcendentals=0, bytes_accessed=20 * rows * width
         ),
         name="total",
-    )(where, global_pos.reshape(1, count), acc, came)
+    )(where, places, acc, came)
 
 
 def by_heads(query_rows, key_rows, value_rows, grad_out, rand_blocks, global_pos):
@@ -327,10 +344,12 @@
     sibling = [(i, i ^ 1) for i in range(head_count)]
     trades = [round_pairs(seq_count, head_count, i) for i in range(rounds)]
 
-    def send(parts, first=0):
-        out = []
-        for n, part in enumerate(parts):
-            out.append(lax.ppermute(part, AXES, trades[first + n]))
+    order = round_order(rounds)
+
+    def send(parts, turns=order):
+        out = {}
+        for n in turns:
+            out[n] = lax.ppermute(parts[n], AXES, trades[n])
         return out
 
     def swap(parts):
@@ -339,34 +358,36 @@
             out.append(lax.ppermute(part, "head", sibling))
         return out
 
-    kv, sides = pack(where, [key_rows, value_rows, query_rows, grad_out], rounds)
+    arrays = [key_rows, value_rows, query_rows, grad_out]
+    kv, sides, places = pack(where, arrays, global_pos, rounds)
     kv = send(kv)
     sides = send(sides)
-    table = rand_blocks.reshape(rand_blocks.size)
-    tables = [table, *swap([table])]
-    parts = kv + swap(kv)
-    mixes, state = [], None
-    for n in range(GROUPS):
-        turns = tuple(range(n * rounds // GROUPS, (n + 1) * rounds // GROUPS))
+    tables = [rand_blocks, *swap([rand_blocks])]
+    parts = [kv[n] for n in range(rounds)]
+    parts += swap(parts)
+    mixes, state = {}, None
+    calls = attend_calls(rounds)
+    for n, turns in enumerate(calls):
         mix, new = attend(
             where,
             tables,
-            global_pos,
+            places,
             parts,
             state,
             [sides[t] for t in turns],
             turns,
             rounds,
             picks,
+            n == len(calls) - 1,
         )
-        mixes += send(mix, turns[0])
+        mixes.update(send(dict(zip(turns, mix)), turns))
         state = new if state is None else (*state[:2], *new)
     _, _, acc, leaving = state
     (came,) = swap([leaving])
-    grads = total(where, global_pos, acc, came, rounds)
+    grads = total(where, places, acc, came, rounds)
     grads = send(grads)
-    attended, grad_query = unpack(where, mixes)
-    grad_key, grad_value = unpack(where, grads)
+    attended, grad_query = unpack(where, [mixes[n] for n in range(rounds)])
+    grad_key, grad_value = unpack(where, [grads[n] for n in range(rounds)])
     return attended, grad_query, grad_key, grad_value
 
 

time: 68.9 us -> 73.4 us (1.065)
  Pallas kernels: 12.8 us -> 19.6 us
  starting transfers between devices: 37.2 us -> 32.7 us
  waiting for transfers between devices: 16.1 us -> 19.1 us
  local copies, waits for them, and re-layouts: 1.65 us -> 0.79 us
    pallas_call x2 -> x3, Pallas kernels: 7.1 us -> 13.9 us  [attend(): pl.pallas_call(functools.partial(attend_kernel, rounds, run_blocks, picks...]
    ppermute x16, starting transfers between devices: 36.5 us -> 31.6 us  [send(): out[n] = lax.ppermute(parts[n], AXES, trades[n])]
    ppermute x16, waiting for transfers between devices: 16.1 us -> 17.8 us  [send(): out[n] = lax.ppermute(parts[n], AXES, trades[n])]
    ppermute x6, waiting for transfers between devices: 0.02 us -> 1.25 us  [swap(): out.append(lax.ppermute(part, 'head', sibling))]
  transfers between devices with their start and end apart: 22 -> 22, of which waited for: 7 -> 8; matrix products, arithmetic and copies ran while one was open for 1% -> 1% of each run, Pallas kernels for 9% -> 16%
where the time goes in v3:
time: 73.4 us; the launch traced here: 73.1 us
  starting transfers between devices  32.7 us (45%)
  Pallas kernels  19.6 us (27%)
  waiting for transfers between devices  19.1 us (26%)
  between operations  0.8 us (1%)
  local copies, waits for them, and re-layouts  0.79 us (1%)
    ppermute x16, starting transfers between devices, send(): out[n] = lax.ppermute(parts[n], AXES, trades[n])  31.6 us
    ppermute x16, waiting for transfers between devices, send(): out[n] = lax.ppermute(parts[n], AXES, trades[n])  17.8 us
    pallas_call x3, Pallas kernels, attend(): pl.pallas_call(functools.partial(attend_kernel, rounds, run_blocks, picks...  13.9 us
    pallas_call x2, Pallas kernels, unpack(): pl.pallas_call(functools.partial(unpack_kernel, rounds, width), out_shape...  2.79 us
    pallas_call x1, Pallas kernels, pack(): pl.pallas_call(functools.partial(pack_kernel, rounds, width), out_shape=[...  1.96 us
  transfers between devices with their start and end apart: 22, of which 8 were waited for; matrix products, arithmetic and copies ran while one was open for 1% of the time, Pallas kernels for 16%

profile of v3, /device:TPU:9, one launch (start us, length us, event | category | flops | bytes accessed | tf_op | source)
XLA Modules:
  0.0 73.1 jit_solution(16007042760057145135)
XLA Ops:
  0.6 0.1 pad_add_fusion.where_ref
  0.7 2.0 %pack.1 = (bf16[2,256,128]{2,1,0:T(8,128)(2,1)S(1)}, bf16[2,256,128]{2,1,0:T(8,128)(2,1)S(1)}, bf16[2,256,128]{2,1,0:T(8,128)(2,1)S(1)}, bf16[2,256,128]{2,1,0:T...) custom-call(s32[2]{0:T(128)S(1)} %pad_add_fusion.where_ref, ...), custom_call_target="tpu_custom_call" | custom-call | bytes 2097152 | tf_op jit(solution)/shard_map/pack/pallas_call | solution.py:79
  2.7 4.8 %collective-permute-start.1 = (bf16[2,256,128]{2,1,0:T(8,128)(2,1)S(1)}, bf16[2,256,128]{2,1,0:T(8,128)(2,1)S(1)}, u32[]{:S(2)}, u32[]{:S(2)}) collective-permute-start(bf16[2,256,128]{2,1,0:T(8,128)(2,1)S(1)} %get-tuple-element.32), channel_id=1, source_target_pairs={{0,0},{1,16},{2,2},{3,18},{4,4},{5,20},{6,6},{7,22},{8,8},{9,24},{... | collective-permute-start | bytes 393224 | tf_op jit(solution)/shard_map/ppermute | solution.py:352
  7.5 1.0 %collective-permute-start.2 = (bf16[2,256,128]{2,1,0:T(8,128)(2,1)S(1)}, bf16[2,256,128]{2,1,0:T(8,128)(2,1)S(1)}, u32[]{:S(2)}, u32[]{:S(2)}) collective-permute-start(bf16[2,256,128]{2,1,0:T(8,128)(2,1)S(1)} %get-tuple-element.33), channel_id=1, source_target_pairs={{0,4},{1,20},{2,6},{3,22},{4,0},{5,16},{6,2},{7,18},{8,12},{9,28},... | collective-permute-start | bytes 393224 | tf_op jit(solution)/shard_map/ppermute | solution.py:352
  8.5 1.6 %collective-permute-start.3 = (bf16[2,256,128]{2,1,0:T(8,128)(2,1)S(1)}, bf16[2,256,128]{2,1,0:T(8,128)(2,1)S(1)}, u32[]{:S(2)}, u32[]{:S(2)}) collective-permute-start(bf16[2,256,128]{2,1,0:T(8,128)(2,1)S(1)} %get-tuple-element.34), channel_id=1, source_target_pairs={{0,8},{1,24},{2,10},{3,26},{4,12},{5,28},{6,14},{7,30},{8,0},{9,16... | collective-permute-start | bytes 393224 | tf_op jit(solution)/shard_map/ppermute | solution.py:352
  10.1 0.2 collective-permute-start.4
  10.3 0.8 %copy.15.mine_ref = s32[1,4,32,3]{3,2,1,0:T(8,128)S(1)} copy(s32[1,4,32,3]{2,1,3,0:T(4,128)} %param.10) | data formatting | bytes 3072 | tf_op args[4]
  11.1 0.1 collective-permute-start
  11.1 1.2 %collective-permute-done.other_table_ref = s32[1,4,32,3]{3,2,1,0:T(8,128)S(1)} collective-permute-done((s32[1,4,32,3]{3,2,1,0:T(8,128)S(1)}, s32[1,4,32,3]{3,2,1,0:T(8,128)S(1)}, u32[]{:S(2)}, u32[]{:S(2)}) %collective-permute-start) | collective-permute-done | bytes 1568 | tf_op jit(solution)/shard_map/ppermute | solution.py:358
  12.4 2.5 %collective-permute-start.9 = (bf16[2,256,128]{2,1,0:T(8,128)(2,1)S(1)}, bf16[2,256,128]{2,1,0:T(8,128)(2,1)S(1)}, u32[]{:S(2)}, u32[]{:S(2)}) collective-permute-start(bf16[2,256,128]{2,1,0:T(8,128)(2,1)S(1)} %get-tuple-element.36), channel_id=1, source_target_pairs={{0,12},{1,28},{2,14},{3,30},{4,8},{5,24},{6,10},{7,26},{8,4},{9,20... | collective-permute-start | bytes 393224 | tf_op jit(solution)/shard_map/ppermute | solution.py:352
  14.8 0.0 collective-permute-done.1.rest_1_
  14.8 0.9 %collective-permute-start.5 = (bf16[2,256,128]{2,1,0:T(8,128)(2,1)S(1)}, bf16[2,256,128]{2,1,0:T(8,128)(2,1)S(1)}, u32[]{:S(2)}, u32[]{:S(2)}) collective-permute-start(bf16[2,256,128]{2,1,0:T(8,128)(2,1)S(1)} %collective-permute-done.1.rest_1_), channel_id=1, source_target_pairs={{0,1},{1,0},{2,3},{3,2},{4,5},{5,4},{6,7},{7,6},{8,9},{9,8},{10,11... | collective-permute-start | bytes 393224 | tf_op jit(solution)/shard_map/ppermute | solution.py:358
  15.7 0.0 collective-permute-done.2.rest_2_
  15.7 0.1 collective-permute-start.6
  15.8 2.8 %collective-permute-done.3.rest_3_ = bf16[2,256,128]{2,1,0:T(8,128)(2,1)S(1)} collective-permute-done((bf16[2,256,128]{2,1,0:T(8,128)(2,1)S(1)}, bf16[2,256,128]{2,1,0:T(8,128)(2,1)S(1)}, u32[]{:S(2)}, u32[]{:S(2)}) %collective-permute-start.3) | collective-permute-done | bytes 131104 | tf_op jit(solution)/shard_map/ppermute | solution.py:352
  18.6 0.0 collective-permute-start.7
  18.6 2.8 %collective-permute-done.4.rest_4_ = bf16[2,256,128]{2,1,0:T(8,128)(2,1)S(1)} collective-permute-done((bf16[2,256,128]{2,1,0:T(8,128)(2,1)S(1)}, bf16[2,256,128]{2,1,0:T(8,128)(2,1)S(1)}, u32[]{:S(2)}, u32[]{:S(2)}) %collective-permute-start.4) | collective-permute-done | bytes 131104 | tf_op jit(solution)/shard_map/ppermute | solution.py:352
  21.4 0.0 collective-permute-start.8
  21.4 1.4 %collective-permute-done.9.rest_9_ = bf16[2,256,128]{2,1,0:T(8,128)(2,1)S(1)} collective-permute-done((bf16[2,256,128]{2,1,0:T(8,128)(2,1)S(1)}, bf16[2,256,128]{2,1,0:T(8,128)(2,1)S(1)}, u32[]{:S(2)}, u32[]{:S(2)}) %collective-permute-start.9) | collective-permute-done | bytes 131104 | tf_op jit(solution)/shard_map/ppermute | solution.py:352
  22.8 2.6 %collective-permute-start.10 = (bf16[2,256,128]{2,1,0:T(8,128)(2,1)S(1)}, bf16[2,256,128]{2,1,0:T(8,128)(2,1)S(1)}, u32[]{:S(2)}, u32[]{:S(2)}) collective-permute-start(bf16[2,256,128]{2,1,0:T(8,128)(2,1)S(1)} %get-tuple-element.40), channel_id=1, source_target_pairs={{0,8},{1,24},{2,10},{3,26},{4,12},{5,28},{6,14},{7,30},{8,0},{9,16... | collective-permute-start | bytes 393224 | tf_op jit(solution)/shard_map/ppermute | solution.py:352
  25.4 0.0 collective-permute-done.5.rest_5_
  25.4 0.0 collective-permute-start.11
  25.4 0.0 collective-permute-done.6.rest_6_
  25.4 4.5 %collective-permute-start.12 = (bf16[2,256,128]{2,1,0:T(8,128)(2,1)S(1)}, bf16[2,256,128]{2,1,0:T(8,128)(2,1)S(1)}, u32[]{:S(2)}, u32[]{:S(2)}) collective-permute-start(bf16[2,256,128]{2,1,0:T(8,128)(2,1)S(1)} %get-tuple-element.43), channel_id=1, source_target_pairs={{0,0},{1,16},{2,2},{3,18},{4,4},{5,20},{6,6},{7,22},{8,8},{9,24},{... | collective-permute-start | bytes 393224 | tf_op jit(solution)/shard_map/ppermute | solution.py:352
  29.9 0.0 collective-permute-done.7.rest_7_
  29.9 0.0 collective-permute-done.8.rest_8_
  29.9 4.8 %attend.3 = (bf16[2,256,128]{2,1,0:T(8,128)(2,1)S(1)}, bf16[2,2048,128]{2,1,0:T(8,128)(2,1)S(1)}, bf16[2,128,128]{2,1,0:T(8,128)(2,1)S(1)}, f32[2,2176,128]{2,1,0:T(8,128)S(1)}) custom-call(s32[2]{0:T(128)S(1)} %pad_add_fusion.where_ref, s32[1,4,32,3]{3,2,1,0:T(8,128)S(1)} %copy.15.mine_ref, s32[1,4,32,3]{3,2,1,0:T(8,128)S(1)} %collective-permute-done.other_table_ref, ...), custom_call_target="tpu_custom_call" | custom-call | flops 201326592 | bytes 1572864 | tf_op jit(solution)/shard_map/attend/pallas_call | solution.py:275
  34.7 0.0 collective-permute-done.10.rest_3_
  34.8 4.2 %attend.4 = (bf16[2,256,128]{2,1,0:T(8,128)(2,1)S(1)}, f32[2,2176,128]{2,1,0:T(8,128)S(1)}) custom-call(s32[2]{0:T(128)S(1)} %pad_add_fusion.where_ref, s32[1,4,32,3]{3,2,1,0:T(8,128)S(1)} %copy.15.mine_ref, s32[1,4,32,3]{3,2,1,0:T(8,128)S(1)} %collective-permute-done.other_table_ref, ...), custom_call_target="tpu_custom_call", output_to_operand_aliasing={{1}: (5, {})} | custom-call | flops 201326592 | bytes 1572864 | tf_op jit(solution)/shard_map/attend/pallas_call | solution.py:275
  38.9 0.0 collective-permute-done.11.rest_3_
  38.9 0.0 collective-permute-done.12.rest_4_
  39.0 4.8 %attend.5 = (bf16[2,256,128]{2,1,0:T(8,128)(2,1)S(1)}, bf16[2,256,128]{2,1,0:T(8,128)(2,1)S(1)}, f32[2,2176,128]{2,1,0:T(8,128)S(1)}, f32[2,1152,128]{2,1,0:T(8,128)S(1)}) custom-call(s32[2]{0:T(128)S(1)} %pad_add_fusion.where_ref, s32[1,4,32,3]{3,2,1,0:T(8,128)S(1)} %copy.15.mine_ref, ...), custom_call_target="tpu_custom_call", output_to_operand_aliasing={{2}: (5, {})} | custom-call | flops 402653184 | bytes 1572864 | tf_op jit(solution)/shard_map/attend/pallas_call | solution.py:275
  43.8 0.1 collective-permute-start.17
  43.9 2.0 %collective-permute-start.13 = (bf16[2,256,128]{2,1,0:T(8,128)(2,1)S(1)}, bf16[2,256,128]{2,1,0:T(8,128)(2,1)S(1)}, u32[]{:S(2)}, u32[]{:S(2)}) collective-permute-start(bf16[2,256,128]{2,1,0:T(8,128)(2,1)S(1)} %get-tuple-element.44), channel_id=1, source_target_pairs={{0,0},{1,16},{2,2},{3,18},{4,4},{5,20},{6,6},{7,22},{8,8},{9,24},{... | collective-permute-start | bytes 393224 | tf_op jit(solution)/shard_map/ppermute | solution.py:352
  45.9 3.6 %collective-permute-start.14 = (bf16[2,256,128]{2,1,0:T(8,128)(2,1)S(1)}, bf16[2,256,128]{2,1,0:T(8,128)(2,1)S(1)}, u32[]{:S(2)}, u32[]{:S(2)}) collective-permute-start(bf16[2,256,128]{2,1,0:T(8,128)(2,1)S(1)} %get-tuple-element.45), channel_id=1, source_target_pairs={{0,4},{1,20},{2,6},{3,22},{4,0},{5,16},{6,2},{7,18},{8,12},{9,28},... | collective-permute-start | bytes 393224 | tf_op jit(solution)/shard_map/ppermute | solution.py:352
  49.4 0.0 collective-permute-start.15
  49.5 1.7 %collective-permute-start.16 = (bf16[2,256,128]{2,1,0:T(8,128)(2,1)S(1)}, bf16[2,256,128]{2,1,0:T(8,128)(2,1)S(1)}, u32[]{:S(2)}, u32[]{:S(2)}) collective-permute-start(bf16[2,256,128]{2,1,0:T(8,128)(2,1)S(1)} %get-tuple-element.47), channel_id=1, source_target_pairs={{0,12},{1,28},{2,14},{3,30},{4,8},{5,24},{6,10},{7,26},{8,4},{9,20... | collective-permute-start | bytes 393224 | tf_op jit(solution)/shard_map/ppermute | solution.py:352
  51.2 0.0 collective-permute-done.17.came_ref
  51.2 1.0 %total.1 = (bf16[2,256,128]{2,1,0:T(8,128)(2,1)S(1)}, bf16[2,256,128]{2,1,0:T(8,128)(2,1)S(1)}, bf16[2,256,128]{2,1,0:T(8,128)(2,1)S(1)}, bf16[2,256,128]{2,1,0:T(8,128)(2,1)S(1)}) custom-call(s32[2]{0:T(128)S(1)} %pad_add_fusion.where_ref, s32[1,128]{1,0:T(1,128)S(1)} %get-tuple-element.31.rest_0_.global_ref, ...), custom_call_target="tpu_custom_call" | custom-call | flops 589824 | bytes 2949120 | tf_op jit(solution)/shard_map/total/pallas_call | solution.py:326
  52.2 3.8 %collective-permute-start.18 = (bf16[2,256,128]{2,1,0:T(8,128)(2,1)S(1)}, bf16[2,256,128]{2,1,0:T(8,128)(2,1)S(1)}, u32[]{:S(2)}, u32[]{:S(2)}) collective-permute-start(bf16[2,256,128]{2,1,0:T(8,128)(2,1)S(1)} %get-tuple-element.52), channel_id=1, source_target_pairs={{0,0},{1,16},{2,2},{3,18},{4,4},{5,20},{6,6},{7,22},{8,8},{9,24},{... | collective-permute-start | bytes 393224 | tf_op jit(solution)/shard_map/ppermute | solution.py:352
  56.0 0.0 collective-permute-done.13.rest_0_
  56.0 1.7 %collective-permute-start.19 = (bf16[2,256,128]{2,1,0:T(8,128)(2,1)S(1)}, bf16[2,256,128]{2,1,0:T(8,128)(2,1)S(1)}, u32[]{:S(2)}, u32[]{:S(2)}) collective-permute-start(bf16[2,256,128]{2,1,0:T(8,128)(2,1)S(1)} %get-tuple-element.53), channel_id=1, source_target_pairs={{0,4},{1,20},{2,6},{3,22},{4,0},{5,16},{6,2},{7,18},{8,12},{9,28},... | collective-permute-start | bytes 393224 | tf_op jit(solution)/shard_map/ppermute | solution.py:352
  57.7 0.0 collective-permute-done.14.rest_1_
  57.7 0.5 collective-permute-start.20
  58.2 0.0 collective-permute-done.15.rest_2_
  58.2 1.2 %collective-permute-start.21 = (bf16[2,256,128]{2,1,0:T(8,128)(2,1)S(1)}, bf16[2,256,128]{2,1,0:T(8,128)(2,1)S(1)}, u32[]{:S(2)}, u32[]{:S(2)}) collective-permute-start(bf16[2,256,128]{2,1,0:T(8,128)(2,1)S(1)} %get-tuple-element.55), channel_id=1, source_target_pairs={{0,12},{1,28},{2,14},{3,30},{4,8},{5,24},{6,10},{7,26},{8,4},{9,20... | collective-permute-start | bytes 393224 | tf_op jit(solution)/shard_map/ppermute | solution.py:352
  59.4 3.8 %collective-permute-done.16.rest_3_ = bf16[2,256,128]{2,1,0:T(8,128)(2,1)S(1)} collective-permute-done((bf16[2,256,128]{2,1,0:T(8,128)(2,1)S(1)}, bf16[2,256,128]{2,1,0:T(8,128)(2,1)S(1)}, u32[]{:S(2)}, u32[]{:S(2)}) %collective-permute-start.16) | collective-permute-done | bytes 131104 | tf_op jit(solution)/shard_map/ppermute | solution.py:352
  63.3 1.4 %unpack.2 = (bf16[1,256,512]{2,1,0:T(8,128)(2,1)}, bf16[1,256,512]{2,1,0:T(8,128)(2,1)}) custom-call(s32[2]{0:T(128)S(1)} %pad_add_fusion.where_ref, bf16[2,256,128]{2,1,0:T(8,128)(2,1)S(1)} %collective-permute-done.13.rest_0_, bf16[2,256,128]{2,1,0:T(8,128)(2,1)S(1)} %collective-permute-done.14.rest_1_, ...), custom_call_target="tpu_custom_call" | custom-call | bytes 1048576 | tf_op jit(solution)/shard_map/unpack/pallas_call | solution.py:118
  64.7 0.0 collective-permute-done.18.rest_0_
  64.7 1.9 %collective-permute-done.19.rest_1_ = bf16[2,256,128]{2,1,0:T(8,128)(2,1)S(1)} collective-permute-done((bf16[2,256,128]{2,1,0:T(8,128)(2,1)S(1)}, bf16[2,256,128]{2,1,0:T(8,128)(2,1)S(1)}, u32[]{:S(2)}, u32[]{:S(2)}) %collective-permute-start.19) | collective-permute-done | bytes 131104 | tf_op jit(solution)/shard_map/ppermute | solution.py:352
  66.5 3.7 %collective-permute-done.20.rest_2_ = bf16[2,256,128]{2,1,0:T(8,128)(2,1)S(1)} collective-permute-done((bf16[2,256,128]{2,1,0:T(8,128)(2,1)S(1)}, bf16[2,256,128]{2,1,0:T(8,128)(2,1)S(1)}, u32[]{:S(2)}, u32[]{:S(2)}) %collective-permute-start.20) | collective-permute-done | bytes 131104 | tf_op jit(solution)/shard_map/ppermute | solution.py:352
  70.3 1.4 %collective-permute-done.21.rest_3_ = bf16[2,256,128]{2,1,0:T(8,128)(2,1)S(1)} collective-permute-done((bf16[2,256,128]{2,1,0:T(8,128)(2,1)S(1)}, bf16[2,256,128]{2,1,0:T(8,128)(2,1)S(1)}, u32[]{:S(2)}, u32[]{:S(2)}) %collective-permute-start.21) | collective-permute-done | bytes 131104 | tf_op jit(solution)/shard_map/ppermute | solution.py:352
  71.7 1.4 %unpack.3 = (bf16[1,256,512]{2,1,0:T(8,128)(2,1)}, bf16[1,256,512]{2,1,0:T(8,128)(2,1)}) custom-call(s32[2]{0:T(128)S(1)} %pad_add_fusion.where_ref, bf16[2,256,128]{2,1,0:T(8,128)(2,1)S(1)} %collective-permute-done.18.rest_0_, bf16[2,256,128]{2,1,0:T(8,128)(2,1)S(1)} %collective-permute-done.19.rest_1_, ...), custom_call_target="tpu_custom_call" | custom-call | bytes 1048576 | tf_op jit(solution)/shard_map/unpack/pallas_call | solution.py:118
Async XLA Ops:
  2.7 12.2 %collective-permute-start.1 = (bf16[2,256,128]{2,1,0:T(8,128)(2,1)S(1)}, bf16[2,256,128]{2,1,0:T(8,128)(2,1)S(1)}, u32[]{:S(2)}, u32[]{:S(2)}) collective-permute-start(bf16[2,256,128]{2,1,0:T(8,128)(2,1)S(1)} %get-tuple-element.32), channel_id=1, source_target_pairs={{0,0},{1,16},{2,2},{3,18},{4,4},{5,20},{6,6},{7,22},{8,8},{9,24},{... | collective-permute-start | bytes 393224 | tf_op jit(solution)/shard_map/ppermute | solution.py:352
  7.5 8.3 %collective-permute-start.2 = (bf16[2,256,128]{2,1,0:T(8,128)(2,1)S(1)}, bf16[2,256,128]{2,1,0:T(8,128)(2,1)S(1)}, u32[]{:S(2)}, u32[]{:S(2)}) collective-permute-start(bf16[2,256,128]{2,1,0:T(8,128)(2,1)S(1)} %get-tuple-element.33), channel_id=1, source_target_pairs={{0,4},{1,20},{2,6},{3,22},{4,0},{5,16},{6,2},{7,18},{8,12},{9,28},... | collective-permute-start | bytes 393224 | tf_op jit(solution)/shard_map/ppermute | solution.py:352
  8.5 10.1 %collective-permute-start.3 = (bf16[2,256,128]{2,1,0:T(8,128)(2,1)S(1)}, bf16[2,256,128]{2,1,0:T(8,128)(2,1)S(1)}, u32[]{:S(2)}, u32[]{:S(2)}) collective-permute-start(bf16[2,256,128]{2,1,0:T(8,128)(2,1)S(1)} %get-tuple-element.34), channel_id=1, source_target_pairs={{0,8},{1,24},{2,10},{3,26},{4,12},{5,28},{6,14},{7,30},{8,0},{9,16... | collective-permute-start | bytes 393224 | tf_op jit(solution)/shard_map/ppermute | solution.py:352
  10.1 11.3 %collective-permute-start.4 = (bf16[2,256,128]{2,1,0:T(8,128)(2,1)S(1)}, bf16[2,256,128]{2,1,0:T(8,128)(2,1)S(1)}, u32[]{:S(2)}, u32[]{:S(2)}) collective-permute-start(bf16[2,256,128]{2,1,0:T(8,128)(2,1)S(1)} %get-tuple-element.35), channel_id=1, source_target_pairs={{0,12},{1,28},{2,14},{3,30},{4,8},{5,24},{6,10},{7,26},{8,4},{9,20... | collective-permute-start | bytes 393224 | tf_op jit(solution)/shard_map/ppermute | solution.py:352
  11.1 1.3 %collective-permute-start = (s32[1,4,32,3]{3,2,1,0:T(8,128)S(1)}, s32[1,4,32,3]{3,2,1,0:T(8,128)S(1)}, u32[]{:S(2)}, u32[]{:S(2)}) collective-permute-start(s32[1,4,32,3]{3,2,1,0:T(8,128)S(1)} %copy.15.mine_ref), channel_id=1, source_target_pairs={{0,1},{1,0},{2,3},{3,2},{4,5},{5,4},{6,7},{7,6},{8,9},{9,8},{10,11... | collective-permute-start | bytes 4616 | tf_op jit(solution)/shard_map/ppermute | solution.py:358
  12.4 10.4 %collective-permute-start.9 = (bf16[2,256,128]{2,1,0:T(8,128)(2,1)S(1)}, bf16[2,256,128]{2,1,0:T(8,128)(2,1)S(1)}, u32[]{:S(2)}, u32[]{:S(2)}) collective-permute-start(bf16[2,256,128]{2,1,0:T(8,128)(2,1)S(1)} %get-tuple-element.36), channel_id=1, source_target_pairs={{0,12},{1,28},{2,14},{3,30},{4,8},{5,24},{6,10},{7,26},{8,4},{9,20... | collective-permute-start | bytes 393224 | tf_op jit(solution)/shard_map/ppermute | solution.py:352
  14.8 10.5 %collective-permute-start.5 = (bf16[2,256,128]{2,1,0:T(8,128)(2,1)S(1)}, bf16[2,256,128]{2,1,0:T(8,128)(2,1)S(1)}, u32[]{:S(2)}, u32[]{:S(2)}) collective-permute-start(bf16[2,256,128]{2,1,0:T(8,128)(2,1)S(1)} %collective-permute-done.1.rest_1_), channel_id=1, source_target_pairs={{0,1},{1,0},{2,3},{3,2},{4,5},{5,4},{6,7},{7,6},{8,9},{9,8},{10,11... | collective-permute-start | bytes 393224 | tf_op jit(solution)/shard_map/ppermute | solution.py:358
  15.7 9.6 %collective-permute-start.6 = (bf16[2,256,128]{2,1,0:T(8,128)(2,1)S(1)}, bf16[2,256,128]{2,1,0:T(8,128)(2,1)S(1)}, u32[]{:S(2)}, u32[]{:S(2)}) collective-permute-start(bf16[2,256,128]{2,1,0:T(8,128)(2,1)S(1)} %collective-permute-done.2.rest_2_), channel_id=1, source_target_pairs={{0,1},{1,0},{2,3},{3,2},{4,5},{5,4},{6,7},{7,6},{8,9},{9,8},{10,11... | collective-permute-start | bytes 393224 | tf_op jit(solution)/shard_map/ppermute | solution.py:358
  18.6 11.3 %collective-permute-start.7 = (bf16[2,256,128]{2,1,0:T(8,128)(2,1)S(1)}, bf16[2,256,128]{2,1,0:T(8,128)(2,1)S(1)}, u32[]{:S(2)}, u32[]{:S(2)}) collective-permute-start(bf16[2,256,128]{2,1,0:T(8,128)(2,1)S(1)} %collective-permute-done.3.rest_3_), channel_id=1, source_target_pairs={{0,1},{1,0},{2,3},{3,2},{4,5},{5,4},{6,7},{7,6},{8,9},{9,8},{10,11... | collective-permute-start | bytes 393224 | tf_op jit(solution)/shard_map/ppermute | solution.py:358
  21.4 8.5 %collective-permute-start.8 = (bf16[2,256,128]{2,1,0:T(8,128)(2,1)S(1)}, bf16[2,256,128]{2,1,0:T(8,128)(2,1)S(1)}, u32[]{:S(2)}, u32[]{:S(2)}) collective-permute-start(bf16[2,256,128]{2,1,0:T(8,128)(2,1)S(1)} %collective-permute-done.4.rest_4_), channel_id=1, source_target_pairs={{0,1},{1,0},{2,3},{3,2},{4,5},{5,4},{6,7},{7,6},{8,9},{9,8},{10,11... | collective-permute-start | bytes 393224 | tf_op jit(solution)/shard_map/ppermute | solution.py:358
  22.8 11.9 %collective-permute-start.10 = (bf16[2,256,128]{2,1,0:T(8,128)(2,1)S(1)}, bf16[2,256,128]{2,1,0:T(8,128)(2,1)S(1)}, u32[]{:S(2)}, u32[]{:S(2)}) collective-permute-start(bf16[2,256,128]{2,1,0:T(8,128)(2,1)S(1)} %get-tuple-element.40), channel_id=1, source_target_pairs={{0,8},{1,24},{2,10},{3,26},{4,12},{5,28},{6,14},{7,30},{8,0},{9,16... | collective-permute-start | bytes 393224 | tf_op jit(solution)/shard_map/ppermute | solution.py:352
  25.4 13.6 %collective-permute-start.11 = (bf16[2,256,128]{2,1,0:T(8,128)(2,1)S(1)}, bf16[2,256,128]{2,1,0:T(8,128)(2,1)S(1)}, u32[]{:S(2)}, u32[]{:S(2)}) collective-permute-start(bf16[2,256,128]{2,1,0:T(8,128)(2,1)S(1)} %get-tuple-element.42), channel_id=1, source_target_pairs={{0,4},{1,20},{2,6},{3,22},{4,0},{5,16},{6,2},{7,18},{8,12},{9,28},... | collective-permute-start | bytes 393224 | tf_op jit(solution)/shard_map/ppermute | solution.py:352
  25.4 13.6 %collective-permute-start.12 = (bf16[2,256,128]{2,1,0:T(8,128)(2,1)S(1)}, bf16[2,256,128]{2,1,0:T(8,128)(2,1)S(1)}, u32[]{:S(2)}, u32[]{:S(2)}) collective-permute-start(bf16[2,256,128]{2,1,0:T(8,128)(2,1)S(1)} %get-tuple-element.43), channel_id=1, source_target_pairs={{0,0},{1,16},{2,2},{3,18},{4,4},{5,20},{6,6},{7,22},{8,8},{9,24},{... | collective-permute-start | bytes 393224 | tf_op jit(solution)/shard_map/ppermute | solution.py:352
  43.8 7.4 %collective-permute-start.17 = (f32[2,1152,128]{2,1,0:T(8,128)S(1)}, f32[2,1152,128]{2,1,0:T(8,128)S(1)}, u32[]{:S(2)}, u32[]{:S(2)}) collective-permute-start(f32[2,1152,128]{2,1,0:T(8,128)S(1)} %get-tuple-element.51), channel_id=1, source_target_pairs={{0,1},{1,0},{2,3},{3,2},{4,5},{5,4},{6,7},{7,6},{8,9},{9,8},{10,11... | collective-permute-start | bytes 3538952 | tf_op jit(solution)/shard_map/ppermute | solution.py:358
  43.9 12.1 %collective-permute-start.13 = (bf16[2,256,128]{2,1,0:T(8,128)(2,1)S(1)}, bf16[2,256,128]{2,1,0:T(8,128)(2,1)S(1)}, u32[]{:S(2)}, u32[]{:S(2)}) collective-permute-start(bf16[2,256,128]{2,1,0:T(8,128)(2,1)S(1)} %get-tuple-element.44), channel_id=1, source_target_pairs={{0,0},{1,16},{2,2},{3,18},{4,4},{5,20},{6,6},{7,22},{8,8},{9,24},{... | collective-permute-start | bytes 393224 | tf_op jit(solution)/shard_map/ppermute | solution.py:352
  45.9 11.9 %collective-permute-start.14 = (bf16[2,256,128]{2,1,0:T(8,128)(2,1)S(1)}, bf16[2,256,128]{2,1,0:T(8,128)(2,1)S(1)}, u32[]{:S(2)}, u32[]{:S(2)}) collective-permute-start(bf16[2,256,128]{2,1,0:T(8,128)(2,1)S(1)} %get-tuple-element.45), channel_id=1, source_target_pairs={{0,4},{1,20},{2,6},{3,22},{4,0},{5,16},{6,2},{7,18},{8,12},{9,28},... | collective-permute-start | bytes 393224 | tf_op jit(solution)/shard_map/ppermute | solution.py:352
  49.4 8.8 %collective-permute-start.15 = (bf16[2,256,128]{2,1,0:T(8,128)(2,1)S(1)}, bf16[2,256,128]{2,1,0:T(8,128)(2,1)S(1)}, u32[]{:S(2)}, u32[]{:S(2)}) collective-permute-start(bf16[2,256,128]{2,1,0:T(8,128)(2,1)S(1)} %get-tuple-element.46), channel_id=1, source_target_pairs={{0,8},{1,24},{2,10},{3,26},{4,12},{5,28},{6,14},{7,30},{8,0},{9,16... | collective-permute-start | bytes 393224 | tf_op jit(solution)/shard_map/ppermute | solution.py:352
  49.5 13.8 %collective-permute-start.16 = (bf16[2,256,128]{2,1,0:T(8,128)(2,1)S(1)}, bf16[2,256,128]{2,1,0:T(8,128)(2,1)S(1)}, u32[]{:S(2)}, u32[]{:S(2)}) collective-permute-start(bf16[2,256,128]{2,1,0:T(8,128)(2,1)S(1)} %get-tuple-element.47), channel_id=1, source_target_pairs={{0,12},{1,28},{2,14},{3,30},{4,8},{5,24},{6,10},{7,26},{8,4},{9,20... | collective-permute-start | bytes 393224 | tf_op jit(solution)/shard_map/ppermute | solution.py:352
  52.2 12.5 %collective-permute-start.18 = (bf16[2,256,128]{2,1,0:T(8,128)(2,1)S(1)}, bf16[2,256,128]{2,1,0:T(8,128)(2,1)S(1)}, u32[]{:S(2)}, u32[]{:S(2)}) collective-permute-start(bf16[2,256,128]{2,1,0:T(8,128)(2,1)S(1)} %get-tuple-element.52), channel_id=1, source_target_pairs={{0,0},{1,16},{2,2},{3,18},{4,4},{5,20},{6,6},{7,22},{8,8},{9,24},{... | collective-permute-start | bytes 393224 | tf_op jit(solution)/shard_map/ppermute | solution.py:352
  56.0 10.5 %collective-permute-start.19 = (bf16[2,256,128]{2,1,0:T(8,128)(2,1)S(1)}, bf16[2,256,128]{2,1,0:T(8,128)(2,1)S(1)}, u32[]{:S(2)}, u32[]{:S(2)}) collective-permute-start(bf16[2,256,128]{2,1,0:T(8,128)(2,1)S(1)} %get-tuple-element.53), channel_id=1, source_target_pairs={{0,4},{1,20},{2,6},{3,22},{4,0},{5,16},{6,2},{7,18},{8,12},{9,28},... | collective-permute-start | bytes 393224 | tf_op jit(solution)/shard_map/ppermute | solution.py:352
  57.7 12.5 %collective-permute-start.20 = (bf16[2,256,128]{2,1,0:T(8,128)(2,1)S(1)}, bf16[2,256,128]{2,1,0:T(8,128)(2,1)S(1)}, u32[]{:S(2)}, u32[]{:S(2)}) collective-permute-start(bf16[2,256,128]{2,1,0:T(8,128)(2,1)S(1)} %get-tuple-element.54), channel_id=1, source_target_pairs={{0,8},{1,24},{2,10},{3,26},{4,12},{5,28},{6,14},{7,30},{8,0},{9,16... | collective-permute-start | bytes 393224 | tf_op jit(solution)/shard_map/ppermute | solution.py:352
  58.2 13.5 %collective-permute-start.21 = (bf16[2,256,128]{2,1,0:T(8,128)(2,1)S(1)}, bf16[2,256,128]{2,1,0:T(8,128)(2,1)S(1)}, u32[]{:S(2)}, u32[]{:S(2)}) collective-permute-start(bf16[2,256,128]{2,1,0:T(8,128)(2,1)S(1)} %get-tuple-element.55), channel_id=1, source_target_pairs={{0,12},{1,28},{2,14},{3,30},{4,8},{5,24},{6,10},{7,26},{8,4},{9,20... | collective-permute-start | bytes 393224 | tf_op jit(solution)/shard_map/ppermute | solution.py:352

commit v4 on v3

--- a/solution.py
+++ b/solution.py
@@ -31,7 +31,7 @@
 
 def attend_calls(rounds):
     order = round_order(rounds)
-    return [order[:1], order[1:2], order[2:]] if rounds > 2 else [order]
+    return [order[: rounds // 2], order[rounds // 2 :]]
 
 
 def round_pairs(seq_count, head_count, i):
@@ -154,7 +154,7 @@
     total_blocks = 2 * rounds * run_blocks
     listed = (3 + picks) * BLOCK
     flip = (h * rounds + lax.rem(k, rounds)) * run_blocks
-    head = lax.rem(k, rounds)
+    head = lax.rem(k, rounds) * (total_blocks * picks)
     mine = k // rounds == h
     scale = all_ref.shape[2] ** -0.5
     column = lax.broadcasted_iota(jnp.int32, (1, 4 * BLOCK), 1)
@@ -185,9 +185,8 @@
             jnp.minimum(index + 1, total_blocks - 1),
         ]
         for m in range(picks):
-            named.append(
-                jnp.where(mine, mine_ref[0, head, index, m], other_table_ref[0, head, index, m])
-            )
+            at = head + index * picks + m
+            named.append(jnp.where(mine, mine_ref[at], other_table_ref[at]))
         rows = [pl.multiple_of((b ^ flip) * BLOCK, BLOCK) for b in named]
         keys, values = [
             jnp.concatenate(
@@ -362,7 +361,8 @@
     kv, sides, places = pack(where, arrays, global_pos, rounds)
     kv = send(kv)
     sides = send(sides)
-    tables = [rand_blocks, *swap([rand_blocks])]
+    table = rand_blocks.reshape(rand_blocks.size)
+    tables = [table, *swap([table])]
     parts = [kv[n] for n in range(rounds)]
     parts += swap(parts)
     mixes, state = {}, None

time: 73.4 us -> 68.6 us (0.935)
  Pallas kernels: 19.6 us -> 11.7 us
  waiting for transfers between devices: 19.1 us -> 21.8 us
    pallas_call x3 -> x2, Pallas kernels: 13.9 us -> 5.98 us  [attend(): pl.pallas_call(functools.partial(attend_kernel, rounds, run_blocks, picks...]
    ppermute x16, waiting for transfers between devices: 17.8 us -> 21.7 us  [send(): out[n] = lax.ppermute(parts[n], AXES, trades[n])]
    ppermute x6, waiting for transfers between devices: 1.25 us -> 0.02 us  [swap(): out.append(lax.ppermute(part, 'head', sibling))]
  transfers between devices with their start and end apart: 22 -> 22, of which waited for: 8 -> 11; matrix products, arithmetic and copies ran while one was open for 1% -> 1% of each run, Pallas kernels for 16% -> 8%
where the time goes in v4:
time: 68.6 us; the launch traced here: 68.3 us
  starting transfers between devices  33 us (48%)
  waiting for transfers between devices  21.8 us (32%)
  Pallas kernels  11.7 us (17%)
  local copies, waits for them, and re-layouts  1 us (1%)
  between operations  0.78 us (1%)
    ppermute x16, starting transfers between devices, send(): out[n] = lax.ppermute(parts[n], AXES, trades[n])  32 us
    ppermute x16, waiting for transfers between devices, send(): out[n] = lax.ppermute(parts[n], AXES, trades[n])  21.7 us
    pallas_call x2, Pallas kernels, attend(): pl.pallas_call(functools.partial(attend_kernel, rounds, run_blocks, picks...  5.98 us
    pallas_call x2, Pallas kernels, unpack(): pl.pallas_call(functools.partial(unpack_kernel, rounds, width), out_shape...  2.79 us
    pallas_call x1, Pallas kernels, pack(): pl.pallas_call(functools.partial(pack_kernel, rounds, width), out_shape=[...  1.96 us
  transfers between devices with their start and end apart: 22, of which 11 were waited for; matrix products, arithmetic and copies ran while one was open for 1% of the time, Pallas kernels for 8%

profile of v4, /device:TPU:9, one launch (start us, length us, event | category | flops | bytes accessed | tf_op | source)
XLA Modules:
  0.0 68.3 jit_solution(2252184428884255636)
XLA Ops:
  0.6 0.1 pad_add_fusion.where_ref
  0.7 2.0 %pack.1 = (bf16[2,256,128]{2,1,0:T(8,128)(2,1)S(1)}, bf16[2,256,128]{2,1,0:T(8,128)(2,1)S(1)}, bf16[2,256,128]{2,1,0:T(8,128)(2,1)S(1)}, bf16[2,256,128]{2,1,0:T...) custom-call(s32[2]{0:T(128)S(1)} %pad_add_fusion.where_ref, ...), custom_call_target="tpu_custom_call" | custom-call | bytes 2097152 | tf_op jit(solution)/shard_map/pack/pallas_call | solution.py:79
  2.7 4.8 %collective-permute-start.1 = (bf16[2,256,128]{2,1,0:T(8,128)(2,1)S(1)}, bf16[2,256,128]{2,1,0:T(8,128)(2,1)S(1)}, u32[]{:S(2)}, u32[]{:S(2)}) collective-permute-start(bf16[2,256,128]{2,1,0:T(8,128)(2,1)S(1)} %get-tuple-element.31), channel_id=1, source_target_pairs={{0,0},{1,16},{2,2},{3,18},{4,4},{5,20},{6,6},{7,22},{8,8},{9,24},{... | collective-permute-start | bytes 393224 | tf_op jit(solution)/shard_map/ppermute | solution.py:351
  7.5 1.0 %collective-permute-start.2 = (bf16[2,256,128]{2,1,0:T(8,128)(2,1)S(1)}, bf16[2,256,128]{2,1,0:T(8,128)(2,1)S(1)}, u32[]{:S(2)}, u32[]{:S(2)}) collective-permute-start(bf16[2,256,128]{2,1,0:T(8,128)(2,1)S(1)} %get-tuple-element.32), channel_id=1, source_target_pairs={{0,4},{1,20},{2,6},{3,22},{4,0},{5,16},{6,2},{7,18},{8,12},{9,28},... | collective-permute-start | bytes 393224 | tf_op jit(solution)/shard_map/ppermute | solution.py:351
  8.5 0.8 %copy.11 = s32[1,4,32,3]{3,2,1,0:T(8,128)S(1)} copy(s32[1,4,32,3]{2,1,3,0:T(4,128)} %param.10) | data formatting | bytes 3072 | tf_op args[4]
  9.3 0.2 reshape.14.mine_ref
  9.5 0.1 collective-permute-start
  9.5 1.7 %collective-permute-start.3 = (bf16[2,256,128]{2,1,0:T(8,128)(2,1)S(1)}, bf16[2,256,128]{2,1,0:T(8,128)(2,1)S(1)}, u32[]{:S(2)}, u32[]{:S(2)}) collective-permute-start(bf16[2,256,128]{2,1,0:T(8,128)(2,1)S(1)} %get-tuple-element.33), channel_id=1, source_target_pairs={{0,8},{1,24},{2,10},{3,26},{4,12},{5,28},{6,14},{7,30},{8,0},{9,16... | collective-permute-start | bytes 393224 | tf_op jit(solution)/shard_map/ppermute | solution.py:351
  11.2 0.1 collective-permute-start.4
  11.4 0.0 collective-permute-done.other_table_ref
  11.4 2.5 %collective-permute-start.9 = (bf16[2,256,128]{2,1,0:T(8,128)(2,1)S(1)}, bf16[2,256,128]{2,1,0:T(8,128)(2,1)S(1)}, u32[]{:S(2)}, u32[]{:S(2)}) collective-permute-start(bf16[2,256,128]{2,1,0:T(8,128)(2,1)S(1)} %get-tuple-element.35), channel_id=1, source_target_pairs={{0,12},{1,28},{2,14},{3,30},{4,8},{5,24},{6,10},{7,26},{8,4},{9,20... | collective-permute-start | bytes 393224 | tf_op jit(solution)/shard_map/ppermute | solution.py:351
  13.9 0.0 collective-permute-done.1.rest_1_
  13.9 0.1 collective-permute-start.10
  14.0 0.2 collective-permute-done.2.rest_2_
  14.2 0.8 %collective-permute-start.5 = (bf16[2,256,128]{2,1,0:T(8,128)(2,1)S(1)}, bf16[2,256,128]{2,1,0:T(8,128)(2,1)S(1)}, u32[]{:S(2)}, u32[]{:S(2)}) collective-permute-start(bf16[2,256,128]{2,1,0:T(8,128)(2,1)S(1)} %collective-permute-done.1.rest_1_), channel_id=1, source_target_pairs={{0,1},{1,0},{2,3},{3,2},{4,5},{5,4},{6,7},{7,6},{8,9},{9,8},{10,11... | collective-permute-start | bytes 393224 | tf_op jit(solution)/shard_map/ppermute | solution.py:357
  15.0 2.2 %collective-permute-done.3.rest_3_ = bf16[2,256,128]{2,1,0:T(8,128)(2,1)S(1)} collective-permute-done((bf16[2,256,128]{2,1,0:T(8,128)(2,1)S(1)}, bf16[2,256,128]{2,1,0:T(8,128)(2,1)S(1)}, u32[]{:S(2)}, u32[]{:S(2)}) %collective-permute-start.3) | collective-permute-done | bytes 131104 | tf_op jit(solution)/shard_map/ppermute | solution.py:351
  17.2 0.0 collective-permute-start.6
  17.2 2.2 %collective-permute-done.4.rest_4_ = bf16[2,256,128]{2,1,0:T(8,128)(2,1)S(1)} collective-permute-done((bf16[2,256,128]{2,1,0:T(8,128)(2,1)S(1)}, bf16[2,256,128]{2,1,0:T(8,128)(2,1)S(1)}, u32[]{:S(2)}, u32[]{:S(2)}) %collective-permute-start.4) | collective-permute-done | bytes 131104 | tf_op jit(solution)/shard_map/ppermute | solution.py:351
  19.4 0.0 collective-permute-start.7
  19.4 2.4 %collective-permute-done.9.rest_9_ = bf16[2,256,128]{2,1,0:T(8,128)(2,1)S(1)} collective-permute-done((bf16[2,256,128]{2,1,0:T(8,128)(2,1)S(1)}, bf16[2,256,128]{2,1,0:T(8,128)(2,1)S(1)}, u32[]{:S(2)}, u32[]{:S(2)}) %collective-permute-start.9) | collective-permute-done | bytes 131104 | tf_op jit(solution)/shard_map/ppermute | solution.py:351
  21.8 0.0 collective-permute-start.8
  21.8 3.6 %collective-permute-done.10.rest_10_ = bf16[2,256,128]{2,1,0:T(8,128)(2,1)S(1)} collective-permute-done((bf16[2,256,128]{2,1,0:T(8,128)(2,1)S(1)}, bf16[2,256,128]{2,1,0:T(8,128)(2,1)S(1)}, u32[]{:S(2)}, u32[]{:S(2)}) %collective-permute-start.10) | collective-permute-done | bytes 131104 | tf_op jit(solution)/shard_map/ppermute | solution.py:351
  25.4 1.4 %collective-permute-start.11 = (bf16[2,256,128]{2,1,0:T(8,128)(2,1)S(1)}, bf16[2,256,128]{2,1,0:T(8,128)(2,1)S(1)}, u32[]{:S(2)}, u32[]{:S(2)}) collective-permute-start(bf16[2,256,128]{2,1,0:T(8,128)(2,1)S(1)} %get-tuple-element.40), channel_id=1, source_target_pairs={{0,4},{1,20},{2,6},{3,22},{4,0},{5,16},{6,2},{7,18},{8,12},{9,28},... | collective-permute-start | bytes 393224 | tf_op jit(solution)/shard_map/ppermute | solution.py:351
  26.8 0.0 collective-permute-done.5.rest_5_
  26.8 3.4 %collective-permute-start.12 = (bf16[2,256,128]{2,1,0:T(8,128)(2,1)S(1)}, bf16[2,256,128]{2,1,0:T(8,128)(2,1)S(1)}, u32[]{:S(2)}, u32[]{:S(2)}) collective-permute-start(bf16[2,256,128]{2,1,0:T(8,128)(2,1)S(1)} %get-tuple-element.41), channel_id=1, source_target_pairs={{0,0},{1,16},{2,2},{3,18},{4,4},{5,20},{6,6},{7,22},{8,8},{9,24},{... | collective-permute-start | bytes 393224 | tf_op jit(solution)/shard_map/ppermute | solution.py:351
  30.2 0.0 collective-permute-done.6.rest_6_
  30.2 0.0 collective-permute-done.7.rest_7_
  30.2 0.0 collective-permute-done.8.rest_8_
  30.2 3.3 %attend.2 = (bf16[2,256,128]{2,1,0:T(8,128)(2,1)S(1)}, bf16[2,256,128]{2,1,0:T(8,128)(2,1)S(1)}, bf16[2,2048,128]{2,1,0:T(8,128)(2,1)S(1)}, bf16[2,128,128]{2,1,0:T(8,128)(2,1)S(1)}, f32[2,2176,128]{2,1,0:T(8,128)S(1)}) custom-call(s32[2]{0:T(128)S(1)} %pad_add_fusion.where_ref, s32[384]{0:T(512)S(1)} %reshape.14.mine_ref, ...), custom_call_target="tpu_custom_call" | custom-call | flops 402653184 | bytes 1572864 | tf_op jit(solution)/shard_map/attend/pallas_call | solution.py:274
  33.6 0.0 collective-permute-done.11.rest_3_
  33.6 0.4 collective-permute-done.12.rest_4_
  34.0 2.7 %attend.3 = (bf16[2,256,128]{2,1,0:T(8,128)(2,1)S(1)}, bf16[2,256,128]{2,1,0:T(8,128)(2,1)S(1)}, f32[2,2176,128]{2,1,0:T(8,128)S(1)}, f32[2,1152,128]{2,1,0:T(8,128)S(1)}) custom-call(s32[2]{0:T(128)S(1)} %pad_add_fusion.where_ref, s32[384]{0:T(512)S(1)} %reshape.14.mine_ref, ...), custom_call_target="tpu_custom_call", output_to_operand_aliasing={{2}: (5, {})} | custom-call | flops 402653184 | bytes 1572864 | tf_op jit(solution)/shard_map/attend/pallas_call | solution.py:274
  36.7 0.1 collective-permute-start.17
  36.8 5.1 %collective-permute-start.13 = (bf16[2,256,128]{2,1,0:T(8,128)(2,1)S(1)}, bf16[2,256,128]{2,1,0:T(8,128)(2,1)S(1)}, u32[]{:S(2)}, u32[]{:S(2)}) collective-permute-start(bf16[2,256,128]{2,1,0:T(8,128)(2,1)S(1)} %get-tuple-element.42), channel_id=1, source_target_pairs={{0,0},{1,16},{2,2},{3,18},{4,4},{5,20},{6,6},{7,22},{8,8},{9,24},{... | collective-permute-start | bytes 393224 | tf_op jit(solution)/shard_map/ppermute | solution.py:351
  41.8 1.2 %collective-permute-start.14 = (bf16[2,256,128]{2,1,0:T(8,128)(2,1)S(1)}, bf16[2,256,128]{2,1,0:T(8,128)(2,1)S(1)}, u32[]{:S(2)}, u32[]{:S(2)}) collective-permute-start(bf16[2,256,128]{2,1,0:T(8,128)(2,1)S(1)} %get-tuple-element.43), channel_id=1, source_target_pairs={{0,4},{1,20},{2,6},{3,22},{4,0},{5,16},{6,2},{7,18},{8,12},{9,28},... | collective-permute-start | bytes 393224 | tf_op jit(solution)/shard_map/ppermute | solution.py:351
  43.0 1.1 %collective-permute-start.15 = (bf16[2,256,128]{2,1,0:T(8,128)(2,1)S(1)}, bf16[2,256,128]{2,1,0:T(8,128)(2,1)S(1)}, u32[]{:S(2)}, u32[]{:S(2)}) collective-permute-start(bf16[2,256,128]{2,1,0:T(8,128)(2,1)S(1)} %get-tuple-element.44), channel_id=1, source_target_pairs={{0,8},{1,24},{2,10},{3,26},{4,12},{5,28},{6,14},{7,30},{8,0},{9,16... | collective-permute-start | bytes 393224 | tf_op jit(solution)/shard_map/ppermute | solution.py:351
  44.1 0.5 collective-permute-start.16
  44.5 0.0 collective-permute-done.17.came_ref
  44.5 1.0 %total.1 = (bf16[2,256,128]{2,1,0:T(8,128)(2,1)S(1)}, bf16[2,256,128]{2,1,0:T(8,128)(2,1)S(1)}, bf16[2,256,128]{2,1,0:T(8,128)(2,1)S(1)}, bf16[2,256,128]{2,1,0:T(8,128)(2,1)S(1)}) custom-call(s32[2]{0:T(128)S(1)} %pad_add_fusion.where_ref, s32[1,128]{1,0:T(1,128)S(1)} %get-tuple-element.30.rest_0_.global_ref, ...), custom_call_target="tpu_custom_call" | custom-call | flops 589824 | bytes 2949120 | tf_op jit(solution)/shard_map/total/pallas_call | solution.py:325
  45.5 6.3 %collective-permute-start.18 = (bf16[2,256,128]{2,1,0:T(8,128)(2,1)S(1)}, bf16[2,256,128]{2,1,0:T(8,128)(2,1)S(1)}, u32[]{:S(2)}, u32[]{:S(2)}) collective-permute-start(bf16[2,256,128]{2,1,0:T(8,128)(2,1)S(1)} %get-tuple-element.50), channel_id=1, source_target_pairs={{0,0},{1,16},{2,2},{3,18},{4,4},{5,20},{6,6},{7,22},{8,8},{9,24},{... | collective-permute-start | bytes 393224 | tf_op jit(solution)/shard_map/ppermute | solution.py:351
  51.9 0.0 collective-permute-done.13.rest_0_
  51.9 0.8 %collective-permute-start.19 = (bf16[2,256,128]{2,1,0:T(8,128)(2,1)S(1)}, bf16[2,256,128]{2,1,0:T(8,128)(2,1)S(1)}, u32[]{:S(2)}, u32[]{:S(2)}) collective-permute-start(bf16[2,256,128]{2,1,0:T(8,128)(2,1)S(1)} %get-tuple-element.51), channel_id=1, source_target_pairs={{0,4},{1,20},{2,6},{3,22},{4,0},{5,16},{6,2},{7,18},{8,12},{9,28},... | collective-permute-start | bytes 393224 | tf_op jit(solution)/shard_map/ppermute | solution.py:351
  52.6 0.0 collective-permute-done.14.rest_1_
  52.6 1.5 %collective-permute-start.20 = (bf16[2,256,128]{2,1,0:T(8,128)(2,1)S(1)}, bf16[2,256,128]{2,1,0:T(8,128)(2,1)S(1)}, u32[]{:S(2)}, u32[]{:S(2)}) collective-permute-start(bf16[2,256,128]{2,1,0:T(8,128)(2,1)S(1)} %get-tuple-element.52), channel_id=1, source_target_pairs={{0,8},{1,24},{2,10},{3,26},{4,12},{5,28},{6,14},{7,30},{8,0},{9,16... | collective-permute-start | bytes 393224 | tf_op jit(solution)/shard_map/ppermute | solution.py:351
  54.1 0.0 collective-permute-done.15.rest_2_
  54.1 0.6 collective-permute-start.21
  54.8 3.8 %collective-permute-done.16.rest_3_ = bf16[2,256,128]{2,1,0:T(8,128)(2,1)S(1)} collective-permute-done((bf16[2,256,128]{2,1,0:T(8,128)(2,1)S(1)}, bf16[2,256,128]{2,1,0:T(8,128)(2,1)S(1)}, u32[]{:S(2)}, u32[]{:S(2)}) %collective-permute-start.16) | collective-permute-done | bytes 131104 | tf_op jit(solution)/shard_map/ppermute | solution.py:351
  58.5 1.4 %unpack.2 = (bf16[1,256,512]{2,1,0:T(8,128)(2,1)}, bf16[1,256,512]{2,1,0:T(8,128)(2,1)}) custom-call(s32[2]{0:T(128)S(1)} %pad_add_fusion.where_ref, bf16[2,256,128]{2,1,0:T(8,128)(2,1)S(1)} %collective-permute-done.13.rest_0_, bf16[2,256,128]{2,1,0:T(8,128)(2,1)S(1)} %collective-permute-done.14.rest_1_, ...), custom_call_target="tpu_custom_call" | custom-call | bytes 1048576 | tf_op jit(solution)/shard_map/unpack/pallas_call | solution.py:118
  59.9 0.5 collective-permute-done.18.rest_0_
  60.4 1.4 %collective-permute-done.19.rest_1_ = bf16[2,256,128]{2,1,0:T(8,128)(2,1)S(1)} collective-permute-done((bf16[2,256,128]{2,1,0:T(8,128)(2,1)S(1)}, bf16[2,256,128]{2,1,0:T(8,128)(2,1)S(1)}, u32[]{:S(2)}, u32[]{:S(2)}) %collective-permute-start.19) | collective-permute-done | bytes 131104 | tf_op jit(solution)/shard_map/ppermute | solution.py:351
  61.8 2.7 %collective-permute-done.20.rest_2_ = bf16[2,256,128]{2,1,0:T(8,128)(2,1)S(1)} collective-permute-done((bf16[2,256,128]{2,1,0:T(8,128)(2,1)S(1)}, bf16[2,256,128]{2,1,0:T(8,128)(2,1)S(1)}, u32[]{:S(2)}, u32[]{:S(2)}) %collective-permute-start.20) | collective-permute-done | bytes 131104 | tf_op jit(solution)/shard_map/ppermute | solution.py:351
  64.6 2.4 %collective-permute-done.21.rest_3_ = bf16[2,256,128]{2,1,0:T(8,128)(2,1)S(1)} collective-permute-done((bf16[2,256,128]{2,1,0:T(8,128)(2,1)S(1)}, bf16[2,256,128]{2,1,0:T(8,128)(2,1)S(1)}, u32[]{:S(2)}, u32[]{:S(2)}) %collective-permute-start.21) | collective-permute-done | bytes 131104 | tf_op jit(solution)/shard_map/ppermute | solution.py:351
  67.0 1.4 %unpack.3 = (bf16[1,256,512]{2,1,0:T(8,128)(2,1)}, bf16[1,256,512]{2,1,0:T(8,128)(2,1)}) custom-call(s32[2]{0:T(128)S(1)} %pad_add_fusion.where_ref, bf16[2,256,128]{2,1,0:T(8,128)(2,1)S(1)} %collective-permute-done.18.rest_0_, bf16[2,256,128]{2,1,0:T(8,128)(2,1)S(1)} %collective-permute-done.19.rest_1_, ...), custom_call_target="tpu_custom_call" | custom-call | bytes 1048576 | tf_op jit(solution)/shard_map/unpack/pallas_call | solution.py:118
Async XLA Ops:
  2.7 11.2 %collective-permute-start.1 = (bf16[2,256,128]{2,1,0:T(8,128)(2,1)S(1)}, bf16[2,256,128]{2,1,0:T(8,128)(2,1)S(1)}, u32[]{:S(2)}, u32[]{:S(2)}) collective-permute-start(bf16[2,256,128]{2,1,0:T(8,128)(2,1)S(1)} %get-tuple-element.31), channel_id=1, source_target_pairs={{0,0},{1,16},{2,2},{3,18},{4,4},{5,20},{6,6},{7,22},{8,8},{9,24},{... | collective-permute-start | bytes 393224 | tf_op jit(solution)/shard_map/ppermute | solution.py:351
  7.5 6.7 %collective-permute-start.2 = (bf16[2,256,128]{2,1,0:T(8,128)(2,1)S(1)}, bf16[2,256,128]{2,1,0:T(8,128)(2,1)S(1)}, u32[]{:S(2)}, u32[]{:S(2)}) collective-permute-start(bf16[2,256,128]{2,1,0:T(8,128)(2,1)S(1)} %get-tuple-element.32), channel_id=1, source_target_pairs={{0,4},{1,20},{2,6},{3,22},{4,0},{5,16},{6,2},{7,18},{8,12},{9,28},... | collective-permute-start | bytes 393224 | tf_op jit(solution)/shard_map/ppermute | solution.py:351
  9.5 1.9 %collective-permute-start = (s32[384]{0:T(512)S(1)}, s32[384]{0:T(512)S(1)}, u32[]{:S(2)}, u32[]{:S(2)}) collective-permute-start(s32[384]{0:T(512)S(1)} %reshape.14.mine_ref), channel_id=1, source_target_pairs={{0,1},{1,0},{2,3},{3,2},{4,5},{5,4},{6,7},{7,6},{8,9},{9,8},{10,11... | collective-permute-start | bytes 4616 | tf_op jit(solution)/shard_map/ppermute | solution.py:357
  9.5 7.6 %collective-permute-start.3 = (bf16[2,256,128]{2,1,0:T(8,128)(2,1)S(1)}, bf16[2,256,128]{2,1,0:T(8,128)(2,1)S(1)}, u32[]{:S(2)}, u32[]{:S(2)}) collective-permute-start(bf16[2,256,128]{2,1,0:T(8,128)(2,1)S(1)} %get-tuple-element.33), channel_id=1, source_target_pairs={{0,8},{1,24},{2,10},{3,26},{4,12},{5,28},{6,14},{7,30},{8,0},{9,16... | collective-permute-start | bytes 393224 | tf_op jit(solution)/shard_map/ppermute | solution.py:351
  11.2 8.2 %collective-permute-start.4 = (bf16[2,256,128]{2,1,0:T(8,128)(2,1)S(1)}, bf16[2,256,128]{2,1,0:T(8,128)(2,1)S(1)}, u32[]{:S(2)}, u32[]{:S(2)}) collective-permute-start(bf16[2,256,128]{2,1,0:T(8,128)(2,1)S(1)} %get-tuple-element.34), channel_id=1, source_target_pairs={{0,12},{1,28},{2,14},{3,30},{4,8},{5,24},{6,10},{7,26},{8,4},{9,20... | collective-permute-start | bytes 393224 | tf_op jit(solution)/shard_map/ppermute | solution.py:351
  11.4 10.4 %collective-permute-start.9 = (bf16[2,256,128]{2,1,0:T(8,128)(2,1)S(1)}, bf16[2,256,128]{2,1,0:T(8,128)(2,1)S(1)}, u32[]{:S(2)}, u32[]{:S(2)}) collective-permute-start(bf16[2,256,128]{2,1,0:T(8,128)(2,1)S(1)} %get-tuple-element.35), channel_id=1, source_target_pairs={{0,12},{1,28},{2,14},{3,30},{4,8},{5,24},{6,10},{7,26},{8,4},{9,20... | collective-permute-start | bytes 393224 | tf_op jit(solution)/shard_map/ppermute | solution.py:351
  13.9 11.5 %collective-permute-start.10 = (bf16[2,256,128]{2,1,0:T(8,128)(2,1)S(1)}, bf16[2,256,128]{2,1,0:T(8,128)(2,1)S(1)}, u32[]{:S(2)}, u32[]{:S(2)}) collective-permute-start(bf16[2,256,128]{2,1,0:T(8,128)(2,1)S(1)} %get-tuple-element.36), channel_id=1, source_target_pairs={{0,8},{1,24},{2,10},{3,26},{4,12},{5,28},{6,14},{7,30},{8,0},{9,16... | collective-permute-start | bytes 393224 | tf_op jit(solution)/shard_map/ppermute | solution.py:351
  14.2 12.7 %collective-permute-start.5 = (bf16[2,256,128]{2,1,0:T(8,128)(2,1)S(1)}, bf16[2,256,128]{2,1,0:T(8,128)(2,1)S(1)}, u32[]{:S(2)}, u32[]{:S(2)}) collective-permute-start(bf16[2,256,128]{2,1,0:T(8,128)(2,1)S(1)} %collective-permute-done.1.rest_1_), channel_id=1, source_target_pairs={{0,1},{1,0},{2,3},{3,2},{4,5},{5,4},{6,7},{7,6},{8,9},{9,8},{10,11... | collective-permute-start | bytes 393224 | tf_op jit(solution)/shard_map/ppermute | solution.py:357
  17.2 13.0 %collective-permute-start.6 = (bf16[2,256,128]{2,1,0:T(8,128)(2,1)S(1)}, bf16[2,256,128]{2,1,0:T(8,128)(2,1)S(1)}, u32[]{:S(2)}, u32[]{:S(2)}) collective-permute-start(bf16[2,256,128]{2,1,0:T(8,128)(2,1)S(1)} %collective-permute-done.2.rest_2_), channel_id=1, source_target_pairs={{0,1},{1,0},{2,3},{3,2},{4,5},{5,4},{6,7},{7,6},{8,9},{9,8},{10,11... | collective-permute-start | bytes 393224 | tf_op jit(solution)/shard_map/ppermute | solution.py:357
  19.4 10.8 %collective-permute-start.7 = (bf16[2,256,128]{2,1,0:T(8,128)(2,1)S(1)}, bf16[2,256,128]{2,1,0:T(8,128)(2,1)S(1)}, u32[]{:S(2)}, u32[]{:S(2)}) collective-permute-start(bf16[2,256,128]{2,1,0:T(8,128)(2,1)S(1)} %collective-permute-done.3.rest_3_), channel_id=1, source_target_pairs={{0,1},{1,0},{2,3},{3,2},{4,5},{5,4},{6,7},{7,6},{8,9},{9,8},{10,11... | collective-permute-start | bytes 393224 | tf_op jit(solution)/shard_map/ppermute | solution.py:357
  21.8 8.5 %collective-permute-start.8 = (bf16[2,256,128]{2,1,0:T(8,128)(2,1)S(1)}, bf16[2,256,128]{2,1,0:T(8,128)(2,1)S(1)}, u32[]{:S(2)}, u32[]{:S(2)}) collective-permute-start(bf16[2,256,128]{2,1,0:T(8,128)(2,1)S(1)} %collective-permute-done.4.rest_4_), channel_id=1, source_target_pairs={{0,1},{1,0},{2,3},{3,2},{4,5},{5,4},{6,7},{7,6},{8,9},{9,8},{10,11... | collective-permute-start | bytes 393224 | tf_op jit(solution)/shard_map/ppermute | solution.py:357
  25.4 8.2 %collective-permute-start.11 = (bf16[2,256,128]{2,1,0:T(8,128)(2,1)S(1)}, bf16[2,256,128]{2,1,0:T(8,128)(2,1)S(1)}, u32[]{:S(2)}, u32[]{:S(2)}) collective-permute-start(bf16[2,256,128]{2,1,0:T(8,128)(2,1)S(1)} %get-tuple-element.40), channel_id=1, source_target_pairs={{0,4},{1,20},{2,6},{3,22},{4,0},{5,16},{6,2},{7,18},{8,12},{9,28},... | collective-permute-start | bytes 393224 | tf_op jit(solution)/shard_map/ppermute | solution.py:351
  26.8 7.2 %collective-permute-start.12 = (bf16[2,256,128]{2,1,0:T(8,128)(2,1)S(1)}, bf16[2,256,128]{2,1,0:T(8,128)(2,1)S(1)}, u32[]{:S(2)}, u32[]{:S(2)}) collective-permute-start(bf16[2,256,128]{2,1,0:T(8,128)(2,1)S(1)} %get-tuple-element.41), channel_id=1, source_target_pairs={{0,0},{1,16},{2,2},{3,18},{4,4},{5,20},{6,6},{7,22},{8,8},{9,24},{... | collective-permute-start | bytes 393224 | tf_op jit(solution)/shard_map/ppermute | solution.py:351
  36.7 7.9 %collective-permute-start.17 = (f32[2,1152,128]{2,1,0:T(8,128)S(1)}, f32[2,1152,128]{2,1,0:T(8,128)S(1)}, u32[]{:S(2)}, u32[]{:S(2)}) collective-permute-start(f32[2,1152,128]{2,1,0:T(8,128)S(1)} %get-tuple-element.49), channel_id=1, source_target_pairs={{0,1},{1,0},{2,3},{3,2},{4,5},{5,4},{6,7},{7,6},{8,9},{9,8},{10,11... | collective-permute-start | bytes 3538952 | tf_op jit(solution)/shard_map/ppermute | solution.py:357
  36.8 15.1 %collective-permute-start.13 = (bf16[2,256,128]{2,1,0:T(8,128)(2,1)S(1)}, bf16[2,256,128]{2,1,0:T(8,128)(2,1)S(1)}, u32[]{:S(2)}, u32[]{:S(2)}) collective-permute-start(bf16[2,256,128]{2,1,0:T(8,128)(2,1)S(1)} %get-tuple-element.42), channel_id=1, source_target_pairs={{0,0},{1,16},{2,2},{3,18},{4,4},{5,20},{6,6},{7,22},{8,8},{9,24},{... | collective-permute-start | bytes 393224 | tf_op jit(solution)/shard_map/ppermute | solution.py:351
  41.8 10.8 %collective-permute-start.14 = (bf16[2,256,128]{2,1,0:T(8,128)(2,1)S(1)}, bf16[2,256,128]{2,1,0:T(8,128)(2,1)S(1)}, u32[]{:S(2)}, u32[]{:S(2)}) collective-permute-start(bf16[2,256,128]{2,1,0:T(8,128)(2,1)S(1)} %get-tuple-element.43), channel_id=1, source_target_pairs={{0,4},{1,20},{2,6},{3,22},{4,0},{5,16},{6,2},{7,18},{8,12},{9,28},... | collective-permute-start | bytes 393224 | tf_op jit(solution)/shard_map/ppermute | solution.py:351
  43.0 11.2 %collective-permute-start.15 = (bf16[2,256,128]{2,1,0:T(8,128)(2,1)S(1)}, bf16[2,256,128]{2,1,0:T(8,128)(2,1)S(1)}, u32[]{:S(2)}, u32[]{:S(2)}) collective-permute-start(bf16[2,256,128]{2,1,0:T(8,128)(2,1)S(1)} %get-tuple-element.44), channel_id=1, source_target_pairs={{0,8},{1,24},{2,10},{3,26},{4,12},{5,28},{6,14},{7,30},{8,0},{9,16... | collective-permute-start | bytes 393224 | tf_op jit(solution)/shard_map/ppermute | solution.py:351
  44.1 14.5 %collective-permute-start.16 = (bf16[2,256,128]{2,1,0:T(8,128)(2,1)S(1)}, bf16[2,256,128]{2,1,0:T(8,128)(2,1)S(1)}, u32[]{:S(2)}, u32[]{:S(2)}) collective-permute-start(bf16[2,256,128]{2,1,0:T(8,128)(2,1)S(1)} %get-tuple-element.45), channel_id=1, source_target_pairs={{0,12},{1,28},{2,14},{3,30},{4,8},{5,24},{6,10},{7,26},{8,4},{9,20... | collective-permute-start | bytes 393224 | tf_op jit(solution)/shard_map/ppermute | solution.py:351
  45.5 14.9 %collective-permute-start.18 = (bf16[2,256,128]{2,1,0:T(8,128)(2,1)S(1)}, bf16[2,256,128]{2,1,0:T(8,128)(2,1)S(1)}, u32[]{:S(2)}, u32[]{:S(2)}) collective-permute-start(bf16[2,256,128]{2,1,0:T(8,128)(2,1)S(1)} %get-tuple-element.50), channel_id=1, source_target_pairs={{0,0},{1,16},{2,2},{3,18},{4,4},{5,20},{6,6},{7,22},{8,8},{9,24},{... | collective-permute-start | bytes 393224 | tf_op jit(solution)/shard_map/ppermute | solution.py:351
  51.9 10.0 %collective-permute-start.19 = (bf16[2,256,128]{2,1,0:T(8,128)(2,1)S(1)}, bf16[2,256,128]{2,1,0:T(8,128)(2,1)S(1)}, u32[]{:S(2)}, u32[]{:S(2)}) collective-permute-start(bf16[2,256,128]{2,1,0:T(8,128)(2,1)S(1)} %get-tuple-element.51), channel_id=1, source_target_pairs={{0,4},{1,20},{2,6},{3,22},{4,0},{5,16},{6,2},{7,18},{8,12},{9,28},... | collective-permute-start | bytes 393224 | tf_op jit(solution)/shard_map/ppermute | solution.py:351
  52.6 11.9 %collective-permute-start.20 = (bf16[2,256,128]{2,1,0:T(8,128)(2,1)S(1)}, bf16[2,256,128]{2,1,0:T(8,128)(2,1)S(1)}, u32[]{:S(2)}, u32[]{:S(2)}) collective-permute-start(bf16[2,256,128]{2,1,0:T(8,128)(2,1)S(1)} %get-tuple-element.52), channel_id=1, source_target_pairs={{0,8},{1,24},{2,10},{3,26},{4,12},{5,28},{6,14},{7,30},{8,0},{9,16... | collective-permute-start | bytes 393224 | tf_op jit(solution)/shard_map/ppermute | solution.py:351
  54.1 12.8 %collective-permute-start.21 = (bf16[2,256,128]{2,1,0:T(8,128)(2,1)S(1)}, bf16[2,256,128]{2,1,0:T(8,128)(2,1)S(1)}, u32[]{:S(2)}, u32[]{:S(2)}) collective-permute-start(bf16[2,256,128]{2,1,0:T(8,128)(2,1)S(1)} %get-tuple-element.53), channel_id=1, source_target_pairs={{0,12},{1,28},{2,14},{3,30},{4,8},{5,24},{6,10},{7,26},{8,4},{9,20... | collective-permute-start | bytes 393224 | tf_op jit(solution)/shard_map/ppermute | solution.py:351

commit v5 on v3

--- a/solution.py
+++ b/solution.py
@@ -13,7 +13,6 @@
 CHUNK = 4
 GRANT = 24 * 1024 * 1024
 VMEM = pl.BlockSpec(memory_space=pltpu.VMEM)
-SMEM = pl.BlockSpec(memory_space=pltpu.SMEM)
 PARAMS = pltpu.CompilerParams(vmem_limit_bytes=GRANT)
 PACK_PARAMS = pltpu.CompilerParams(vmem_limit_bytes=GRANT)
 HBM = pl.BlockSpec(memory_space=pltpu.HBM)
@@ -26,12 +25,12 @@
 
 
 def round_order(rounds):
-    return tuple(reversed(range(rounds)))
+    return (*range(1, rounds, 2), *range(0, rounds, 2))
 
 
 def attend_calls(rounds):
     order = round_order(rounds)
-    return [order[:1], order[1:2], order[2:]] if rounds > 2 else [order]
+    return [order[: rounds // 2], order[rounds // 2 :]]
 
 
 def round_pairs(seq_count, head_count, i):
@@ -49,10 +48,10 @@
     return pltpu.with_memory_space_constraint(array, pltpu.HBM)
 
 
-def pack_kernel(rounds, width, where_ref, *rest):
-    ins, place_ref = rest[:4], rest[4]
-    outs, place_out, sem, place_sem = rest[5:-3], rest[-3], rest[-2], rest[-1]
-    turn = lax.rem(where_ref[0], rounds)
+def pack_kernel(rounds, width, *rest):
+    ins, smalls = rest[:4], rest[4:6]
+    outs, small_outs, sem, small_sem = rest[6:-4], rest[-4:-2], rest[-2], rest[-1]
+    turn = lax.rem(lax.axis_index("seq"), rounds)
     copies = []
     for m in range(2):
         for i in range(rounds):
@@ -65,39 +64,40 @@
                 )
                 copy.start()
                 copies.append(copy)
-    copy = pltpu.make_async_copy(place_ref, place_out, place_sem.at[0])
-    copy.start()
-    copies.append(copy)
+    for m in range(2):
+        copy = pltpu.make_async_copy(smalls[m], small_outs[m], small_sem.at[m])
+        copy.start()
+        copies.append(copy)
     for copy in copies:
         copy.wait()
 
 
-def pack(where, arrays, global_pos, rounds):
+def pack(arrays, smalls, rounds):
     _, tokens, columns = arrays[0].shape
     width = columns // rounds
     out = jax.ShapeDtypeStruct((2, tokens, width), BF16)
     outs = pl.pallas_call(
         functools.partial(pack_kernel, rounds, width),
         out_shape=[out] * (2 * rounds)
-        + [jax.ShapeDtypeStruct((1, global_pos.shape[0]), jnp.int32)],
-        in_specs=[SMEM] + [HBM] * 5,
-        out_specs=[VMEM] * (2 * rounds + 1),
+        + [jax.ShapeDtypeStruct(a.shape, a.dtype) for a in smalls],
+        in_specs=[HBM] * 6,
+        out_specs=[VMEM] * (2 * rounds + 2),
         scratch_shapes=[
             pltpu.SemaphoreType.DMA((2 * rounds, 2)),
-            pltpu.SemaphoreType.DMA((1,)),
+            pltpu.SemaphoreType.DMA((2,)),
         ],
         compiler_params=PACK_PARAMS,
         cost_estimate=pl.CostEstimate(
             flops=0, transcendentals=0, bytes_accessed=16 * tokens * columns
         ),
         name="pack",
-    )(where, *[keep_in_hbm(a) for a in arrays], keep_in_hbm(global_pos.reshape(1, -1)))
-    return outs[:rounds], outs[rounds:-1], outs[-1]
-
-
-def unpack_kernel(rounds, width, where_ref, *rest):
+    )(*[keep_in_hbm(a) for a in (*arrays, *smalls)])
+    return outs[:rounds], outs[rounds:-2], outs[-2], outs[-1]
+
+
+def unpack_kernel(rounds, width, *rest):
     ins, outs, sem = rest[:rounds], rest[rounds:-1], rest[-1]
-    turn = lax.rem(where_ref[0], rounds)
+    turn = lax.rem(lax.axis_index("seq"), rounds)
     copies = []
     for i in range(rounds):
         col = pl.multiple_of((turn ^ i) * width, width)
@@ -111,14 +111,14 @@
         copy.wait()
 
 
-def unpack(where, parts):
+def unpack(parts):
     rounds = len(parts)
     _, tokens, width = parts[0].shape
     out = jax.ShapeDtypeStruct((1, tokens, rounds * width), BF16)
     return pl.pallas_call(
         functools.partial(unpack_kernel, rounds, width),
         out_shape=[out] * 2,
-        in_specs=[SMEM] + [VMEM] * rounds,
+        in_specs=[VMEM] * rounds,
         out_specs=[HBM] * 2,
         scratch_shapes=[pltpu.SemaphoreType.DMA((rounds, 2))],
         compiler_params=PARAMS,
@@ -126,11 +126,11 @@
             flops=0, transcendentals=0, bytes_accessed=8 * rounds * tokens * width
         ),
         name="unpack",
-    )(where, *parts)
+    )(*parts)
 
 
 def attend_kernel(
-    rounds, run_blocks, picks, turns, opens, closes, where_ref, mine_ref, other_table_ref, *rest
+    rounds, run_blocks, picks, turns, opens, closes, mine_ref, other_table_ref, *rest
 ):
     rest = list(rest)
     take = lambda n: [rest.pop(0) for _ in range(n)]
@@ -146,16 +146,19 @@
     (acc,) = take(1)
     if closes:
         (send_ref,) = take(1)
-    (keep,) = take(1)
-
-    k, h = where_ref[0], where_ref[1]
+    keep, table, table_sem = take(3)
+
+    k, h = lax.axis_index("seq"), lax.rem(lax.axis_index("head"), 2)
     tokens = run_blocks * BLOCK
     half = rounds * tokens
     total_blocks = 2 * rounds * run_blocks
     listed = (3 + picks) * BLOCK
     flip = (h * rounds + lax.rem(k, rounds)) * run_blocks
     head = lax.rem(k, rounds)
-    mine = k // rounds == h
+    held_here = pltpu.make_async_copy(mine_ref, table, table_sem.at[0])
+    held_there = pltpu.make_async_copy(other_table_ref, table, table_sem.at[0])
+    pl.when(k // rounds == h)(held_here.start)
+    pl.when(k // rounds != h)(held_there.start)
     scale = all_ref.shape[2] ** -0.5
     column = lax.broadcasted_iota(jnp.int32, (1, 4 * BLOCK), 1)
 
@@ -175,6 +178,8 @@
             picked_ref[m] = sums[m].astype(BF16)
         acc[...] = jnp.zeros_like(acc)
 
+    held_here.wait()
+
     def begin(n, block):
         rows_of = slice(block * BLOCK, (block + 1) * BLOCK)
         query, grad = sides[n][0, rows_of], sides[n][1, rows_of]
@@ -186,7 +191,7 @@
         ]
         for m in range(picks):
             named.append(
-                jnp.where(mine, mine_ref[0, head, index, m], other_table_ref[0, head, index, m])
+                table[m, head, index]
             )
         rows = [pl.multiple_of((b ^ flip) * BLOCK, BLOCK) for b in named]
         keys, values = [
@@ -248,7 +253,7 @@
             send_ref[m, half:] = shared
 
 
-def attend(where, tables, places, parts, state, sides, turns, rounds, picks, closes):
+def attend(tables, places, parts, state, sides, turns, rounds, picks, closes):
     opens = state is None
     _, tokens, width = sides[0].shape
     run_blocks = tokens // BLOCK
@@ -268,7 +273,7 @@
         aliases = {}
     else:
         given = list(state)
-        aliases = {3 + len(given) - 1: count}
+        aliases = {2 + len(given) - 1: count}
     out_shape += [acc]
     if closes:
         out_shape += [jax.ShapeDtypeStruct((2, half + shared, width), F32)]
@@ -277,10 +282,14 @@
             attend_kernel, rounds, run_blocks, picks, turns, opens, closes
         ),
         out_shape=out_shape,
-        in_specs=[SMEM] * 3 + [VMEM] * (len(given) + count),
+        in_specs=[VMEM] * (2 + len(given) + count),
         out_specs=[VMEM] * len(out_shape),
         input_output_aliases=aliases,
-        scratch_shapes=[pltpu.VMEM((count, 2, tokens, shared), BF16)],
+        scratch_shapes=[
+            pltpu.VMEM((count, 2, tokens, shared), BF16),
+            pltpu.SMEM(tables[0].shape, jnp.int32),
+            pltpu.SemaphoreType.DMA((1,)),
+        ],
         compiler_params=PARAMS,
         cost_estimate=pl.CostEstimate(
             flops=12 * count * tokens * entries * width,
@@ -288,16 +297,17 @@
             bytes_accessed=12 * half * width,
         ),
         name="attend",
-    )(where, *tables, *given, *sides)
+    )(*tables, *given, *sides)
     return outs[:count], outs[count:]
 
 
-def total_kernel(rounds, where_ref, global_ref, acc_ref, came_ref, *outs):
+def total_kernel(rounds, global_ref, acc_ref, came_ref, *outs):
     tokens, width = outs[0].shape[1:]
     half = rounds * tokens
     count = global_ref.shape[1]
     scale = width**-0.5
-    flip = (where_ref[1] * rounds + lax.rem(where_ref[0], rounds)) * tokens
+    k, h = lax.axis_index("seq"), lax.rem(lax.axis_index("head"), 2)
+    flip = (h * rounds + lax.rem(k, rounds)) * tokens
     spots = global_ref[...] ^ flip
     halves = []
     for n in range(2):
@@ -319,28 +329,26 @@
             outs[i][n] = whole.astype(BF16)
 
 
-def total(where, places, acc, came, rounds):
+def total(places, acc, came, rounds):
     rows, width = came.shape[1:]
     count = places.shape[1]
     tokens = (rows - count) // rounds
     return pl.pallas_call(
         functools.partial(total_kernel, rounds),
         out_shape=[jax.ShapeDtypeStruct((2, tokens, width), BF16)] * rounds,
-        in_specs=[SMEM] + [VMEM] * 3,
+        in_specs=[VMEM] * 3,
         out_specs=[VMEM] * rounds,
         compiler_params=PARAMS,
         cost_estimate=pl.CostEstimate(
             flops=4 * rows * width, transcendentals=0, bytes_accessed=20 * rows * width
         ),
         name="total",
-    )(where, places, acc, came)
+    )(places, acc, came)
 
 
 def by_heads(query_rows, key_rows, value_rows, grad_out, rand_blocks, global_pos):
     seq_count, head_count = lax.axis_size("seq"), lax.axis_size("head")
     _, rounds, _, picks = rand_blocks.shape
-    k, head_index = lax.axis_index("seq"), lax.axis_index("head")
-    where = jnp.stack([k, head_index & 1]).astype(jnp.int32)
     sibling = [(i, i ^ 1) for i in range(head_count)]
     trades = [round_pairs(seq_count, head_count, i) for i in range(rounds)]
 
@@ -359,17 +367,17 @@
         return out
 
     arrays = [key_rows, value_rows, query_rows, grad_out]
-    kv, sides, places = pack(where, arrays, global_pos, rounds)
+    smalls = [global_pos.reshape(1, -1), rand_blocks[0].transpose(2, 0, 1)]
+    kv, sides, places, table = pack(arrays, smalls, rounds)
     kv = send(kv)
     sides = send(sides)
-    tables = [rand_blocks, *swap([rand_blocks])]
+    tables = [table, *swap([table])]
     parts = [kv[n] for n in range(rounds)]
     parts += swap(parts)
     mixes, state = {}, None
     calls = attend_calls(rounds)
     for n, turns in enumerate(calls):
         mix, new = attend(
-            where,
             tables,
             places,
             parts,
@@ -384,10 +392,10 @@
         state = new if state is None else (*state[:2], *new)
     _, _, acc, leaving = state
     (came,) = swap([leaving])
-    grads = total(where, places, acc, came, rounds)
+    grads = total(places, acc, came, rounds)
     grads = send(grads)
-    attended, grad_query = unpack(where, [mixes[n] for n in range(rounds)])
-    grad_key, grad_value = unpack(where, [grads[n] for n in range(rounds)])
+    attended, grad_query = unpack([mixes[n] for n in range(rounds)])
+    grad_key, grad_value = unpack([grads[n] for n in range(rounds)])
     return attended, grad_query, grad_key, grad_value
 
 

time: 73.4 us -> 68.2 us (0.929)
  the two profiles are of different devices: /device:TPU:9 before, /device:TPU:13 now
where the time goes in v5:
time: 68.2 us; the launch traced here: 67.9 us
  starting transfers between devices  33 us (48%)
  waiting for transfers between devices  24.6 us (36%)
  Pallas kernels  9.51 us (14%)
  between operations  0.78 us (1%)
    ppermute x16, starting transfers between devices, send(): out[n] = lax.ppermute(parts[n], AXES, trades[n])  32.9 us
    ppermute x16, waiting for transfers between devices, send(): out[n] = lax.ppermute(parts[n], AXES, trades[n])  24.6 us
    pallas_call x2, Pallas kernels, attend(): pl.pallas_call(functools.partial(attend_kernel, rounds, run_blocks, picks...  5.92 us
    pallas_call x2, Pallas kernels, unpack(): pl.pallas_call(functools.partial(unpack_kernel, rounds, width), out_shape...  1.69 us
    pallas_call x1, Pallas kernels, pack(): pl.pallas_call(functools.partial(pack_kernel, rounds, width), out_shape=[...  1.45 us
  transfers between devices with their start and end apart: 22, of which 8 were waited for; matrix products, arithmetic and copies ran while one was open for 0% of the time, Pallas kernels for 7%

profile of v5, /device:TPU:13, one launch (start us, length us, event | category | flops | bytes accessed | tf_op | source)
XLA Modules:
  0.0 67.9 jit_solution(3440842483958124750)
XLA Ops:
  0.6 1.4 %pack.1 = (bf16[2,256,128]{2,1,0:T(8,128)(2,1)S(1)}, bf16[2,256,128]{2,1,0:T(8,128)(2,1)S(1)}, bf16[2,256,128]{2,1,0:T(8,128)(2,1)S(1)}, bf16[2,256,128]{2,1,0:T...) custom-call(bf16[1,256,512]{2,1,0:T(8,128)(2,1)} %rest_0_.1, ...), custom_call_target="tpu_custom_call" | custom-call | bytes 2097152 | tf_op jit(solution)/shard_map/pack/pallas_call | solution.py:79
  2.1 4.8 %collective-permute-start.1 = (bf16[2,256,128]{2,1,0:T(8,128)(2,1)S(1)}, bf16[2,256,128]{2,1,0:T(8,128)(2,1)S(1)}, u32[]{:S(2)}, u32[]{:S(2)}) collective-permute-start(bf16[2,256,128]{2,1,0:T(8,128)(2,1)S(1)} %get-tuple-element.33), channel_id=1, source_target_pairs={{0,0},{1,16},{2,2},{3,18},{4,4},{5,20},{6,6},{7,22},{8,8},{9,24},{... | collective-permute-start | bytes 393224 | tf_op jit(solution)/shard_map/ppermute | solution.py:360
  6.9 1.0 %collective-permute-start.2 = (bf16[2,256,128]{2,1,0:T(8,128)(2,1)S(1)}, bf16[2,256,128]{2,1,0:T(8,128)(2,1)S(1)}, u32[]{:S(2)}, u32[]{:S(2)}) collective-permute-start(bf16[2,256,128]{2,1,0:T(8,128)(2,1)S(1)} %get-tuple-element.34), channel_id=1, source_target_pairs={{0,4},{1,20},{2,6},{3,22},{4,0},{5,16},{6,2},{7,18},{8,12},{9,28},... | collective-permute-start | bytes 393224 | tf_op jit(solution)/shard_map/ppermute | solution.py:360
  7.9 0.0 collective-permute-start
  7.9 1.6 %collective-permute-start.3 = (bf16[2,256,128]{2,1,0:T(8,128)(2,1)S(1)}, bf16[2,256,128]{2,1,0:T(8,128)(2,1)S(1)}, u32[]{:S(2)}, u32[]{:S(2)}) collective-permute-start(bf16[2,256,128]{2,1,0:T(8,128)(2,1)S(1)} %get-tuple-element.35), channel_id=1, source_target_pairs={{0,8},{1,24},{2,10},{3,26},{4,12},{5,28},{6,14},{7,30},{8,0},{9,16... | collective-permute-start | bytes 393224 | tf_op jit(solution)/shard_map/ppermute | solution.py:360
  9.5 0.3 collective-permute-start.4
  9.8 0.0 collective-permute-done.other_table_ref
  9.8 5.2 %collective-permute-start.9 = (bf16[2,256,128]{2,1,0:T(8,128)(2,1)S(1)}, bf16[2,256,128]{2,1,0:T(8,128)(2,1)S(1)}, u32[]{:S(2)}, u32[]{:S(2)}) collective-permute-start(bf16[2,256,128]{2,1,0:T(8,128)(2,1)S(1)} %get-tuple-element.37), channel_id=1, source_target_pairs={{0,4},{1,20},{2,6},{3,22},{4,0},{5,16},{6,2},{7,18},{8,12},{9,28},... | collective-permute-start | bytes 393224 | tf_op jit(solution)/shard_map/ppermute | solution.py:360
  15.0 0.0 collective-permute-done.1.rest_1_
  15.0 0.0 collective-permute-start.10
  15.0 0.0 collective-permute-done.2.rest_2_
  15.0 0.1 collective-permute-start.5
  15.1 1.5 %collective-permute-done.3.rest_3_ = bf16[2,256,128]{2,1,0:T(8,128)(2,1)S(1)} collective-permute-done((bf16[2,256,128]{2,1,0:T(8,128)(2,1)S(1)}, bf16[2,256,128]{2,1,0:T(8,128)(2,1)S(1)}, u32[]{:S(2)}, u32[]{:S(2)}) %collective-permute-start.3) | collective-permute-done | bytes 131104 | tf_op jit(solution)/shard_map/ppermute | solution.py:360
  16.6 0.0 collective-permute-start.6
  16.6 5.0 %collective-permute-done.4.rest_4_ = bf16[2,256,128]{2,1,0:T(8,128)(2,1)S(1)} collective-permute-done((bf16[2,256,128]{2,1,0:T(8,128)(2,1)S(1)}, bf16[2,256,128]{2,1,0:T(8,128)(2,1)S(1)}, u32[]{:S(2)}, u32[]{:S(2)}) %collective-permute-start.4) | collective-permute-done | bytes 131104 | tf_op jit(solution)/shard_map/ppermute | solution.py:360
  21.5 0.0 collective-permute-start.7
  21.5 1.4 %collective-permute-done.9.rest_9_ = bf16[2,256,128]{2,1,0:T(8,128)(2,1)S(1)} collective-permute-done((bf16[2,256,128]{2,1,0:T(8,128)(2,1)S(1)}, bf16[2,256,128]{2,1,0:T(8,128)(2,1)S(1)}, u32[]{:S(2)}, u32[]{:S(2)}) %collective-permute-start.9) | collective-permute-done | bytes 131104 | tf_op jit(solution)/shard_map/ppermute | solution.py:360
  22.9 0.0 collective-permute-start.8
  22.9 2.0 %collective-permute-done.10.rest_10_ = bf16[2,256,128]{2,1,0:T(8,128)(2,1)S(1)} collective-permute-done((bf16[2,256,128]{2,1,0:T(8,128)(2,1)S(1)}, bf16[2,256,128]{2,1,0:T(8,128)(2,1)S(1)}, u32[]{:S(2)}, u32[]{:S(2)}) %collective-permute-start.10) | collective-permute-done | bytes 131104 | tf_op jit(solution)/shard_map/ppermute | solution.py:360
  24.9 4.0 %collective-permute-start.11 = (bf16[2,256,128]{2,1,0:T(8,128)(2,1)S(1)}, bf16[2,256,128]{2,1,0:T(8,128)(2,1)S(1)}, u32[]{:S(2)}, u32[]{:S(2)}) collective-permute-start(bf16[2,256,128]{2,1,0:T(8,128)(2,1)S(1)} %get-tuple-element.42), channel_id=1, source_target_pairs={{0,0},{1,16},{2,2},{3,18},{4,4},{5,20},{6,6},{7,22},{8,8},{9,24},{... | collective-permute-start | bytes 393224 | tf_op jit(solution)/shard_map/ppermute | solution.py:360
  29.0 0.0 collective-permute-done.5.rest_5_
  29.0 0.6 collective-permute-start.12
  29.5 0.0 collective-permute-done.6.rest_6_
  29.6 0.0 collective-permute-done.7.rest_7_
  29.6 0.0 collective-permute-done.8.rest_8_
  29.6 3.2 %attend.2 = (bf16[2,256,128]{2,1,0:T(8,128)(2,1)S(1)}, bf16[2,256,128]{2,1,0:T(8,128)(2,1)S(1)}, bf16[2,2048,128]{2,1,0:T(8,128)(2,1)S(1)}, bf16[2,128,128]{2,1,0:T(8,128)(2,1)S(1)}, f32[2,2176,128]{2,1,0:T(8,128)S(1)}) custom-call(s32[3,4,32]{2,1,0:T(4,128)S(1)} %get-tuple-element.31.mine_ref, s32[3,4,32]{2,1,0:T(4,128)S(1)} %collective-permute-done.other_table_ref, ...), custom_call_target="tpu_custom_call" | custom-call | flops 402653184 | bytes 1572864 | tf_op jit(solution)/shard_map/attend/pallas_call | solution.py:280
  32.7 0.0 collective-permute-done.11.rest_3_
  32.8 3.6 %collective-permute-done.12.rest_4_ = bf16[2,256,128]{2,1,0:T(8,128)(2,1)S(1)} collective-permute-done((bf16[2,256,128]{2,1,0:T(8,128)(2,1)S(1)}, bf16[2,256,128]{2,1,0:T(8,128)(2,1)S(1)}, u32[]{:S(2)}, u32[]{:S(2)}) %collective-permute-start.12) | collective-permute-done | bytes 131104 | tf_op jit(solution)/shard_map/ppermute | solution.py:360
  36.3 2.7 %attend.3 = (bf16[2,256,128]{2,1,0:T(8,128)(2,1)S(1)}, bf16[2,256,128]{2,1,0:T(8,128)(2,1)S(1)}, f32[2,2176,128]{2,1,0:T(8,128)S(1)}, f32[2,1152,128]{2,1,0:T(8,128)S(1)}) custom-call(s32[3,4,32]{2,1,0:T(4,128)S(1)} %get-tuple-element.31.mine_ref, s32[3,4,32]{2,1,0:T(4,128)S(1)} %collective-permute-done.other_table_ref, ...), custom_call_target="tpu_custom_call", output_to_operand_aliasing={{2}: (4, {})} | custom-call | flops 402653184 | bytes 1572864 | tf_op jit(solution)/shard_map/attend/pallas_call | solution.py:280
  39.1 0.1 collective-permute-start.17
  39.1 2.7 %collective-permute-start.13 = (bf16[2,256,128]{2,1,0:T(8,128)(2,1)S(1)}, bf16[2,256,128]{2,1,0:T(8,128)(2,1)S(1)}, u32[]{:S(2)}, u32[]{:S(2)}) collective-permute-start(bf16[2,256,128]{2,1,0:T(8,128)(2,1)S(1)} %get-tuple-element.44), channel_id=1, source_target_pairs={{0,0},{1,16},{2,2},{3,18},{4,4},{5,20},{6,6},{7,22},{8,8},{9,24},{... | collective-permute-start | bytes 393224 | tf_op jit(solution)/shard_map/ppermute | solution.py:360
  41.9 1.4 %collective-permute-start.15 = (bf16[2,256,128]{2,1,0:T(8,128)(2,1)S(1)}, bf16[2,256,128]{2,1,0:T(8,128)(2,1)S(1)}, u32[]{:S(2)}, u32[]{:S(2)}) collective-permute-start(bf16[2,256,128]{2,1,0:T(8,128)(2,1)S(1)} %get-tuple-element.46), channel_id=1, source_target_pairs={{0,8},{1,24},{2,10},{3,26},{4,12},{5,28},{6,14},{7,30},{8,0},{9,16... | collective-permute-start | bytes 393224 | tf_op jit(solution)/shard_map/ppermute | solution.py:360
  43.3 2.8 %collective-permute-start.14 = (bf16[2,256,128]{2,1,0:T(8,128)(2,1)S(1)}, bf16[2,256,128]{2,1,0:T(8,128)(2,1)S(1)}, u32[]{:S(2)}, u32[]{:S(2)}) collective-permute-start(bf16[2,256,128]{2,1,0:T(8,128)(2,1)S(1)} %get-tuple-element.45), channel_id=1, source_target_pairs={{0,4},{1,20},{2,6},{3,22},{4,0},{5,16},{6,2},{7,18},{8,12},{9,28},... | collective-permute-start | bytes 393224 | tf_op jit(solution)/shard_map/ppermute | solution.py:360
  46.0 1.3 %collective-permute-start.16 = (bf16[2,256,128]{2,1,0:T(8,128)(2,1)S(1)}, bf16[2,256,128]{2,1,0:T(8,128)(2,1)S(1)}, u32[]{:S(2)}, u32[]{:S(2)}) collective-permute-start(bf16[2,256,128]{2,1,0:T(8,128)(2,1)S(1)} %get-tuple-element.47), channel_id=1, source_target_pairs={{0,12},{1,28},{2,14},{3,30},{4,8},{5,24},{6,10},{7,26},{8,4},{9,20... | collective-permute-start | bytes 393224 | tf_op jit(solution)/shard_map/ppermute | solution.py:360
  47.3 0.0 collective-permute-done.17.came_ref
  47.3 0.5 total.1
  47.8 2.7 %collective-permute-start.18 = (bf16[2,256,128]{2,1,0:T(8,128)(2,1)S(1)}, bf16[2,256,128]{2,1,0:T(8,128)(2,1)S(1)}, u32[]{:S(2)}, u32[]{:S(2)}) collective-permute-start(bf16[2,256,128]{2,1,0:T(8,128)(2,1)S(1)} %get-tuple-element.52), channel_id=1, source_target_pairs={{0,0},{1,16},{2,2},{3,18},{4,4},{5,20},{6,6},{7,22},{8,8},{9,24},{... | collective-permute-start | bytes 393224 | tf_op jit(solution)/shard_map/ppermute | solution.py:360
  50.5 0.0 collective-permute-done.13.rest_0_
  50.5 2.0 %collective-permute-start.19 = (bf16[2,256,128]{2,1,0:T(8,128)(2,1)S(1)}, bf16[2,256,128]{2,1,0:T(8,128)(2,1)S(1)}, u32[]{:S(2)}, u32[]{:S(2)}) collective-permute-start(bf16[2,256,128]{2,1,0:T(8,128)(2,1)S(1)} %get-tuple-element.53), channel_id=1, source_target_pairs={{0,4},{1,20},{2,6},{3,22},{4,0},{5,16},{6,2},{7,18},{8,12},{9,28},... | collective-permute-start | bytes 393224 | tf_op jit(solution)/shard_map/ppermute | solution.py:360
  52.6 0.0 collective-permute-done.15.rest_2_
  52.6 1.2 %collective-permute-start.20 = (bf16[2,256,128]{2,1,0:T(8,128)(2,1)S(1)}, bf16[2,256,128]{2,1,0:T(8,128)(2,1)S(1)}, u32[]{:S(2)}, u32[]{:S(2)}) collective-permute-start(bf16[2,256,128]{2,1,0:T(8,128)(2,1)S(1)} %get-tuple-element.54), channel_id=1, source_target_pairs={{0,8},{1,24},{2,10},{3,26},{4,12},{5,28},{6,14},{7,30},{8,0},{9,16... | collective-permute-start | bytes 393224 | tf_op jit(solution)/shard_map/ppermute | solution.py:360
  53.8 0.0 collective-permute-done.14.rest_1_
  53.8 1.3 %collective-permute-start.21 = (bf16[2,256,128]{2,1,0:T(8,128)(2,1)S(1)}, bf16[2,256,128]{2,1,0:T(8,128)(2,1)S(1)}, u32[]{:S(2)}, u32[]{:S(2)}) collective-permute-start(bf16[2,256,128]{2,1,0:T(8,128)(2,1)S(1)} %get-tuple-element.55), channel_id=1, source_target_pairs={{0,12},{1,28},{2,14},{3,30},{4,8},{5,24},{6,10},{7,26},{8,4},{9,20... | collective-permute-start | bytes 393224 | tf_op jit(solution)/shard_map/ppermute | solution.py:360
  55.1 6.4 %collective-permute-done.16.rest_3_ = bf16[2,256,128]{2,1,0:T(8,128)(2,1)S(1)} collective-permute-done((bf16[2,256,128]{2,1,0:T(8,128)(2,1)S(1)}, bf16[2,256,128]{2,1,0:T(8,128)(2,1)S(1)}, u32[]{:S(2)}, u32[]{:S(2)}) %collective-permute-start.16) | collective-permute-done | bytes 131104 | tf_op jit(solution)/shard_map/ppermute | solution.py:360
  61.4 0.8 %unpack.2 = (bf16[1,256,512]{2,1,0:T(8,128)(2,1)}, bf16[1,256,512]{2,1,0:T(8,128)(2,1)}) custom-call(bf16[2,256,128]{2,1,0:T(8,128)(2,1)S(1)} %collective-permute-done.13.rest_0_, bf16[2,256,128]{2,1,0:T(8,128)(2,1)S(1)} %collective-permute-done.14.rest_1_, bf16[2,256,128]{2,1,0:T(8,128)(2,1)S(1)} %collective-permute-done.15.rest_2_, ...), custom_call_target="tpu_custom_call" | custom-call | bytes 1048576 | tf_op jit(solution)/shard_map/unpack/pallas_call | solution.py:118
  62.3 0.0 collective-permute-done.18.rest_0_
  62.3 0.0 collective-permute-done.19.rest_1_
  62.3 3.2 %collective-permute-done.20.rest_2_ = bf16[2,256,128]{2,1,0:T(8,128)(2,1)S(1)} collective-permute-done((bf16[2,256,128]{2,1,0:T(8,128)(2,1)S(1)}, bf16[2,256,128]{2,1,0:T(8,128)(2,1)S(1)}, u32[]{:S(2)}, u32[]{:S(2)}) %collective-permute-start.20) | collective-permute-done | bytes 131104 | tf_op jit(solution)/shard_map/ppermute | solution.py:360
  65.5 1.6 %collective-permute-done.21.rest_3_ = bf16[2,256,128]{2,1,0:T(8,128)(2,1)S(1)} collective-permute-done((bf16[2,256,128]{2,1,0:T(8,128)(2,1)S(1)}, bf16[2,256,128]{2,1,0:T(8,128)(2,1)S(1)}, u32[]{:S(2)}, u32[]{:S(2)}) %collective-permute-start.21) | collective-permute-done | bytes 131104 | tf_op jit(solution)/shard_map/ppermute | solution.py:360
  67.1 0.8 %unpack.3 = (bf16[1,256,512]{2,1,0:T(8,128)(2,1)}, bf16[1,256,512]{2,1,0:T(8,128)(2,1)}) custom-call(bf16[2,256,128]{2,1,0:T(8,128)(2,1)S(1)} %collective-permute-done.18.rest_0_, bf16[2,256,128]{2,1,0:T(8,128)(2,1)S(1)} %collective-permute-done.19.rest_1_, bf16[2,256,128]{2,1,0:T(8,128)(2,1)S(1)} %collective-permute-done.20.rest_2_, ...), custom_call_target="tpu_custom_call" | custom-call | bytes 1048576 | tf_op jit(solution)/shard_map/unpack/pallas_call | solution.py:118
Async XLA Ops:
  2.1 12.9 %collective-permute-start.1 = (bf16[2,256,128]{2,1,0:T(8,128)(2,1)S(1)}, bf16[2,256,128]{2,1,0:T(8,128)(2,1)S(1)}, u32[]{:S(2)}, u32[]{:S(2)}) collective-permute-start(bf16[2,256,128]{2,1,0:T(8,128)(2,1)S(1)} %get-tuple-element.33), channel_id=1, source_target_pairs={{0,0},{1,16},{2,2},{3,18},{4,4},{5,20},{6,6},{7,22},{8,8},{9,24},{... | collective-permute-start | bytes 393224 | tf_op jit(solution)/shard_map/ppermute | solution.py:360
  6.9 8.1 %collective-permute-start.2 = (bf16[2,256,128]{2,1,0:T(8,128)(2,1)S(1)}, bf16[2,256,128]{2,1,0:T(8,128)(2,1)S(1)}, u32[]{:S(2)}, u32[]{:S(2)}) collective-permute-start(bf16[2,256,128]{2,1,0:T(8,128)(2,1)S(1)} %get-tuple-element.34), channel_id=1, source_target_pairs={{0,4},{1,20},{2,6},{3,22},{4,0},{5,16},{6,2},{7,18},{8,12},{9,28},... | collective-permute-start | bytes 393224 | tf_op jit(solution)/shard_map/ppermute | solution.py:360
  7.9 1.9 %collective-permute-start = (s32[3,4,32]{2,1,0:T(4,128)S(1)}, s32[3,4,32]{2,1,0:T(4,128)S(1)}, u32[]{:S(2)}, u32[]{:S(2)}) collective-permute-start(s32[3,4,32]{2,1,0:T(4,128)S(1)} %get-tuple-element.31.mine_ref), channel_id=1, source_target_pairs={{0,1},{1,0},{2,3},{3,2},{4,5},{5,4},{6,7},{7,6},{8,9},{9,8},{10,11... | collective-permute-start | bytes 4616 | tf_op jit(solution)/shard_map/ppermute | solution.py:366
  7.9 8.7 %collective-permute-start.3 = (bf16[2,256,128]{2,1,0:T(8,128)(2,1)S(1)}, bf16[2,256,128]{2,1,0:T(8,128)(2,1)S(1)}, u32[]{:S(2)}, u32[]{:S(2)}) collective-permute-start(bf16[2,256,128]{2,1,0:T(8,128)(2,1)S(1)} %get-tuple-element.35), channel_id=1, source_target_pairs={{0,8},{1,24},{2,10},{3,26},{4,12},{5,28},{6,14},{7,30},{8,0},{9,16... | collective-permute-start | bytes 393224 | tf_op jit(solution)/shard_map/ppermute | solution.py:360
  9.5 12.0 %collective-permute-start.4 = (bf16[2,256,128]{2,1,0:T(8,128)(2,1)S(1)}, bf16[2,256,128]{2,1,0:T(8,128)(2,1)S(1)}, u32[]{:S(2)}, u32[]{:S(2)}) collective-permute-start(bf16[2,256,128]{2,1,0:T(8,128)(2,1)S(1)} %get-tuple-element.36), channel_id=1, source_target_pairs={{0,12},{1,28},{2,14},{3,30},{4,8},{5,24},{6,10},{7,26},{8,4},{9,20... | collective-permute-start | bytes 393224 | tf_op jit(solution)/shard_map/ppermute | solution.py:360
  9.8 13.1 %collective-permute-start.9 = (bf16[2,256,128]{2,1,0:T(8,128)(2,1)S(1)}, bf16[2,256,128]{2,1,0:T(8,128)(2,1)S(1)}, u32[]{:S(2)}, u32[]{:S(2)}) collective-permute-start(bf16[2,256,128]{2,1,0:T(8,128)(2,1)S(1)} %get-tuple-element.37), channel_id=1, source_target_pairs={{0,4},{1,20},{2,6},{3,22},{4,0},{5,16},{6,2},{7,18},{8,12},{9,28},... | collective-permute-start | bytes 393224 | tf_op jit(solution)/shard_map/ppermute | solution.py:360
  15.0 10.0 %collective-permute-start.10 = (bf16[2,256,128]{2,1,0:T(8,128)(2,1)S(1)}, bf16[2,256,128]{2,1,0:T(8,128)(2,1)S(1)}, u32[]{:S(2)}, u32[]{:S(2)}) collective-permute-start(bf16[2,256,128]{2,1,0:T(8,128)(2,1)S(1)} %get-tuple-element.38), channel_id=1, source_target_pairs={{0,12},{1,28},{2,14},{3,30},{4,8},{5,24},{6,10},{7,26},{8,4},{9,20... | collective-permute-start | bytes 393224 | tf_op jit(solution)/shard_map/ppermute | solution.py:360
  15.0 14.0 %collective-permute-start.5 = (bf16[2,256,128]{2,1,0:T(8,128)(2,1)S(1)}, bf16[2,256,128]{2,1,0:T(8,128)(2,1)S(1)}, u32[]{:S(2)}, u32[]{:S(2)}) collective-permute-start(bf16[2,256,128]{2,1,0:T(8,128)(2,1)S(1)} %collective-permute-done.1.rest_1_), channel_id=1, source_target_pairs={{0,1},{1,0},{2,3},{3,2},{4,5},{5,4},{6,7},{7,6},{8,9},{9,8},{10,11... | collective-permute-start | bytes 393224 | tf_op jit(solution)/shard_map/ppermute | solution.py:366
  16.6 13.0 %collective-permute-start.6 = (bf16[2,256,128]{2,1,0:T(8,128)(2,1)S(1)}, bf16[2,256,128]{2,1,0:T(8,128)(2,1)S(1)}, u32[]{:S(2)}, u32[]{:S(2)}) collective-permute-start(bf16[2,256,128]{2,1,0:T(8,128)(2,1)S(1)} %collective-permute-done.2.rest_2_), channel_id=1, source_target_pairs={{0,1},{1,0},{2,3},{3,2},{4,5},{5,4},{6,7},{7,6},{8,9},{9,8},{10,11... | collective-permute-start | bytes 393224 | tf_op jit(solution)/shard_map/ppermute | solution.py:366
  21.5 8.0 %collective-permute-start.7 = (bf16[2,256,128]{2,1,0:T(8,128)(2,1)S(1)}, bf16[2,256,128]{2,1,0:T(8,128)(2,1)S(1)}, u32[]{:S(2)}, u32[]{:S(2)}) collective-permute-start(bf16[2,256,128]{2,1,0:T(8,128)(2,1)S(1)} %collective-permute-done.3.rest_3_), channel_id=1, source_target_pairs={{0,1},{1,0},{2,3},{3,2},{4,5},{5,4},{6,7},{7,6},{8,9},{9,8},{10,11... | collective-permute-start | bytes 393224 | tf_op jit(solution)/shard_map/ppermute | solution.py:366
  22.9 6.6 %collective-permute-start.8 = (bf16[2,256,128]{2,1,0:T(8,128)(2,1)S(1)}, bf16[2,256,128]{2,1,0:T(8,128)(2,1)S(1)}, u32[]{:S(2)}, u32[]{:S(2)}) collective-permute-start(bf16[2,256,128]{2,1,0:T(8,128)(2,1)S(1)} %collective-permute-done.4.rest_4_), channel_id=1, source_target_pairs={{0,1},{1,0},{2,3},{3,2},{4,5},{5,4},{6,7},{7,6},{8,9},{9,8},{10,11... | collective-permute-start | bytes 393224 | tf_op jit(solution)/shard_map/ppermute | solution.py:366
  24.9 7.8 %collective-permute-start.11 = (bf16[2,256,128]{2,1,0:T(8,128)(2,1)S(1)}, bf16[2,256,128]{2,1,0:T(8,128)(2,1)S(1)}, u32[]{:S(2)}, u32[]{:S(2)}) collective-permute-start(bf16[2,256,128]{2,1,0:T(8,128)(2,1)S(1)} %get-tuple-element.42), channel_id=1, source_target_pairs={{0,0},{1,16},{2,2},{3,18},{4,4},{5,20},{6,6},{7,22},{8,8},{9,24},{... | collective-permute-start | bytes 393224 | tf_op jit(solution)/shard_map/ppermute | solution.py:360
  29.0 7.3 %collective-permute-start.12 = (bf16[2,256,128]{2,1,0:T(8,128)(2,1)S(1)}, bf16[2,256,128]{2,1,0:T(8,128)(2,1)S(1)}, u32[]{:S(2)}, u32[]{:S(2)}) collective-permute-start(bf16[2,256,128]{2,1,0:T(8,128)(2,1)S(1)} %get-tuple-element.43), channel_id=1, source_target_pairs={{0,8},{1,24},{2,10},{3,26},{4,12},{5,28},{6,14},{7,30},{8,0},{9,16... | collective-permute-start | bytes 393224 | tf_op jit(solution)/shard_map/ppermute | solution.py:360
  39.1 8.3 %collective-permute-start.17 = (f32[2,1152,128]{2,1,0:T(8,128)S(1)}, f32[2,1152,128]{2,1,0:T(8,128)S(1)}, u32[]{:S(2)}, u32[]{:S(2)}) collective-permute-start(f32[2,1152,128]{2,1,0:T(8,128)S(1)} %get-tuple-element.51), channel_id=1, source_target_pairs={{0,1},{1,0},{2,3},{3,2},{4,5},{5,4},{6,7},{7,6},{8,9},{9,8},{10,11... | collective-permute-start | bytes 3538952 | tf_op jit(solution)/shard_map/ppermute | solution.py:366
  39.1 11.4 %collective-permute-start.13 = (bf16[2,256,128]{2,1,0:T(8,128)(2,1)S(1)}, bf16[2,256,128]{2,1,0:T(8,128)(2,1)S(1)}, u32[]{:S(2)}, u32[]{:S(2)}) collective-permute-start(bf16[2,256,128]{2,1,0:T(8,128)(2,1)S(1)} %get-tuple-element.44), channel_id=1, source_target_pairs={{0,0},{1,16},{2,2},{3,18},{4,4},{5,20},{6,6},{7,22},{8,8},{9,24},{... | collective-permute-start | bytes 393224 | tf_op jit(solution)/shard_map/ppermute | solution.py:360
  41.9 10.7 %collective-permute-start.15 = (bf16[2,256,128]{2,1,0:T(8,128)(2,1)S(1)}, bf16[2,256,128]{2,1,0:T(8,128)(2,1)S(1)}, u32[]{:S(2)}, u32[]{:S(2)}) collective-permute-start(bf16[2,256,128]{2,1,0:T(8,128)(2,1)S(1)} %get-tuple-element.46), channel_id=1, source_target_pairs={{0,8},{1,24},{2,10},{3,26},{4,12},{5,28},{6,14},{7,30},{8,0},{9,16... | collective-permute-start | bytes 393224 | tf_op jit(solution)/shard_map/ppermute | solution.py:360
  43.3 10.5 %collective-permute-start.14 = (bf16[2,256,128]{2,1,0:T(8,128)(2,1)S(1)}, bf16[2,256,128]{2,1,0:T(8,128)(2,1)S(1)}, u32[]{:S(2)}, u32[]{:S(2)}) collective-permute-start(bf16[2,256,128]{2,1,0:T(8,128)(2,1)S(1)} %get-tuple-element.45), channel_id=1, source_target_pairs={{0,4},{1,20},{2,6},{3,22},{4,0},{5,16},{6,2},{7,18},{8,12},{9,28},... | collective-permute-start | bytes 393224 | tf_op jit(solution)/shard_map/ppermute | solution.py:360
  46.0 15.4 %collective-permute-start.16 = (bf16[2,256,128]{2,1,0:T(8,128)(2,1)S(1)}, bf16[2,256,128]{2,1,0:T(8,128)(2,1)S(1)}, u32[]{:S(2)}, u32[]{:S(2)}) collective-permute-start(bf16[2,256,128]{2,1,0:T(8,128)(2,1)S(1)} %get-tuple-element.47), channel_id=1, source_target_pairs={{0,12},{1,28},{2,14},{3,30},{4,8},{5,24},{6,10},{7,26},{8,4},{9,20... | collective-permute-start | bytes 393224 | tf_op jit(solution)/shard_map/ppermute | solution.py:360
  47.8 14.5 %collective-permute-start.18 = (bf16[2,256,128]{2,1,0:T(8,128)(2,1)S(1)}, bf16[2,256,128]{2,1,0:T(8,128)(2,1)S(1)}, u32[]{:S(2)}, u32[]{:S(2)}) collective-permute-start(bf16[2,256,128]{2,1,0:T(8,128)(2,1)S(1)} %get-tuple-element.52), channel_id=1, source_target_pairs={{0,0},{1,16},{2,2},{3,18},{4,4},{5,20},{6,6},{7,22},{8,8},{9,24},{... | collective-permute-start | bytes 393224 | tf_op jit(solution)/shard_map/ppermute | solution.py:360
  50.5 11.8 %collective-permute-start.19 = (bf16[2,256,128]{2,1,0:T(8,128)(2,1)S(1)}, bf16[2,256,128]{2,1,0:T(8,128)(2,1)S(1)}, u32[]{:S(2)}, u32[]{:S(2)}) collective-permute-start(bf16[2,256,128]{2,1,0:T(8,128)(2,1)S(1)} %get-tuple-element.53), channel_id=1, source_target_pairs={{0,4},{1,20},{2,6},{3,22},{4,0},{5,16},{6,2},{7,18},{8,12},{9,28},... | collective-permute-start | bytes 393224 | tf_op jit(solution)/shard_map/ppermute | solution.py:360
  52.6 12.9 %collective-permute-start.20 = (bf16[2,256,128]{2,1,0:T(8,128)(2,1)S(1)}, bf16[2,256,128]{2,1,0:T(8,128)(2,1)S(1)}, u32[]{:S(2)}, u32[]{:S(2)}) collective-permute-start(bf16[2,256,128]{2,1,0:T(8,128)(2,1)S(1)} %get-tuple-element.54), channel_id=1, source_target_pairs={{0,8},{1,24},{2,10},{3,26},{4,12},{5,28},{6,14},{7,30},{8,0},{9,16... | collective-permute-start | bytes 393224 | tf_op jit(solution)/shard_map/ppermute | solution.py:360
  53.8 13.3 %collective-permute-start.21 = (bf16[2,256,128]{2,1,0:T(8,128)(2,1)S(1)}, bf16[2,256,128]{2,1,0:T(8,128)(2,1)S(1)}, u32[]{:S(2)}, u32[]{:S(2)}) collective-permute-start(bf16[2,256,128]{2,1,0:T(8,128)(2,1)S(1)} %get-tuple-element.55), channel_id=1, source_target_pairs={{0,12},{1,28},{2,14},{3,30},{4,8},{5,24},{6,10},{7,26},{8,4},{9,20... | collective-permute-start | bytes 393224 | tf_op jit(solution)/shard_map/ppermute | solution.py:360

commit v6 on v5

--- a/solution.py
+++ b/solution.py
@@ -25,7 +25,7 @@
 
 
 def round_order(rounds):
-    return (*range(1, rounds, 2), *range(0, rounds, 2))
+    return (*range(rounds - 1, 0, -2), *range(0, rounds, 2))
 
 
 def attend_calls(rounds):
@@ -48,23 +48,21 @@
     return pltpu.with_memory_space_constraint(array, pltpu.HBM)
 
 
-def pack_kernel(rounds, width, *rest):
-    ins, smalls = rest[:4], rest[4:6]
-    outs, small_outs, sem, small_sem = rest[6:-4], rest[-4:-2], rest[-2], rest[-1]
+def pack_kernel(rounds, width, extra, *rest):
+    ins, smalls = rest[:2], rest[2 : 2 + extra]
+    outs = rest[2 + extra : 2 + extra + rounds]
+    small_outs, (sem, small_sem) = rest[2 + extra + rounds : -2], rest[-2:]
     turn = lax.rem(lax.axis_index("seq"), rounds)
     copies = []
-    for m in range(2):
-        for i in range(rounds):
-            col = pl.multiple_of((turn ^ i) * width, width)
-            for n in range(2):
-                copy = pltpu.make_async_copy(
-                    ins[2 * m + n].at[0, :, pl.ds(col, width)],
-                    outs[m * rounds + i].at[n],
-                    sem.at[m * rounds + i, n],
-                )
-                copy.start()
-                copies.append(copy)
-    for m in range(2):
+    for i in range(rounds):
+        col = pl.multiple_of((turn ^ i) * width, width)
+        for n in range(2):
+            copy = pltpu.make_async_copy(
+                ins[n].at[0, :, pl.ds(col, width)], outs[i].at[n], sem.at[i, n]
+            )
+            copy.start()
+            copies.append(copy)
+    for m in range(extra):
         copy = pltpu.make_async_copy(smalls[m], small_outs[m], small_sem.at[m])
         copy.start()
         copies.append(copy)
@@ -77,13 +75,13 @@
     width = columns // rounds
     out = jax.ShapeDtypeStruct((2, tokens, width), BF16)
     outs = pl.pallas_call(
-        functools.partial(pack_kernel, rounds, width),
-        out_shape=[out] * (2 * rounds)
+        functools.partial(pack_kernel, rounds, width, len(smalls)),
+        out_shape=[out] * rounds
         + [jax.ShapeDtypeStruct(a.shape, a.dtype) for a in smalls],
-        in_specs=[HBM] * 6,
-        out_specs=[VMEM] * (2 * rounds + 2),
+        in_specs=[HBM] * (2 + len(smalls)),
+        out_specs=[VMEM] * (rounds + len(smalls)),
         scratch_shapes=[
-            pltpu.SemaphoreType.DMA((2 * rounds, 2)),
+            pltpu.SemaphoreType.DMA((rounds, 2)),
             pltpu.SemaphoreType.DMA((2,)),
         ],
         compiler_params=PACK_PARAMS,
@@ -92,7 +90,7 @@
         ),
         name="pack",
     )(*[keep_in_hbm(a) for a in (*arrays, *smalls)])
-    return outs[:rounds], outs[rounds:-2], outs[-2], outs[-1]
+    return outs[:rounds], outs[rounds:]
 
 
 def unpack_kernel(rounds, width, *rest):
@@ -366,9 +364,9 @@
             out.append(lax.ppermute(part, "head", sibling))
         return out
 
-    arrays = [key_rows, value_rows, query_rows, grad_out]
     smalls = [global_pos.reshape(1, -1), rand_blocks[0].transpose(2, 0, 1)]
-    kv, sides, places, table = pack(arrays, smalls, rounds)
+    kv, _ = pack([key_rows, value_rows], [], rounds)
+    sides, (places, table) = pack([query_rows, grad_out], smalls, rounds)
     kv = send(kv)
     sides = send(sides)
     tables = [table, *swap([table])]
@@ -388,7 +386,7 @@
             picks,
             n == len(calls) - 1,
         )
-        mixes.update(send(dict(zip(turns, mix)), turns))
+        mixes.update(send(dict(zip(turns, mix)), turns[::-1]))
         state = new if state is None else (*state[:2], *new)
     _, _, acc, leaving = state
     (came,) = swap([leaving])

time: 68.2 us -> 67.6 us (level)
  the two profiles are of different devices: /device:TPU:13 before, /device:TPU:9 now
where the time goes in v6:
time: 67.6 us; the launch traced here: 67.3 us
  starting transfers between devices  35.1 us (52%)
  waiting for transfers between devices  21 us (31%)
  Pallas kernels  10.4 us (15%)
  between operations  0.81 us (1%)
    ppermute x16, starting transfers between devices, send(): out[n] = lax.ppermute(parts[n], AXES, trades[n])  34.7 us
    ppermute x16, waiting for transfers between devices, send(): out[n] = lax.ppermute(parts[n], AXES, trades[n])  21 us
    pallas_call x2, Pallas kernels, attend(): pl.pallas_call(functools.partial(attend_kernel, rounds, run_blocks, picks...  5.92 us
    pallas_call x2, Pallas kernels, pack(): pl.pallas_call(functools.partial(pack_kernel, rounds, width, len(smalls))...  2.35 us
    pallas_call x2, Pallas kernels, unpack(): pl.pallas_call(functools.partial(unpack_kernel, rounds, width), out_shape...  1.69 us
  transfers between devices with their start and end apart: 22, of which 8 were waited for; matrix products, arithmetic and copies ran while one was open for 0% of the time, Pallas kernels for 8%

profile of v6, /device:TPU:9, one launch (start us, length us, event | category | flops | bytes accessed | tf_op | source)
XLA Modules:
  0.0 67.3 jit_solution(5822741961804388930)
XLA Ops:
  0.6 1.2 %pack.3 = (bf16[2,256,128]{2,1,0:T(8,128)(2,1)S(1)}, bf16[2,256,128]{2,1,0:T(8,128)(2,1)S(1)}, bf16[2,256,128]{2,1,0:T(8,128)(2,1)S(1)}, bf16[2,256,128]{2,1,0:T(8,128)(2,1)S(1)}) custom-call(bf16[1,256,512]{2,1,0:T(8,128)(2,1)} %rest_0_.3, bf16[1,256,512]{2,1,0:T(8,128)(2,1)} %rest_1_.3), custom_call_target="tpu_custom_call" | custom-call | bytes 2097152 | tf_op jit(solution)/shard_map/pack/pallas_call | solution.py:77
  1.8 4.8 %collective-permute-start.1 = (bf16[2,256,128]{2,1,0:T(8,128)(2,1)S(1)}, bf16[2,256,128]{2,1,0:T(8,128)(2,1)S(1)}, u32[]{:S(2)}, u32[]{:S(2)}) collective-permute-start(bf16[2,256,128]{2,1,0:T(8,128)(2,1)S(1)} %get-tuple-element.33), channel_id=1, source_target_pairs={{0,0},{1,16},{2,2},{3,18},{4,4},{5,20},{6,6},{7,22},{8,8},{9,24},{... | collective-permute-start | bytes 393224 | tf_op jit(solution)/shard_map/ppermute | solution.py:358
  6.6 1.0 %collective-permute-start.2 = (bf16[2,256,128]{2,1,0:T(8,128)(2,1)S(1)}, bf16[2,256,128]{2,1,0:T(8,128)(2,1)S(1)}, u32[]{:S(2)}, u32[]{:S(2)}) collective-permute-start(bf16[2,256,128]{2,1,0:T(8,128)(2,1)S(1)} %get-tuple-element.34), channel_id=1, source_target_pairs={{0,4},{1,20},{2,6},{3,22},{4,0},{5,16},{6,2},{7,18},{8,12},{9,28},... | collective-permute-start | bytes 393224 | tf_op jit(solution)/shard_map/ppermute | solution.py:358
  7.6 1.2 %pack.2 = (bf16[2,256,128]{2,1,0:T(8,128)(2,1)S(1)}, bf16[2,256,128]{2,1,0:T(8,128)(2,1)S(1)}, bf16[2,256,128]{2,1,0:T(8,128)(2,1)S(1)}, bf16[2,256,128]{2,1,0:T...) custom-call(bf16[1,256,512]{2,1,0:T(8,128)(2,1)} %rest_0_.2, bf16[1,256,512]{2,1,0:T(8,128)(2,1)} %rest_1_.2, ...), custom_call_target="tpu_custom_call" | custom-call | bytes 2097152 | tf_op jit(solution)/shard_map/pack/pallas_call | solution.py:77
  8.8 0.1 collective-permute-start
  8.9 1.7 %collective-permute-start.3 = (bf16[2,256,128]{2,1,0:T(8,128)(2,1)S(1)}, bf16[2,256,128]{2,1,0:T(8,128)(2,1)S(1)}, u32[]{:S(2)}, u32[]{:S(2)}) collective-permute-start(bf16[2,256,128]{2,1,0:T(8,128)(2,1)S(1)} %get-tuple-element.35), channel_id=1, source_target_pairs={{0,8},{1,24},{2,10},{3,26},{4,12},{5,28},{6,14},{7,30},{8,0},{9,16... | collective-permute-start | bytes 393224 | tf_op jit(solution)/shard_map/ppermute | solution.py:358
  10.6 0.1 collective-permute-start.4
  10.7 0.0 collective-permute-done.other_table_ref
  10.7 2.5 %collective-permute-start.9 = (bf16[2,256,128]{2,1,0:T(8,128)(2,1)S(1)}, bf16[2,256,128]{2,1,0:T(8,128)(2,1)S(1)}, u32[]{:S(2)}, u32[]{:S(2)}) collective-permute-start(bf16[2,256,128]{2,1,0:T(8,128)(2,1)S(1)} %get-tuple-element.37), channel_id=1, source_target_pairs={{0,12},{1,28},{2,14},{3,30},{4,8},{5,24},{6,10},{7,26},{8,4},{9,20... | collective-permute-start | bytes 393224 | tf_op jit(solution)/shard_map/ppermute | solution.py:358
  13.2 0.0 collective-permute-done.1.rest_1_
  13.2 2.9 %collective-permute-start.10 = (bf16[2,256,128]{2,1,0:T(8,128)(2,1)S(1)}, bf16[2,256,128]{2,1,0:T(8,128)(2,1)S(1)}, u32[]{:S(2)}, u32[]{:S(2)}) collective-permute-start(bf16[2,256,128]{2,1,0:T(8,128)(2,1)S(1)} %get-tuple-element.38), channel_id=1, source_target_pairs={{0,4},{1,20},{2,6},{3,22},{4,0},{5,16},{6,2},{7,18},{8,12},{9,28},... | collective-permute-start | bytes 393224 | tf_op jit(solution)/shard_map/ppermute | solution.py:358
  16.1 0.0 collective-permute-done.2.rest_2_
  16.1 0.0 collective-permute-start.5
  16.1 0.3 collective-permute-done.3.rest_3_
  16.4 0.2 collective-permute-start.6
  16.6 2.0 %collective-permute-done.4.rest_4_ = bf16[2,256,128]{2,1,0:T(8,128)(2,1)S(1)} collective-permute-done((bf16[2,256,128]{2,1,0:T(8,128)(2,1)S(1)}, bf16[2,256,128]{2,1,0:T(8,128)(2,1)S(1)}, u32[]{:S(2)}, u32[]{:S(2)}) %collective-permute-start.4) | collective-permute-done | bytes 131104 | tf_op jit(solution)/shard_map/ppermute | solution.py:358
  18.6 0.0 collective-permute-start.7
  18.6 4.7 %collective-permute-done.9.rest_9_ = bf16[2,256,128]{2,1,0:T(8,128)(2,1)S(1)} collective-permute-done((bf16[2,256,128]{2,1,0:T(8,128)(2,1)S(1)}, bf16[2,256,128]{2,1,0:T(8,128)(2,1)S(1)}, u32[]{:S(2)}, u32[]{:S(2)}) %collective-permute-start.9) | collective-permute-done | bytes 131104 | tf_op jit(solution)/shard_map/ppermute | solution.py:358
  23.3 0.0 collective-permute-start.8
  23.3 0.6 collective-permute-done.10.rest_10_
  23.8 6.2 %collective-permute-start.11 = (bf16[2,256,128]{2,1,0:T(8,128)(2,1)S(1)}, bf16[2,256,128]{2,1,0:T(8,128)(2,1)S(1)}, u32[]{:S(2)}, u32[]{:S(2)}) collective-permute-start(bf16[2,256,128]{2,1,0:T(8,128)(2,1)S(1)} %get-tuple-element.42), channel_id=1, source_target_pairs={{0,0},{1,16},{2,2},{3,18},{4,4},{5,20},{6,6},{7,22},{8,8},{9,24},{... | collective-permute-start | bytes 393224 | tf_op jit(solution)/shard_map/ppermute | solution.py:358
  30.1 0.0 collective-permute-done.5.rest_5_
  30.1 0.1 collective-permute-start.12
  30.2 0.0 collective-permute-done.6.rest_6_
  30.2 0.0 collective-permute-done.7.rest_7_
  30.2 0.0 collective-permute-done.8.rest_8_
  30.2 3.2 %attend.2 = (bf16[2,256,128]{2,1,0:T(8,128)(2,1)S(1)}, bf16[2,256,128]{2,1,0:T(8,128)(2,1)S(1)}, bf16[2,2048,128]{2,1,0:T(8,128)(2,1)S(1)}, bf16[2,128,128]{2,1,0:T(8,128)(2,1)S(1)}, f32[2,2176,128]{2,1,0:T(8,128)S(1)}) custom-call(s32[3,4,32]{2,1,0:T(4,128)S(1)} %get-tuple-element.31.mine_ref, s32[3,4,32]{2,1,0:T(4,128)S(1)} %collective-permute-done.other_table_ref, ...), custom_call_target="tpu_custom_call" | custom-call | flops 402653184 | bytes 1572864 | tf_op jit(solution)/shard_map/attend/pallas_call | solution.py:278
  33.4 0.0 collective-permute-done.11.rest_3_
  33.4 2.7 %collective-permute-done.12.rest_4_ = bf16[2,256,128]{2,1,0:T(8,128)(2,1)S(1)} collective-permute-done((bf16[2,256,128]{2,1,0:T(8,128)(2,1)S(1)}, bf16[2,256,128]{2,1,0:T(8,128)(2,1)S(1)}, u32[]{:S(2)}, u32[]{:S(2)}) %collective-permute-start.12) | collective-permute-done | bytes 131104 | tf_op jit(solution)/shard_map/ppermute | solution.py:358
  36.1 2.7 %attend.3 = (bf16[2,256,128]{2,1,0:T(8,128)(2,1)S(1)}, bf16[2,256,128]{2,1,0:T(8,128)(2,1)S(1)}, f32[2,2176,128]{2,1,0:T(8,128)S(1)}, f32[2,1152,128]{2,1,0:T(8,128)S(1)}) custom-call(s32[3,4,32]{2,1,0:T(4,128)S(1)} %get-tuple-element.31.mine_ref, s32[3,4,32]{2,1,0:T(4,128)S(1)} %collective-permute-done.other_table_ref, ...), custom_call_target="tpu_custom_call", output_to_operand_aliasing={{2}: (4, {})} | custom-call | flops 402653184 | bytes 1572864 | tf_op jit(solution)/shard_map/attend/pallas_call | solution.py:278
  38.8 0.1 collective-permute-start.17
  38.9 2.6 %collective-permute-start.13 = (bf16[2,256,128]{2,1,0:T(8,128)(2,1)S(1)}, bf16[2,256,128]{2,1,0:T(8,128)(2,1)S(1)}, u32[]{:S(2)}, u32[]{:S(2)}) collective-permute-start(bf16[2,256,128]{2,1,0:T(8,128)(2,1)S(1)} %get-tuple-element.44), channel_id=1, source_target_pairs={{0,0},{1,16},{2,2},{3,18},{4,4},{5,20},{6,6},{7,22},{8,8},{9,24},{... | collective-permute-start | bytes 393224 | tf_op jit(solution)/shard_map/ppermute | solution.py:358
  41.5 0.6 collective-permute-start.15
  42.1 3.4 %collective-permute-start.14 = (bf16[2,256,128]{2,1,0:T(8,128)(2,1)S(1)}, bf16[2,256,128]{2,1,0:T(8,128)(2,1)S(1)}, u32[]{:S(2)}, u32[]{:S(2)}) collective-permute-start(bf16[2,256,128]{2,1,0:T(8,128)(2,1)S(1)} %get-tuple-element.45), channel_id=1, source_target_pairs={{0,4},{1,20},{2,6},{3,22},{4,0},{5,16},{6,2},{7,18},{8,12},{9,28},... | collective-permute-start | bytes 393224 | tf_op jit(solution)/shard_map/ppermute | solution.py:358
  45.6 1.5 %collective-permute-start.16 = (bf16[2,256,128]{2,1,0:T(8,128)(2,1)S(1)}, bf16[2,256,128]{2,1,0:T(8,128)(2,1)S(1)}, u32[]{:S(2)}, u32[]{:S(2)}) collective-permute-start(bf16[2,256,128]{2,1,0:T(8,128)(2,1)S(1)} %get-tuple-element.47), channel_id=1, source_target_pairs={{0,12},{1,28},{2,14},{3,30},{4,8},{5,24},{6,10},{7,26},{8,4},{9,20... | collective-permute-start | bytes 393224 | tf_op jit(solution)/shard_map/ppermute | solution.py:358
  47.1 0.0 collective-permute-done.17.came_ref
  47.1 0.5 total.1
  47.5 2.7 %collective-permute-start.18 = (bf16[2,256,128]{2,1,0:T(8,128)(2,1)S(1)}, bf16[2,256,128]{2,1,0:T(8,128)(2,1)S(1)}, u32[]{:S(2)}, u32[]{:S(2)}) collective-permute-start(bf16[2,256,128]{2,1,0:T(8,128)(2,1)S(1)} %get-tuple-element.52), channel_id=1, source_target_pairs={{0,0},{1,16},{2,2},{3,18},{4,4},{5,20},{6,6},{7,22},{8,8},{9,24},{... | collective-permute-start | bytes 393224 | tf_op jit(solution)/shard_map/ppermute | solution.py:358
  50.2 0.0 collective-permute-done.13.rest_0_
  50.2 2.7 %collective-permute-start.19 = (bf16[2,256,128]{2,1,0:T(8,128)(2,1)S(1)}, bf16[2,256,128]{2,1,0:T(8,128)(2,1)S(1)}, u32[]{:S(2)}, u32[]{:S(2)}) collective-permute-start(bf16[2,256,128]{2,1,0:T(8,128)(2,1)S(1)} %get-tuple-element.53), channel_id=1, source_target_pairs={{0,4},{1,20},{2,6},{3,22},{4,0},{5,16},{6,2},{7,18},{8,12},{9,28},... | collective-permute-start | bytes 393224 | tf_op jit(solution)/shard_map/ppermute | solution.py:358
  52.9 0.0 collective-permute-done.15.rest_2_
  52.9 0.4 collective-permute-start.20
  53.3 0.0 collective-permute-done.14.rest_1_
  53.3 1.5 %collective-permute-start.21 = (bf16[2,256,128]{2,1,0:T(8,128)(2,1)S(1)}, bf16[2,256,128]{2,1,0:T(8,128)(2,1)S(1)}, u32[]{:S(2)}, u32[]{:S(2)}) collective-permute-start(bf16[2,256,128]{2,1,0:T(8,128)(2,1)S(1)} %get-tuple-element.55), channel_id=1, source_target_pairs={{0,12},{1,28},{2,14},{3,30},{4,8},{5,24},{6,10},{7,26},{8,4},{9,20... | collective-permute-start | bytes 393224 | tf_op jit(solution)/shard_map/ppermute | solution.py:358
  54.8 6.1 %collective-permute-done.16.rest_3_ = bf16[2,256,128]{2,1,0:T(8,128)(2,1)S(1)} collective-permute-done((bf16[2,256,128]{2,1,0:T(8,128)(2,1)S(1)}, bf16[2,256,128]{2,1,0:T(8,128)(2,1)S(1)}, u32[]{:S(2)}, u32[]{:S(2)}) %collective-permute-start.16) | collective-permute-done | bytes 131104 | tf_op jit(solution)/shard_map/ppermute | solution.py:358
  60.9 0.8 %unpack.2 = (bf16[1,256,512]{2,1,0:T(8,128)(2,1)}, bf16[1,256,512]{2,1,0:T(8,128)(2,1)}) custom-call(bf16[2,256,128]{2,1,0:T(8,128)(2,1)S(1)} %collective-permute-done.13.rest_0_, bf16[2,256,128]{2,1,0:T(8,128)(2,1)S(1)} %collective-permute-done.14.rest_1_, bf16[2,256,128]{2,1,0:T(8,128)(2,1)S(1)} %collective-permute-done.15.rest_2_, ...), custom_call_target="tpu_custom_call" | custom-call | bytes 1048576 | tf_op jit(solution)/shard_map/unpack/pallas_call | solution.py:116
  61.7 0.0 collective-permute-done.18.rest_0_
  61.7 0.0 collective-permute-done.19.rest_1_
  61.7 2.9 %collective-permute-done.20.rest_2_ = bf16[2,256,128]{2,1,0:T(8,128)(2,1)S(1)} collective-permute-done((bf16[2,256,128]{2,1,0:T(8,128)(2,1)S(1)}, bf16[2,256,128]{2,1,0:T(8,128)(2,1)S(1)}, u32[]{:S(2)}, u32[]{:S(2)}) %collective-permute-start.20) | collective-permute-done | bytes 131104 | tf_op jit(solution)/shard_map/ppermute | solution.py:358
  64.7 1.8 %collective-permute-done.21.rest_3_ = bf16[2,256,128]{2,1,0:T(8,128)(2,1)S(1)} collective-permute-done((bf16[2,256,128]{2,1,0:T(8,128)(2,1)S(1)}, bf16[2,256,128]{2,1,0:T(8,128)(2,1)S(1)}, u32[]{:S(2)}, u32[]{:S(2)}) %collective-permute-start.21) | collective-permute-done | bytes 131104 | tf_op jit(solution)/shard_map/ppermute | solution.py:358
  66.5 0.8 %unpack.3 = (bf16[1,256,512]{2,1,0:T(8,128)(2,1)}, bf16[1,256,512]{2,1,0:T(8,128)(2,1)}) custom-call(bf16[2,256,128]{2,1,0:T(8,128)(2,1)S(1)} %collective-permute-done.18.rest_0_, bf16[2,256,128]{2,1,0:T(8,128)(2,1)S(1)} %collective-permute-done.19.rest_1_, bf16[2,256,128]{2,1,0:T(8,128)(2,1)S(1)} %collective-permute-done.20.rest_2_, ...), custom_call_target="tpu_custom_call" | custom-call | bytes 1048576 | tf_op jit(solution)/shard_map/unpack/pallas_call | solution.py:116
Async XLA Ops:
  1.8 11.4 %collective-permute-start.1 = (bf16[2,256,128]{2,1,0:T(8,128)(2,1)S(1)}, bf16[2,256,128]{2,1,0:T(8,128)(2,1)S(1)}, u32[]{:S(2)}, u32[]{:S(2)}) collective-permute-start(bf16[2,256,128]{2,1,0:T(8,128)(2,1)S(1)} %get-tuple-element.33), channel_id=1, source_target_pairs={{0,0},{1,16},{2,2},{3,18},{4,4},{5,20},{6,6},{7,22},{8,8},{9,24},{... | collective-permute-start | bytes 393224 | tf_op jit(solution)/shard_map/ppermute | solution.py:358
  6.6 9.5 %collective-permute-start.2 = (bf16[2,256,128]{2,1,0:T(8,128)(2,1)S(1)}, bf16[2,256,128]{2,1,0:T(8,128)(2,1)S(1)}, u32[]{:S(2)}, u32[]{:S(2)}) collective-permute-start(bf16[2,256,128]{2,1,0:T(8,128)(2,1)S(1)} %get-tuple-element.34), channel_id=1, source_target_pairs={{0,4},{1,20},{2,6},{3,22},{4,0},{5,16},{6,2},{7,18},{8,12},{9,28},... | collective-permute-start | bytes 393224 | tf_op jit(solution)/shard_map/ppermute | solution.py:358
  8.8 1.9 %collective-permute-start = (s32[3,4,32]{2,1,0:T(4,128)S(1)}, s32[3,4,32]{2,1,0:T(4,128)S(1)}, u32[]{:S(2)}, u32[]{:S(2)}) collective-permute-start(s32[3,4,32]{2,1,0:T(4,128)S(1)} %get-tuple-element.31.mine_ref), channel_id=1, source_target_pairs={{0,1},{1,0},{2,3},{3,2},{4,5},{5,4},{6,7},{7,6},{8,9},{9,8},{10,11... | collective-permute-start | bytes 4616 | tf_op jit(solution)/shard_map/ppermute | solution.py:364
  8.9 7.5 %collective-permute-start.3 = (bf16[2,256,128]{2,1,0:T(8,128)(2,1)S(1)}, bf16[2,256,128]{2,1,0:T(8,128)(2,1)S(1)}, u32[]{:S(2)}, u32[]{:S(2)}) collective-permute-start(bf16[2,256,128]{2,1,0:T(8,128)(2,1)S(1)} %get-tuple-element.35), channel_id=1, source_target_pairs={{0,8},{1,24},{2,10},{3,26},{4,12},{5,28},{6,14},{7,30},{8,0},{9,16... | collective-permute-start | bytes 393224 | tf_op jit(solution)/shard_map/ppermute | solution.py:358
  10.6 8.1 %collective-permute-start.4 = (bf16[2,256,128]{2,1,0:T(8,128)(2,1)S(1)}, bf16[2,256,128]{2,1,0:T(8,128)(2,1)S(1)}, u32[]{:S(2)}, u32[]{:S(2)}) collective-permute-start(bf16[2,256,128]{2,1,0:T(8,128)(2,1)S(1)} %get-tuple-element.36), channel_id=1, source_target_pairs={{0,12},{1,28},{2,14},{3,30},{4,8},{5,24},{6,10},{7,26},{8,4},{9,20... | collective-permute-start | bytes 393224 | tf_op jit(solution)/shard_map/ppermute | solution.py:358
  10.7 12.6 %collective-permute-start.9 = (bf16[2,256,128]{2,1,0:T(8,128)(2,1)S(1)}, bf16[2,256,128]{2,1,0:T(8,128)(2,1)S(1)}, u32[]{:S(2)}, u32[]{:S(2)}) collective-permute-start(bf16[2,256,128]{2,1,0:T(8,128)(2,1)S(1)} %get-tuple-element.37), channel_id=1, source_target_pairs={{0,12},{1,28},{2,14},{3,30},{4,8},{5,24},{6,10},{7,26},{8,4},{9,20... | collective-permute-start | bytes 393224 | tf_op jit(solution)/shard_map/ppermute | solution.py:358
  13.2 10.6 %collective-permute-start.10 = (bf16[2,256,128]{2,1,0:T(8,128)(2,1)S(1)}, bf16[2,256,128]{2,1,0:T(8,128)(2,1)S(1)}, u32[]{:S(2)}, u32[]{:S(2)}) collective-permute-start(bf16[2,256,128]{2,1,0:T(8,128)(2,1)S(1)} %get-tuple-element.38), channel_id=1, source_target_pairs={{0,4},{1,20},{2,6},{3,22},{4,0},{5,16},{6,2},{7,18},{8,12},{9,28},... | collective-permute-start | bytes 393224 | tf_op jit(solution)/shard_map/ppermute | solution.py:358
  16.1 14.0 %collective-permute-start.5 = (bf16[2,256,128]{2,1,0:T(8,128)(2,1)S(1)}, bf16[2,256,128]{2,1,0:T(8,128)(2,1)S(1)}, u32[]{:S(2)}, u32[]{:S(2)}) collective-permute-start(bf16[2,256,128]{2,1,0:T(8,128)(2,1)S(1)} %collective-permute-done.1.rest_1_), channel_id=1, source_target_pairs={{0,1},{1,0},{2,3},{3,2},{4,5},{5,4},{6,7},{7,6},{8,9},{9,8},{10,11... | collective-permute-start | bytes 393224 | tf_op jit(solution)/shard_map/ppermute | solution.py:364
  16.4 13.8 %collective-permute-start.6 = (bf16[2,256,128]{2,1,0:T(8,128)(2,1)S(1)}, bf16[2,256,128]{2,1,0:T(8,128)(2,1)S(1)}, u32[]{:S(2)}, u32[]{:S(2)}) collective-permute-start(bf16[2,256,128]{2,1,0:T(8,128)(2,1)S(1)} %collective-permute-done.2.rest_2_), channel_id=1, source_target_pairs={{0,1},{1,0},{2,3},{3,2},{4,5},{5,4},{6,7},{7,6},{8,9},{9,8},{10,11... | collective-permute-start | bytes 393224 | tf_op jit(solution)/shard_map/ppermute | solution.py:364
  18.6 11.6 %collective-permute-start.7 = (bf16[2,256,128]{2,1,0:T(8,128)(2,1)S(1)}, bf16[2,256,128]{2,1,0:T(8,128)(2,1)S(1)}, u32[]{:S(2)}, u32[]{:S(2)}) collective-permute-start(bf16[2,256,128]{2,1,0:T(8,128)(2,1)S(1)} %collective-permute-done.3.rest_3_), channel_id=1, source_target_pairs={{0,1},{1,0},{2,3},{3,2},{4,5},{5,4},{6,7},{7,6},{8,9},{9,8},{10,11... | collective-permute-start | bytes 393224 | tf_op jit(solution)/shard_map/ppermute | solution.py:364
  23.3 6.9 %collective-permute-start.8 = (bf16[2,256,128]{2,1,0:T(8,128)(2,1)S(1)}, bf16[2,256,128]{2,1,0:T(8,128)(2,1)S(1)}, u32[]{:S(2)}, u32[]{:S(2)}) collective-permute-start(bf16[2,256,128]{2,1,0:T(8,128)(2,1)S(1)} %collective-permute-done.4.rest_4_), channel_id=1, source_target_pairs={{0,1},{1,0},{2,3},{3,2},{4,5},{5,4},{6,7},{7,6},{8,9},{9,8},{10,11... | collective-permute-start | bytes 393224 | tf_op jit(solution)/shard_map/ppermute | solution.py:364
  23.8 9.6 %collective-permute-start.11 = (bf16[2,256,128]{2,1,0:T(8,128)(2,1)S(1)}, bf16[2,256,128]{2,1,0:T(8,128)(2,1)S(1)}, u32[]{:S(2)}, u32[]{:S(2)}) collective-permute-start(bf16[2,256,128]{2,1,0:T(8,128)(2,1)S(1)} %get-tuple-element.42), channel_id=1, source_target_pairs={{0,0},{1,16},{2,2},{3,18},{4,4},{5,20},{6,6},{7,22},{8,8},{9,24},{... | collective-permute-start | bytes 393224 | tf_op jit(solution)/shard_map/ppermute | solution.py:358
  30.1 6.0 %collective-permute-start.12 = (bf16[2,256,128]{2,1,0:T(8,128)(2,1)S(1)}, bf16[2,256,128]{2,1,0:T(8,128)(2,1)S(1)}, u32[]{:S(2)}, u32[]{:S(2)}) collective-permute-start(bf16[2,256,128]{2,1,0:T(8,128)(2,1)S(1)} %get-tuple-element.43), channel_id=1, source_target_pairs={{0,8},{1,24},{2,10},{3,26},{4,12},{5,28},{6,14},{7,30},{8,0},{9,16... | collective-permute-start | bytes 393224 | tf_op jit(solution)/shard_map/ppermute | solution.py:358
  38.8 8.3 %collective-permute-start.17 = (f32[2,1152,128]{2,1,0:T(8,128)S(1)}, f32[2,1152,128]{2,1,0:T(8,128)S(1)}, u32[]{:S(2)}, u32[]{:S(2)}) collective-permute-start(f32[2,1152,128]{2,1,0:T(8,128)S(1)} %get-tuple-element.51), channel_id=1, source_target_pairs={{0,1},{1,0},{2,3},{3,2},{4,5},{5,4},{6,7},{7,6},{8,9},{9,8},{10,11... | collective-permute-start | bytes 3538952 | tf_op jit(solution)/shard_map/ppermute | solution.py:364
  38.9 11.3 %collective-permute-start.13 = (bf16[2,256,128]{2,1,0:T(8,128)(2,1)S(1)}, bf16[2,256,128]{2,1,0:T(8,128)(2,1)S(1)}, u32[]{:S(2)}, u32[]{:S(2)}) collective-permute-start(bf16[2,256,128]{2,1,0:T(8,128)(2,1)S(1)} %get-tuple-element.44), channel_id=1, source_target_pairs={{0,0},{1,16},{2,2},{3,18},{4,4},{5,20},{6,6},{7,22},{8,8},{9,24},{... | collective-permute-start | bytes 393224 | tf_op jit(solution)/shard_map/ppermute | solution.py:358
  41.5 11.4 %collective-permute-start.15 = (bf16[2,256,128]{2,1,0:T(8,128)(2,1)S(1)}, bf16[2,256,128]{2,1,0:T(8,128)(2,1)S(1)}, u32[]{:S(2)}, u32[]{:S(2)}) collective-permute-start(bf16[2,256,128]{2,1,0:T(8,128)(2,1)S(1)} %get-tuple-element.46), channel_id=1, source_target_pairs={{0,8},{1,24},{2,10},{3,26},{4,12},{5,28},{6,14},{7,30},{8,0},{9,16... | collective-permute-start | bytes 393224 | tf_op jit(solution)/shard_map/ppermute | solution.py:358
  42.1 11.2 %collective-permute-start.14 = (bf16[2,256,128]{2,1,0:T(8,128)(2,1)S(1)}, bf16[2,256,128]{2,1,0:T(8,128)(2,1)S(1)}, u32[]{:S(2)}, u32[]{:S(2)}) collective-permute-start(bf16[2,256,128]{2,1,0:T(8,128)(2,1)S(1)} %get-tuple-element.45), channel_id=1, source_target_pairs={{0,4},{1,20},{2,6},{3,22},{4,0},{5,16},{6,2},{7,18},{8,12},{9,28},... | collective-permute-start | bytes 393224 | tf_op jit(solution)/shard_map/ppermute | solution.py:358
  45.6 15.3 %collective-permute-start.16 = (bf16[2,256,128]{2,1,0:T(8,128)(2,1)S(1)}, bf16[2,256,128]{2,1,0:T(8,128)(2,1)S(1)}, u32[]{:S(2)}, u32[]{:S(2)}) collective-permute-start(bf16[2,256,128]{2,1,0:T(8,128)(2,1)S(1)} %get-tuple-element.47), channel_id=1, source_target_pairs={{0,12},{1,28},{2,14},{3,30},{4,8},{5,24},{6,10},{7,26},{8,4},{9,20... | collective-permute-start | bytes 393224 | tf_op jit(solution)/shard_map/ppermute | solution.py:358
  47.5 14.2 %collective-permute-start.18 = (bf16[2,256,128]{2,1,0:T(8,128)(2,1)S(1)}, bf16[2,256,128]{2,1,0:T(8,128)(2,1)S(1)}, u32[]{:S(2)}, u32[]{:S(2)}) collective-permute-start(bf16[2,256,128]{2,1,0:T(8,128)(2,1)S(1)} %get-tuple-element.52), channel_id=1, source_target_pairs={{0,0},{1,16},{2,2},{3,18},{4,4},{5,20},{6,6},{7,22},{8,8},{9,24},{... | collective-permute-start | bytes 393224 | tf_op jit(solution)/shard_map/ppermute | solution.py:358
  50.2 11.5 %collective-permute-start.19 = (bf16[2,256,128]{2,1,0:T(8,128)(2,1)S(1)}, bf16[2,256,128]{2,1,0:T(8,128)(2,1)S(1)}, u32[]{:S(2)}, u32[]{:S(2)}) collective-permute-start(bf16[2,256,128]{2,1,0:T(8,128)(2,1)S(1)} %get-tuple-element.53), channel_id=1, source_target_pairs={{0,4},{1,20},{2,6},{3,22},{4,0},{5,16},{6,2},{7,18},{8,12},{9,28},... | collective-permute-start | bytes 393224 | tf_op jit(solution)/shard_map/ppermute | solution.py:358
  52.9 11.8 %collective-permute-start.20 = (bf16[2,256,128]{2,1,0:T(8,128)(2,1)S(1)}, bf16[2,256,128]{2,1,0:T(8,128)(2,1)S(1)}, u32[]{:S(2)}, u32[]{:S(2)}) collective-permute-start(bf16[2,256,128]{2,1,0:T(8,128)(2,1)S(1)} %get-tuple-element.54), channel_id=1, source_target_pairs={{0,8},{1,24},{2,10},{3,26},{4,12},{5,28},{6,14},{7,30},{8,0},{9,16... | collective-permute-start | bytes 393224 | tf_op jit(solution)/shard_map/ppermute | solution.py:358
  53.3 13.2 %collective-permute-start.21 = (bf16[2,256,128]{2,1,0:T(8,128)(2,1)S(1)}, bf16[2,256,128]{2,1,0:T(8,128)(2,1)S(1)}, u32[]{:S(2)}, u32[]{:S(2)}) collective-permute-start(bf16[2,256,128]{2,1,0:T(8,128)(2,1)S(1)} %get-tuple-element.55), channel_id=1, source_target_pairs={{0,12},{1,28},{2,14},{3,30},{4,8},{5,24},{6,10},{7,26},{8,4},{9,20... | collective-permute-start | bytes 393224 | tf_op jit(solution)/shard_map/ppermute | solution.py:358
